TPU v7x, 32 devices: a whole 2x2x4 slice. The times are simulated.
32 devices in a mesh: obs: 4 (over x, core), ord: 8 (over z, y).
Axes of the slice: x: 2, y: 2, z: 4, core: 2. Of those that a mesh axis runs over, the one named last changes fastest.
Arguments:
- longitude: float32 [4, 32768], P('obs'), may hold values from -3.140625 to 3.140625
- cycle_of: int32 [4, 32768], P('obs'), may hold values from 0 to 255, never falling along the last dimension, each value on 1 to 256 neighbouring positions
- obs_count: int32 [4], P('obs'), may hold values from 16384 to 32768
- observed: float32 [4, 32768], P('obs'), may hold values from -896 to 896
- obs_weight: float32 [4, 32768], P('obs'), may hold values from 0.3 to 3
- legendre: float32 [4, 72, 288, 256], P('obs', 'ord'), as said below
- precond_inv: float32 [72, 288, 288], P('ord'), as said below
- order_of_slot: int32 [72], P('ord'), may hold values from 0 to 71, each once
Outputs:
- solution: float32 [72, 2, 288], P('ord')
- residual: float32 [72, 2, 288], P('ord')
Inputs may be any that keep to these rules, and one draw needn't show every extreme that they name: `cycle_of`: cycle numbers never fall along a slab; each cycle holds at least one observation slot. `obs_count`: observation slots at or beyond a slab's count carry no weight. legendre[b, m, n, j] is the fully normalized associated Legendre function of degree n and order m at the colatitude of cycle j of slab b, and 0 for n < m. `precond_inv`: every block is symmetric positive definite. order_of_slot names each order once; slot s lies on ord index s // 9.
All inputs are finite; a program needn't handle non-finite values.
Results may differ from a plain program's by a relative error of at most 0.0003.
Values sent between devices are 32-bit elements; how exact they have to be, the bound alone decides.
No kernel may reach another device: no remote copies, remote signals or barrier semaphores. Data moves between devices by JAX's collectives and lax.ppermute only.
A program may use at most 128 MiB of HBM per device.

v0:
```python
import math

import jax
import jax.numpy as jnp
from jax import lax
from jax.sharding import PartitionSpec as P

ITERS = 2


PRECISE = lax.Precision.HIGHEST


def block_split(cycle_ids):
    slab_size = cycle_ids.shape[0]
    block = math.gcd(slab_size, 4096)
    return (block, slab_size // block)


def spread_cycles(cycle_values, cycle_ids):
    rows = cycle_values.shape[0] * cycle_values.shape[1]
    cycle_count = cycle_values.shape[2]
    flat_cycles = cycle_values.reshape(rows, cycle_count)
    block, blocks = block_split(cycle_ids)
    cycle_iota = jnp.arange(cycle_count, dtype=jnp.int32)

    def one_block(id_block):
        onehot = (id_block[:, None] == cycle_iota[None, :]).astype(jnp.float32)
        return jnp.dot(onehot, flat_cycles.T, precision=PRECISE, preferred_element_type=jnp.float32)

    pieces = lax.map(one_block, cycle_ids.reshape(blocks, block))
    at_points = pieces.reshape(blocks * block, rows).T
    return at_points.reshape(cycle_values.shape[0], cycle_values.shape[1], blocks * block)


def collect_cycles(weighted, cycle_ids, cycle_count):
    lead = weighted.shape[0]
    pair = weighted.shape[1]
    rows = lead * pair
    block, blocks = block_split(cycle_ids)
    cycle_iota = jnp.arange(cycle_count, dtype=jnp.int32)
    flat = jnp.moveaxis(weighted.reshape(rows, blocks, block), 1, 0)

    def add_block(total, block_data):
        id_block, value_block = block_data
        onehot = (id_block[:, None] == cycle_iota[None, :]).astype(jnp.float32)
        return (
            total
            + jnp.dot(value_block, onehot, precision=PRECISE, preferred_element_type=jnp.float32),
            None,
        )

    total, unused = lax.scan(
        add_block,
        jnp.zeros((rows, cycle_count), jnp.float32),
        (cycle_ids.reshape(blocks, block), flat),
    )
    return total.reshape(lead, pair, cycle_count)


def synthesize(coefficients, legendre_here, harmonic, cycle_ids):
    cycle_values = jnp.einsum("okn,onr->okr", coefficients, legendre_here, precision=PRECISE)
    at_points = spread_cycles(cycle_values, cycle_ids)
    return jnp.sum(at_points * harmonic, axis=(0, 1))


def adjoint(values, legendre_here, harmonic, cycle_ids):
    weighted = harmonic * values[None, None, :]
    per_cycle = collect_cycles(weighted, cycle_ids, legendre_here.shape[2])
    return jnp.einsum("okr,onr->okn", per_cycle, legendre_here, precision=PRECISE)


def body(
    longitude, cycle_of, obs_count, observed, obs_weight, legendre, precond_inv, order_of_slot
):
    count_here = legendre.shape[1]
    degrees = legendre.shape[2]
    legendre_here = legendre[0]
    east = longitude[0]
    cycle_ids = cycle_of[0]
    slab_size = east.shape[0]
    positions = jnp.arange(slab_size, dtype=jnp.int32)
    total_obs = slab_size * lax.axis_size("obs")
    obs_scale = obs_weight[0] * (positions < obs_count[0]).astype(jnp.float32) / total_obs
    first_order = lax.axis_index("ord") * count_here
    block_orders = first_order + jnp.arange(count_here, dtype=jnp.int32)
    angles = block_orders.astype(jnp.float32)[:, None] * east[None, :]
    harmonic = jnp.stack([jnp.cos(angles), jnp.sin(angles)], axis=1)
    every_owner = lax.all_gather(order_of_slot, "ord", axis=0, tiled=True)
    slot_ids = jnp.arange(every_owner.shape[0], dtype=jnp.int32)
    slot_of_block = jnp.sum(
        jnp.where(every_owner[None, :] == block_orders[:, None], slot_ids[None, :], 0), axis=1
    )
    live_mask = (
        jnp.arange(degrees, dtype=jnp.int32)[None, None, :] >= order_of_slot[:, None, None]
    ).astype(jnp.float32)

    def owner_rows(partial_value):
        summed = lax.psum(partial_value, "obs")
        everyone = lax.all_gather(summed, "ord", axis=0, tiled=True)
        return jnp.take(everyone, order_of_slot, axis=0)

    def precondition(values):
        return live_mask * jnp.einsum("snj,skj->skn", precond_inv, values, precision=PRECISE)

    def energy(values, precond):
        return lax.psum(jnp.sum(values * precond), "ord")

    residual = owner_rows(adjoint(obs_scale * observed[0], legendre_here, harmonic, cycle_ids))
    solution = jnp.zeros_like(residual)
    precond = precondition(residual)
    direction = precond
    energy_now = energy(residual, precond)
    for iteration in range(ITERS):
        block_everyone = lax.all_gather(direction, "ord", axis=0, tiled=True)
        coefficients = jnp.take(block_everyone, slot_of_block, axis=0)
        gradient = lax.psum(synthesize(coefficients, legendre_here, harmonic, cycle_ids), "ord")
        weighted = obs_scale * gradient
        curvature_sum = lax.psum(jnp.sum(weighted * gradient), "obs")
        image = owner_rows(adjoint(weighted, legendre_here, harmonic, cycle_ids))
        image, curvature_sum = (image, curvature_sum)
        step_size = energy_now / curvature_sum
        solution = solution + step_size * direction
        residual = residual - step_size * image
        if iteration + 1 < ITERS:
            precond = precondition(residual)
            energy_next = energy(residual, precond)
            direction = precond + energy_next / energy_now * direction
            energy_now = energy_next
    return (solution, residual)


def solution(mesh):
    placed = (
        P("obs", None),
        P("obs", None),
        P("obs"),
        P("obs", None),
        P("obs", None),
        P("obs", "ord", None, None),
        P("ord", None, None),
        P("ord"),
    )
    return jax.shard_map(
        body,
        mesh=mesh,
        in_specs=placed,
        out_specs=(P("ord", None, None), P("ord", None, None)),
        check_vma=False,
    )
```

profile of v0, /device:TPU:0, one launch (start us, length us, event | category | flops | bytes accessed | tf_op | source)
XLA Modules:
  0.0 720.2 jit_solution(2464493801423855208)
XLA Ops:
  12.2 13.1 %all-reduce = s32[72]{0:T(128)S(1)} all-reduce(s32[72]{0:T(128)S(1)} %dynamic-update-slice), channel_id=1, replica_groups=mesh['obs'=4,'ord'=8] {'ord'}, use_global_device_ids=true, to_apply=%add | all-reduce | flops 72 | bytes 576
  25.5 33.9 %multiply_cosine_fusion = (f32[9,1,32768]{2,1,0:T(1,128)S(1)}, f32[9,1,32768]{2,1,0:T(1,128)S(1)}) fusion(f32[32768]{0:T(1024)} %bitcast.105, f32[9]{0:T(128)S(1)} %fusion.46), kind=kLoop, calls=%fused_computation.58 | loop fusion | flops 294912 | bytes 2490404 | tf_op jit(solution)/shard_map/cos | solution.py:88
  59.4 3.5 pad_maximum_fusion
  62.9 4.2 stack.10
  67.2 4.6 stack.11
  76.1 3.3 multiply_bitcast_fusion.2
  79.4 28.7 %while.57 = (s32[]{:T(128)}, f32[18,256]{1,0:T(8,128)S(1)}, f32[8,18,4096]{2,0,1:T(8,128)}, s32[8,4096]{1,0:T(8,128)S(1)}, s32[]{:T(128)}, /*index=5*/s32[]{:T(128)}) while((s32[]{:T(128)}, f32[18,256]{1,0:T(8,128)S(1)}, f32[8,18,4096]{2,0,1:T(8,128)}, s32[8,4096]{1,0:T(8,128)S(1)}, s32[]{:T(128)}, /*index=5*/s32[]{:T(128)}) %tuple.107), condition=%wide.region_1.2_spmd.clone, body=%wide.region_0.1_spmd.clone.sunk | while | flops 227550208 | bytes 970839 | solution.py:53
  110.4 10.3 %psum.63 = f32[9,2,288]{2,1,0:T(2,128)S(1)} all-reduce(f32[9,2,288]{2,1,0:T(2,128)S(1)} %fusion.31), channel_id=1, replica_groups=mesh['obs'=4,'ord'=8] {'obs'}, use_global_device_ids=true, to_apply=%region_2.3 | all-reduce | flops 5184 | bytes 41472 | tf_op jit(solution)/shard_map/psum | solution.py:99
  120.7 30.7 %all_gather.18 = f32[72,2,288]{2,1,0:T(2,128)S(1)} all-gather(f32[9,2,288]{2,1,0:T(2,128)S(1)} %psum.63), channel_id=1, replica_groups=mesh['obs'=4,'ord'=8] {'ord'}, dimensions={0}, use_global_device_ids=true | all-gather | bytes 186624 | tf_op jit(solution)/shard_map/all_gather | solution.py:100
  152.0 6.2 multiply_reduce_fusion.3
  158.2 30.7 %all_gather.19 = f32[72,2,288]{2,1,0:T(2,128)S(1)} all-gather(f32[9,2,288]{2,1,0:T(2,128)S(1)} %get-tuple-element.301), channel_id=1, replica_groups=mesh['obs'=4,'ord'=8] {'ord'}, dimensions={0}, use_global_device_ids=true | all-gather | bytes 186624 | tf_op jit(solution)/shard_map/all_gather | solution.py:115
  192.6 75.7 %while.55 = (s32[]{:T(128)}, f32[8,4096,18]{1,0,2:T(8,128)}, s32[8,4096]{1,0:T(8,128)S(1)}, f32[18,256]{1,0:T(8,128)S(1)}, s32[]{:T(128)}, /*index=5*/s32[]{:T(128)}) while((s32[]{:T(128)}, f32[8,4096,18]{1,0,2:T(8,128)}, s32[8,4096]{1,0:T(8,128)S(1)}, f32[18,256]{1,0:T(8,128)S(1)}, s32[]{:T(128)}, /*index=5*/s32[]{:T(128)}) %tuple.126), condition=%wide.region_7.9_spmd.clone, body=%wide.region_6.8_spmd.clone.sunk | while | flops 227540992 | bytes 1542221 | solution.py:31
  195.5 6.6 dynamic_update_slice.11
  204.9 6.6 dynamic_update_slice.11
  214.4 6.6 dynamic_update_slice.11
  221.0 2.6 convolution_bitcast_fusion.4
  223.9 6.6 dynamic_update_slice.11
  230.4 2.6 convolution_bitcast_fusion.4
  233.3 6.6 dynamic_update_slice.11
  239.9 2.6 convolution_bitcast_fusion.4
  242.8 6.6 dynamic_update_slice.11
  252.2 6.6 dynamic_update_slice.11
  258.8 2.6 convolution_bitcast_fusion.4
  261.7 6.6 dynamic_update_slice.11
  273.5 19.6 %psum.64 = f32[]{:T(128)} all-reduce(f32[]{:T(128)} %get-tuple-element.300), channel_id=1, replica_groups=mesh['obs'=4,'ord'=8] {'ord'}, use_global_device_ids=true, to_apply=%region_4.6 | all-reduce | flops 1 | bytes 8 | tf_op jit(solution)/shard_map/psum | solution.py:107
  293.1 49.5 %all-reduce.6.cloned.1.call-done = f32[32768]{0:T(1024)} async-done(((f32[32768]{0:T(1024)}), f32[32768]{0:T(1024)}) %all-reduce.6.cloned.1.call-update) | async-done | bytes 131088 | tf_op jit(solution)/shard_map/psum | solution.py:117
  344.1 3.3 multiply_bitcast_fusion.1
  347.4 28.2 %while.58 = (s32[]{:T(128)}, f32[18,256]{1,0:T(8,128)S(1)}, f32[8,18,4096]{2,0,1:T(8,128)}, s32[8,4096]{1,0:T(8,128)S(1)}, s32[]{:T(128)}, /*index=5*/s32[]{:T(128)}) while((s32[]{:T(128)}, f32[18,256]{1,0:T(8,128)S(1)}, f32[8,18,4096]{2,0,1:T(8,128)}, s32[8,4096]{1,0:T(8,128)S(1)}, s32[]{:T(128)}, /*index=5*/s32[]{:T(128)}) %tuple.127), condition=%wide.region_13.15_spmd.clone, body=%wide.region_12.14_spmd.clone.sunk | while | flops 227550208 | bytes 970839 | solution.py:53
  377.9 11.3 %all-reduce.2 = (f32[9,2,288]{2,1,0:T(2,128)S(1)}, f32[]{:T(128)}) all-reduce(f32[9,2,288]{2,1,0:T(2,128)S(1)} %fusion.27, f32[]{:T(128)} %get-tuple-element.296), channel_id=1, replica_groups=mesh['obs'=4,'ord'=8] {'obs'}, use_global_device_ids=true, to_apply=%region_14.16 | all-reduce | flops 5185 | bytes 41480 | tf_op jit(solution)/shard_map/psum | solution.py:99
  389.2 30.8 %all_gather.21 = f32[72,2,288]{2,1,0:T(2,128)S(1)} all-gather(f32[9,2,288]{2,1,0:T(2,128)S(1)} %get-tuple-element.292), channel_id=1, replica_groups=mesh['obs'=4,'ord'=8] {'ord'}, dimensions={0}, use_global_device_ids=true | all-gather | bytes 186624 | tf_op jit(solution)/shard_map/all_gather | solution.py:100
  421.9 6.2 multiply_reduce_fusion.2
  428.1 20.1 %psum.68 = f32[]{:T(128)} all-reduce(f32[]{:T(128)} %get-tuple-element.302), channel_id=1, replica_groups=mesh['obs'=4,'ord'=8] {'ord'}, use_global_device_ids=true, to_apply=%region_16.18 | all-reduce | flops 1 | bytes 8 | tf_op jit(solution)/shard_map/psum | solution.py:107
  449.4 30.7 %all_gather.22 = f32[72,2,288]{2,1,0:T(2,128)S(1)} all-gather(f32[9,2,288]{2,1,0:T(2,128)S(1)} %multiply_add_fusion.1), channel_id=1, replica_groups=mesh['obs'=4,'ord'=8] {'ord'}, dimensions={0}, use_global_device_ids=true | all-gather | bytes 186624 | tf_op jit(solution)/shard_map/all_gather | solution.py:115
  483.8 75.9 %while.56 = (s32[]{:T(128)}, f32[8,4096,18]{1,0,2:T(8,128)}, s32[8,4096]{1,0:T(8,128)S(1)}, f32[18,256]{1,0:T(8,128)S(1)}, s32[]{:T(128)}, /*index=5*/s32[]{:T(128)}) while((s32[]{:T(128)}, f32[8,4096,18]{1,0,2:T(8,128)}, s32[8,4096]{1,0:T(8,128)S(1)}, f32[18,256]{1,0:T(8,128)S(1)}, s32[]{:T(128)}, /*index=5*/s32[]{:T(128)}) %tuple.128), condition=%wide.region_18.20_spmd.clone, body=%wide.region_17.19_spmd.clone.sunk | while | flops 227540992 | bytes 1542221 | solution.py:31
  486.9 6.6 dynamic_update_slice.12
  496.4 6.6 dynamic_update_slice.12
  505.9 6.6 dynamic_update_slice.12
  515.3 6.6 dynamic_update_slice.12
  524.8 6.6 dynamic_update_slice.12
  531.4 2.6 convolution_bitcast_fusion.5
  534.3 6.6 dynamic_update_slice.12
  543.7 6.6 dynamic_update_slice.12
  553.2 6.6 dynamic_update_slice.12
  564.9 67.5 %all-reduce.8.cloned.1.call-done = f32[32768]{0:T(1024)} async-done(((f32[32768]{0:T(1024)}), f32[32768]{0:T(1024)}) %all-reduce.8.cloned.1.call-update) | async-done | bytes 131088 | tf_op jit(solution)/shard_map/psum | solution.py:117
  634.0 3.3 multiply_bitcast_fusion
  637.4 28.2 %while.59 = (s32[]{:T(128)}, f32[18,256]{1,0:T(8,128)S(1)}, f32[8,18,4096]{2,0,1:T(8,128)}, s32[8,4096]{1,0:T(8,128)S(1)}, s32[]{:T(128)}, /*index=5*/s32[]{:T(128)}) while((s32[]{:T(128)}, f32[18,256]{1,0:T(8,128)S(1)}, f32[8,18,4096]{2,0,1:T(8,128)}, s32[8,4096]{1,0:T(8,128)S(1)}, s32[]{:T(128)}, /*index=5*/s32[]{:T(128)}) %tuple.129), condition=%wide.region_24.26_spmd.clone, body=%wide.region_23.25_spmd.clone.sunk | while | flops 227550208 | bytes 970839 | solution.py:53
  667.9 11.3 %all-reduce.1 = (f32[]{:T(128)}, f32[9,2,288]{2,1,0:T(2,128)S(1)}) all-reduce(f32[]{:T(128)} %get-tuple-element.294, f32[9,2,288]{2,1,0:T(2,128)S(1)} %fusion.23), channel_id=1, replica_groups=mesh['obs'=4,'ord'=8] {'obs'}, use_global_device_ids=true, to_apply=%region_22.24 | all-reduce | flops 5185 | bytes 41480 | tf_op jit(solution)/shard_map/psum | solution.py:119
  679.2 30.8 %all_gather.23 = f32[72,2,288]{2,1,0:T(2,128)S(1)} all-gather(f32[9,2,288]{2,1,0:T(2,128)S(1)} %get-tuple-element.291), channel_id=1, replica_groups=mesh['obs'=4,'ord'=8] {'ord'}, dimensions={0}, use_global_device_ids=true | all-gather | bytes 186624 | tf_op jit(solution)/shard_map/all_gather | solution.py:100
  (187 shorter events, 156.2 us)
Async XLA Ops:
  7.2 101.0 %copy-start = (f32[1,9,288,256]{3,2,1,0:T(8,128)S(1)}, f32[1,9,288,256]{3,2,1,0:T(8,128)}, u32[]{:S(2)}) copy-start(f32[1,9,288,256]{3,2,1,0:T(8,128)} %param.25) | copy-start | bytes 7962628
  7.2 335.4 %all-reduce.6.cloned.1.call-start = ((), (), s32[]{:S(2)}) async-start(), calls=%async_computation | async-start | bytes 262144 | tf_op jit(solution)/shard_map/psum | solution.py:117
  67.2 5.7 copy-start.3
  67.2 6.6 copy-start.4
  67.2 8.0 %copy-start.5 = (s32[1,32768]{1,0:T(1,128)S(1)}, s32[1,32768]{1,0:T(1,128)}, u32[]{:S(2)}) copy-start(s32[1,32768]{1,0:T(1,128)} %param.21) | copy-start | bytes 393220
  270.2 1.9 copy-start.1
  273.5 359.0 %all-reduce.8.cloned.1.call-start = ((), (), s32[]{:S(2)}) async-start(), calls=%async_computation.1 | async-start | bytes 262144 | tf_op jit(solution)/shard_map/psum | solution.py:117
  561.7 1.9 copy-start.2
Sparse Core Ops, SparseCore 0:
  273.6 68.9 all-reduce.5
  565.1 67.3 all-reduce.7
where the time goes:
time: 733 us; the launch traced here: 720 us
  blocking collectives  239 us (33%)
  local copies, waits for them, and re-layouts  183 us (25%)
  waiting for transfers between devices  117 us (16%)
  matrix products  99.8 us (14%)
  other arithmetic  59.5 us (8%)
  between operations  19.7 us (3%)
    psum x2, waiting for transfers between devices, body(): lax.psum(synthesize(coefficients, legendre_here, harmonic, cycle_ids), 'o...  117 us
    dynamic_update_slice x32, local copies, waits for them, and re-layouts, spread_cycles(): pieces = lax.map(one_block, cycle_ids.reshape(blocks, block))  110 us
    all_gather x3, blocking collectives, owner_rows(): everyone = lax.all_gather(summed, 'ord', axis=0, tiled=True)  92.2 us
    all_gather x2, blocking collectives, body(): block_everyone = lax.all_gather(direction, 'ord', axis=0, tiled=True)  61.4 us
    dynamic_slice x64, local copies, waits for them, and re-layouts, collect_cycles(): lax.scan(add_block, jnp.zeros((rows, cycle_count), jnp.float32), (cycle_i...  47 us
    dot_general x16, matrix products, one_block(): jnp.dot(onehot, flat_cycles.T, precision=PRECISE, preferred_element_type=...  40.8 us
    psum x2, blocking collectives, energy(): return lax.psum(jnp.sum(values * precond), 'ord')  39.6 us
    dot_general x24, matrix products, add_block(): jnp.dot(value_block, onehot, precision=PRECISE, preferred_element_type=jn...  36.9 us
  transfers between devices with their start and end apart: 2, of which 2 were waited for; matrix products, arithmetic and copies ran while one was open for 0% of the time, Pallas kernels for 0%

commit v1 on v0

v1 whole, which is shorter than its diff:
```python
import functools

import jax
import jax.numpy as jnp
from jax import lax
from jax.experimental import pallas as pl
from jax.experimental.pallas import tpu as pltpu
from jax.sharding import PartitionSpec as P

ITERS = 2
SEGMENTS = 2
CHUNK = 1024
F32 = jnp.float32
BF16 = jnp.bfloat16

VMEM = pl.BlockSpec(memory_space=pltpu.VMEM)
SMEM = pl.BlockSpec(memory_space=pltpu.SMEM)


def up(value, unit):
    return -(-value // unit) * unit


def iota(shape, axis):
    return lax.broadcasted_iota(jnp.int32, shape, axis)


class Sizes:
    def __init__(self, legendre, slab):
        self.cnt, self.nb, self.cyc = legendre.shape[1:]
        self.nord = lax.axis_size("ord")
        self.nobs = lax.axis_size("obs")
        self.no = self.cnt * self.nord
        self.slab = slab
        self.rows = slab // 128
        self.halves = self.cyc // 128
        self.steps = self.nb // 8
        per = 128 // self.steps
        while self.cnt % per or per * self.steps == 128:
            per -= 1
        self.per = per
        self.groups = self.cnt // per
        self.tiles = 2 * self.groups
        self.seg = SEGMENTS
        self.seg_len = self.nb // SEGMENTS
        self.seed_rows = 2 * self.seg + 1
        self.id_row = self.cnt * self.seed_rows
        self.seeds = up(self.id_row + 1, 8)
        self.pay = up(2 * self.cnt + 1, 8)
        self.off = up(self.no, 8)
        self.freq = up(2 * self.no - 1, 16)
        self.table = self.off + self.freq
        self.own = up(self.cnt, 16)


def seeds_kernel(z, first_ref, own_ref, leg_ref, out_ref, keep):
    i = pl.program_id(0)
    base = i * z.seed_rows
    for s in range(z.seg):
        for t in range(2):
            keep[pl.ds(base + 2 * s + t, 1), :] = leg_ref[0, 0, s * z.seg_len + t : s * z.seg_len + t + 1, :]
    order = first_ref[0] + i
    keep[pl.ds(base + 2 * z.seg, 1), :] = leg_ref[0, 0, pl.ds(order, 1), :]

    @pl.when(i == z.cnt - 1)
    def _():
        lane = iota((z.seeds - z.id_row, z.cyc), 1)
        ids = jnp.zeros(lane.shape, F32)
        for slot in range(z.cnt):
            ids = jnp.where(lane == slot, own_ref[slot].astype(F32), ids)
        keep[z.id_row :, :] = ids
        for d in range(z.nord):
            out_ref[d] = keep[...]


def make_seeds(z, first, own, legendre):
    return pl.pallas_call(
        functools.partial(seeds_kernel, z),
        grid=(z.cnt,),
        in_specs=[SMEM, SMEM, pl.BlockSpec((1, 1, z.nb, z.cyc), lambda i: (0, i, 0, 0))],
        out_specs=pl.BlockSpec((z.nord, z.seeds, z.cyc), lambda i: (0, 0, 0)),
        out_shape=jax.ShapeDtypeStruct((z.nord, z.seeds, z.cyc), F32),
        scratch_shapes=[pltpu.VMEM((z.seeds, z.cyc), F32)],
        name="seeds",
    )(first, own, legendre)


def sincos(angle):
    turn = jnp.round(angle * 0.6366197723675814)
    rest = angle - turn * 1.5703125
    rest = rest - turn * 4.837512969970703e-4
    rest = rest - turn * 7.549789948768648e-8
    sq = rest * rest
    sine = rest + rest * sq * (-0.16666654611 + sq * (8.3321608736e-3 + sq * -1.9515295891e-4))
    cosine = 1.0 - 0.5 * sq + sq * sq * (4.166664568298827e-2 + sq * (-1.388731625493765e-3 + sq * 2.443315711809948e-5))
    quarter = turn.astype(jnp.int32)
    odd = (quarter & 1) == 1
    c = jnp.where(odd, sine, cosine)
    s = jnp.where(odd, cosine, sine)
    c = jnp.where(((quarter + 1) & 2) == 2, -c, c)
    s = jnp.where((quarter & 2) == 2, -s, s)
    return c, s


def split(value):
    high = value.astype(BF16)
    return high, (value - high.astype(F32)).astype(BF16)


def tables_kernel(z, count_ref, own_ref, lon_ref, cyc_ref, data_ref, weight_ref, tc_ref, ts_ref, ty_ref,
                  bc, bs, yc, ys, c8, s8, lhs, hot, acc):
    total = z.slab * z.nobs
    lon = lon_ref[...]
    place = iota((z.rows, 128), 0) * 128 + iota((z.rows, 128), 1)
    scale = weight_ref[...] * (place < count_ref[0]).astype(F32) / total
    c1, s1 = sincos(lon)
    cp, sp = c1, s1
    bc[0 : z.rows, :] = scale
    bs[0 : z.rows, :] = jnp.zeros_like(scale)
    for p in range(1, 8):
        bc[p * z.rows : (p + 1) * z.rows, :] = scale * cp
        bs[p * z.rows : (p + 1) * z.rows, :] = scale * sp
        cp, sp = cp * c1 - sp * s1, sp * c1 + cp * s1
    c8[...] = cp
    s8[...] = sp
    scaled = scale * data_ref[...]

    def own_order(i, carry):
        c, s = sincos(own_ref[i].astype(F32) * lon_ref[...])
        yc[pl.ds(pl.multiple_of(i * z.rows, 8), z.rows), :] = c * scaled
        ys[pl.ds(pl.multiple_of(i * z.rows, 8), z.rows), :] = s * scaled
        return carry

    lax.fori_loop(0, z.cnt, own_order, 0)
    for i in range(z.cnt, z.own):
        yc[i * z.rows : (i + 1) * z.rows, :] = jnp.zeros_like(lon)
        ys[i * z.rows : (i + 1) * z.rows, :] = jnp.zeros_like(lon)
    acc[...] = jnp.zeros_like(acc)
    cycle_id = iota((z.cyc, 128), 0)
    top = 4 * z.freq
    width = min(CHUNK, z.slab) // 128

    def chunk(step, carry):
        for k in range(width):
            r = step * width + k
            lanes = slice(k * 128, (k + 1) * 128)
            c = bc[pl.ds(r, 8, stride=z.rows), :]
            s = bs[pl.ds(r, 8, stride=z.rows), :]
            cr = jnp.broadcast_to(c8[pl.ds(r, 1), :], (8, 128))
            sr = jnp.broadcast_to(s8[pl.ds(r, 1), :], (8, 128))
            for pair in range(z.freq // 16):
                c2 = c * cr - s * sr
                s2 = s * cr + c * sr
                high, low = split(jnp.concatenate([c, c2], 0))
                lhs[pair * 16 : pair * 16 + 16, lanes] = high
                lhs[z.freq + pair * 16 : z.freq + pair * 16 + 16, lanes] = low
                high, low = split(jnp.concatenate([s, s2], 0))
                lhs[2 * z.freq + pair * 16 : 2 * z.freq + pair * 16 + 16, lanes] = high
                lhs[3 * z.freq + pair * 16 : 3 * z.freq + pair * 16 + 16, lanes] = low
                c = c2 * cr - s2 * sr
                s = s2 * cr + c2 * sr
            for part, table in enumerate((yc, ys)):
                for block in range(z.own // 16):
                    a = table[pl.ds(block * 16 * z.rows + r, 8, stride=z.rows), :]
                    b = table[pl.ds((block * 16 + 8) * z.rows + r, 8, stride=z.rows), :]
                    high, low = split(jnp.concatenate([a, b], 0))
                    at = top + 2 * part * z.own + block * 16
                    lhs[at : at + 16, lanes] = high
                    lhs[at + z.own : at + z.own + 16, lanes] = low
            hot[:, lanes] = jnp.where(cycle_id == cyc_ref[pl.ds(r, 1), :], 1.0, 0.0).astype(BF16)
        acc[...] += lax.dot_general(lhs[...], hot[...], (((1,), (1,)), ((), ())), preferred_element_type=F32)
        return carry

    lax.fori_loop(0, z.rows // width, chunk, 0)
    for h in range(z.halves):
        lanes = slice(h * 128, (h + 1) * 128)
        tc_ref[h, z.off :, :] = acc[0 : z.freq, lanes] + acc[z.freq : 2 * z.freq, lanes]
        ts_ref[h, z.off :, :] = acc[2 * z.freq : 3 * z.freq, lanes] + acc[3 * z.freq : 4 * z.freq, lanes]

    def mirror(q, carry):
        for h in range(z.halves):
            tc_ref[h, pl.ds(z.off - q, 1), :] = tc_ref[h, pl.ds(z.off + q, 1), :]
            ts_ref[h, pl.ds(z.off - q, 1), :] = -ts_ref[h, pl.ds(z.off + q, 1), :]
        return carry

    lax.fori_loop(1, z.no, mirror, 0)
    for part in range(2):
        at = top + 2 * part * z.own
        for h in range(z.halves):
            lanes = slice(h * 128, (h + 1) * 128)
            ty_ref[h, part * z.cnt : (part + 1) * z.cnt, :] = (
                acc[at : at + z.cnt, lanes] + acc[at + z.own : at + z.own + z.cnt, lanes]
            )


def make_tables(z, count, own, lon, cyc, data, weight):
    lhs_rows = 4 * z.freq + 4 * z.own
    table = jax.ShapeDtypeStruct((z.halves, z.table, 128), F32)
    return pl.pallas_call(
        functools.partial(tables_kernel, z),
        in_specs=[SMEM, SMEM] + [VMEM] * 4,
        out_specs=[VMEM] * 3,
        out_shape=[table, table, jax.ShapeDtypeStruct((z.halves, z.pay, 128), F32)],
        scratch_shapes=[pltpu.VMEM((8 * z.rows, 128), F32)] * 2
        + [pltpu.VMEM((z.own * z.rows, 128), F32)] * 2
        + [pltpu.VMEM((z.rows, 128), F32)] * 2
        + [
            pltpu.VMEM((lhs_rows, min(CHUNK, z.slab)), BF16),
            pltpu.VMEM((z.cyc, min(CHUNK, z.slab)), BF16),
            pltpu.VMEM((lhs_rows, z.cyc), F32),
        ],
        name="tables",
    )(count, own, lon, cyc, data, weight)


def adjoint_into(z, func_ref, rows_ref, out_ref):
    lane = iota((8, 128), 1)

    def group(g, carry):
        tiles = [jnp.zeros((8, 128), F32)] * 2
        for p in range(z.per):
            slot = g * z.per + p
            w = [
                [
                    jnp.broadcast_to(rows_ref[h, pl.ds(k * z.cnt + slot, 1), :], (8, 128))
                    for h in range(z.halves)
                ]
                for k in range(2)
            ]
            for a in range(z.steps):
                at = pl.multiple_of(slot * z.nb + 8 * a, 8)
                f = [func_ref[h, pl.ds(at, 8), :] for h in range(z.halves)]
                for k in range(2):
                    prod = f[0] * w[k][0]
                    for h in range(1, z.halves):
                        prod = prod + f[h] * w[k][h]
                    tiles[k] = jnp.where(lane == p * z.steps + a, jnp.sum(prod, axis=1, keepdims=True), tiles[k])
        for k in range(2):
            out_ref[k * z.groups + g] = tiles[k]
        return carry

    lax.fori_loop(0, z.groups, group, 0)


def functions_kernel(z, own_ref, recv_ref, ty_ref, func_ref, out_ref, seed0, seed1, first):
    total = z.seg * z.cnt
    padded = up(total, 8)
    for slot in range(z.cnt):
        order = own_ref[slot]
        block = order // z.cnt
        base = (order - block * z.cnt) * z.seed_rows
        for s in range(z.seg):
            r = slot * z.seg + s
            seed0[r : r + 1, :] = recv_ref[block, pl.ds(base + 2 * s, 1), :]
            seed1[r : r + 1, :] = recv_ref[block, pl.ds(base + 2 * s + 1, 1), :]
            first[r : r + 1, :] = recv_ref[block, pl.ds(base + 2 * z.seg, 1), :]
    cosine = recv_ref[0, 1:2, :] / (recv_ref[0, 0:1, :] * 1.7320508075688772)
    lanes_len = up(z.seg_len, 128)
    row = iota((padded, lanes_len), 0)
    order_of = jnp.zeros(row.shape, F32)
    degree = jnp.zeros(row.shape, F32) + iota(row.shape, 1).astype(F32)
    for slot in range(z.cnt):
        for s in range(z.seg):
            hit = row == slot * z.seg + s
            order_of = jnp.where(hit, own_ref[slot].astype(F32), order_of)
            degree = jnp.where(hit, degree + float(s * z.seg_len), degree)
    minus = jnp.maximum(degree - order_of, 1.0)
    plus = jnp.maximum(degree + order_of, 1.0)
    rise = jnp.sqrt(jnp.maximum((2.0 * degree - 1.0) * (2.0 * degree + 1.0), 0.0) / (minus * plus))
    rise = jnp.where(degree > order_of, rise, 0.0)
    top = jnp.maximum((2.0 * degree + 1.0) * (degree + order_of - 1.0) * (degree - order_of - 1.0), 0.0)
    fall = jnp.sqrt(top / (minus * plus * jnp.maximum(2.0 * degree - 3.0, 1.0)))
    fall = jnp.where(degree > order_of + 1.0, fall, 0.0)
    starts = (degree == order_of).astype(F32)
    for h in range(z.halves):
        lanes = slice(h * 128, (h + 1) * 128)
        x = jnp.broadcast_to(cosine[:, lanes], (8, 128))
        for tile in range(padded // 8):
            rows = slice(tile * 8, tile * 8 + 8)
            left = min(8, total - tile * 8)
            before, prev = None, None
            for t in range(z.seg_len):
                if t == 0:
                    now = seed0[rows, lanes]
                elif t == 1:
                    now = seed1[rows, lanes]
                else:
                    now = (rise[rows, t : t + 1] * x) * prev - fall[rows, t : t + 1] * before
                    now = jnp.where(starts[rows, t : t + 1] > 0.5, first[rows, lanes], now)
                func_ref[h, pl.ds(tile * 8 * z.seg_len + t, left, stride=z.seg_len), :] = now[:left]
                before, prev = prev, now
    adjoint_into(z, func_ref, ty_ref, out_ref)


def make_functions(z, own, recv, ty):
    padded = up(z.seg * z.cnt, 8)
    return pl.pallas_call(
        functools.partial(functions_kernel, z),
        in_specs=[SMEM, VMEM, VMEM],
        out_specs=[VMEM] * 2,
        out_shape=[
            jax.ShapeDtypeStruct((z.halves, z.cnt * z.nb, 128), F32),
            jax.ShapeDtypeStruct((z.tiles, 8, 128), F32),
        ],
        scratch_shapes=[pltpu.VMEM((padded, z.cyc), F32)] * 3,
        name="functions",
    )(own, recv, ty)


def total_of(z, gathered_ref):
    summed = [gathered_ref[0, t] for t in range(z.tiles)]
    for b in range(1, z.nobs):
        summed = [summed[t] + gathered_ref[b, t] for t in range(z.tiles)]
    lane = iota((8, 128), 1)
    curvature = jnp.max(jnp.where((lane == 127) & (iota((8, 128), 0) == 0), summed[0], -jnp.inf), axis=1, keepdims=True)
    curvature = jnp.max(curvature, axis=0, keepdims=True)
    used = lane < z.per * z.steps
    return [jnp.where(used, s, 0.0) for s in summed], curvature


def full_sum(value):
    return jnp.sum(jnp.sum(value, axis=1, keepdims=True), axis=0, keepdims=True)


def step_kernel(z, later, own_ref, *refs):
    if later:
        gathered_ref, inv_ref, func_ref, energy_ref, res_ref, dir_ref = refs[:6]
        out_ref, newres_ref, prec_ref, sol_ref, flat = refs[6:]
    else:
        gathered_ref, inv_ref, func_ref = refs[:3]
        out_ref, newres_ref, prec_ref, flat = refs[3:]
    summed, curvature = total_of(z, gathered_ref)
    if later:
        step_size = energy_ref[0:1, 0:1] / curvature
        for t in range(z.tiles):
            sol_ref[t] = step_size * dir_ref[t]
            newres_ref[t] = res_ref[t] - step_size * summed[t]
    else:
        for t in range(z.tiles):
            newres_ref[t] = summed[t]
    lane = iota((8, 128), 1)
    wide = up(z.nb, 128)

    def apply(g, carry):
        for p in range(z.per):
            slot = g * z.per + p
            acc = [jnp.zeros((8, z.nb), F32)] * 2
            for a in range(z.steps):
                block = inv_ref[slot, 8 * a : 8 * a + 8, :]
                for k in range(2):
                    col = newres_ref[k * z.groups + g][:, p * z.steps + a : p * z.steps + a + 1]
                    acc[k] = acc[k] + block * col
            live = iota((1, z.nb), 1) >= own_ref[slot]
            for k in range(2):
                value = jnp.where(live, jnp.sum(acc[k], axis=0, keepdims=True), 0.0)
                for c in range(wide // 128):
                    size = min(128, z.nb - c * 128)
                    flat[c, pl.ds(k * z.cnt + slot, 1), 0:size] = value[:, c * 128 : c * 128 + size]
        return carry

    flat[...] = jnp.zeros_like(flat)
    lax.fori_loop(0, z.groups, apply, 0)
    columns = jnp.concatenate([flat[c].T for c in range(wide // 128)], 0)
    energy = jnp.zeros((8, 128), F32)
    for g in range(z.groups):
        tiles = [jnp.zeros((8, 128), F32)] * 2
        for p in range(z.per):
            slot = g * z.per + p
            acc = [[jnp.zeros((8, 128), F32)] * z.halves for k in range(2)]
            for a in range(z.steps):
                f = [func_ref[h, slot * z.nb + 8 * a : slot * z.nb + 8 * a + 8, :] for h in range(z.halves)]
                for k in range(2):
                    r = k * z.cnt + slot
                    col = jnp.broadcast_to(columns[8 * a : 8 * a + 8, r : r + 1], (8, 128))
                    tiles[k] = jnp.where(lane == p * z.steps + a, col, tiles[k])
                    for h in range(z.halves):
                        acc[k][h] = acc[k][h] + f[h] * col
            for k in range(2):
                r = k * z.cnt + slot
                for h in range(z.halves):
                    out_ref[0, r : r + 1, h * 128 : (h + 1) * 128] = jnp.sum(acc[k][h], axis=0, keepdims=True)
        for k in range(2):
            t = k * z.groups + g
            prec_ref[t] = tiles[k]
            energy = energy + tiles[k] * newres_ref[t]
    rest = z.pay - 2 * z.cnt
    out_ref[0, 2 * z.cnt :, :] = jnp.broadcast_to(full_sum(energy), (rest, z.cyc))
    for d in range(1, z.nord):
        out_ref[d] = out_ref[0]


def make_step(z, own, gathered, inv, func, state=None):
    later = state is not None
    tile = jax.ShapeDtypeStruct((z.tiles, 8, 128), F32)
    outs = [jax.ShapeDtypeStruct((z.nord, z.pay, z.cyc), F32), tile, tile] + [tile] * later
    args = [own, gathered, inv, func] + (list(state) if later else [])
    return pl.pallas_call(
        functools.partial(step_kernel, z, later),
        in_specs=[SMEM] + [VMEM] * (len(args) - 1),
        out_specs=[VMEM] * len(outs),
        out_shape=outs,
        scratch_shapes=[pltpu.VMEM((up(z.nb, 128) // 128, up(2 * z.cnt, 8), 128), F32)],
        name="step",
    )(*args)


def image_kernel(z, later, own_ref, ids_ref, recv_ref, tc_ref, ts_ref, func_ref, *refs):
    if later:
        old_ref, old_energy_ref, prec_ref, old_dir_ref = refs[:4]
        out_ref, energy_ref, dir_ref, val_ref, all_rows, rows = refs[4:]
    else:
        out_ref, energy_ref, val_ref, all_rows, rows = refs
    energy = recv_ref[0, 2 * z.cnt : 2 * z.cnt + 1, 0:128]
    for o in range(1, z.nord):
        energy = energy + recv_ref[o, 2 * z.cnt : 2 * z.cnt + 1, 0:128]
    energy_ref[...] = jnp.broadcast_to(energy, (8, 128))

    def place(o, carry):
        for i in range(z.cnt):
            order = ids_ref[o * z.cnt + i]
            for k in range(2):
                for h in range(z.halves):
                    val_ref[k, h, pl.ds(order, 1), :] = recv_ref[o, k * z.cnt + i : k * z.cnt + i + 1, h * 128 : (h + 1) * 128]
        return carry

    lax.fori_loop(0, z.nord, place, 0)
    if later:
        ratio = energy / old_energy_ref[0:1, :]
        for k in range(2):
            for h in range(z.halves):
                val_ref[k, h] = val_ref[k, h] + ratio * old_ref[k, h]
        for t in range(z.tiles):
            dir_ref[t] = prec_ref[t] + ratio * old_dir_ref[t]

    def one_order(m, total):
        for h in range(z.halves):
            vc, vs = val_ref[0, h], val_ref[1, h]
            near, far = tc_ref[h, pl.ds(z.off - m, z.no), :], tc_ref[h, pl.ds(z.off + m, z.no), :]
            snear, sfar = ts_ref[h, pl.ds(z.off - m, z.no), :], ts_ref[h, pl.ds(z.off + m, z.no), :]
            wc = 0.5 * jnp.sum((near + far) * vc + (sfar + snear) * vs, axis=0, keepdims=True)
            ws = 0.5 * jnp.sum((sfar - snear) * vc + (near - far) * vs, axis=0, keepdims=True)
            all_rows[h, pl.ds(m, 1), :] = wc
            all_rows[z.halves + h, pl.ds(m, 1), :] = ws
        return total

    lax.fori_loop(0, z.no, one_order, 0)
    curvature = jnp.zeros((z.no, 128), F32)
    for k in range(2):
        for h in range(z.halves):
            curvature = curvature + all_rows[k * z.halves + h] * val_ref[k, h]
    for i in range(z.cnt):
        for k in range(2):
            for h in range(z.halves):
                rows[h, k * z.cnt + i : k * z.cnt + i + 1, :] = all_rows[
                    k * z.halves + h, pl.ds(own_ref[i], 1), :
                ]
    adjoint_into(z, func_ref, rows, out_ref)
    mark = (iota((8, 128), 1) == 127) & (iota((8, 128), 0) == 0)
    out_ref[0] = jnp.where(mark, full_sum(curvature), out_ref[0])


def make_image(z, own, ids, recv, tc, ts, func, state=None):
    later = state is not None
    tile = jax.ShapeDtypeStruct((z.tiles, 8, 128), F32)
    outs = [tile, jax.ShapeDtypeStruct((8, 128), F32)] + [tile] * later
    outs.append(jax.ShapeDtypeStruct((2, z.halves, z.no, 128), F32))
    args = [own, ids, recv, tc, ts, func] + (list(state) if later else [])
    return pl.pallas_call(
        functools.partial(image_kernel, z, later),
        in_specs=[SMEM, SMEM] + [VMEM] * (len(args) - 2),
        out_specs=[VMEM] * len(outs),
        out_shape=outs,
        scratch_shapes=[
            pltpu.VMEM((2 * z.halves, z.no, 128), F32),
            pltpu.VMEM((z.halves, z.pay, 128), F32),
        ],
        name="image",
    )(*args)


def last_kernel(z, gathered_ref, energy_ref, res_ref, sol_ref, dir_ref, out_sol, out_res):
    summed, curvature = total_of(z, gathered_ref)
    step_size = energy_ref[0:1, 0:1] / curvature
    lane = iota((8, 128), 1)
    finals = (
        [sol_ref[t] + step_size * dir_ref[t] for t in range(z.tiles)],
        [res_ref[t] - step_size * summed[t] for t in range(z.tiles)],
    )
    wide = up(z.nb, 128)
    for tiles, out in zip(finals, (out_sol, out_res)):
        columns = []
        for a in range(z.steps):
            tile = jnp.zeros((8, 128), F32)
            for slot in range(z.cnt):
                g, p = divmod(slot, z.per)
                for k in range(2):
                    col = tiles[k * z.groups + g][:, p * z.steps + a : p * z.steps + a + 1]
                    tile = jnp.where(lane == 2 * slot + k, col, tile)
            columns.append(tile)
        columns += [jnp.zeros((8, 128), F32)] * ((wide - z.nb) // 8)
        for c in range(wide // 128):
            flat = jnp.concatenate(columns[16 * c : 16 * c + 16], 0).T
            size = min(128, z.nb - c * 128)
            for slot in range(z.cnt):
                out[slot, :, c * 128 : c * 128 + size] = flat[2 * slot : 2 * slot + 2, 0:size]


def make_last(z, gathered, energy, res, sol, direction):
    out = jax.ShapeDtypeStruct((z.cnt, 2, z.nb), F32)
    return pl.pallas_call(
        functools.partial(last_kernel, z),
        in_specs=[VMEM] * 5,
        out_specs=[VMEM] * 2,
        out_shape=[out, out],
        name="last",
    )(gathered, energy, res, sol, direction)


def body(longitude, cycle_of, obs_count, observed, obs_weight, legendre, precond_inv, order_of_slot):
    z = Sizes(legendre, longitude.shape[1])
    dense = lambda value: value.reshape(z.rows, 128)
    first = (lax.axis_index("ord") * z.cnt).astype(jnp.int32).reshape(1)
    seeds = make_seeds(z, first, order_of_slot, legendre)
    recv = lax.all_to_all(seeds, "ord", 0, 0)
    tc, ts, ty = make_tables(
        z, obs_count, order_of_slot, dense(longitude), dense(cycle_of), dense(observed), dense(obs_weight)
    )
    ids = recv[:, z.id_row, : z.cnt].reshape(z.no).astype(jnp.int32)
    func, part = make_functions(z, order_of_slot, recv, ty)
    gathered = lax.all_gather(part, "obs", axis=0)
    values, res, direction = make_step(z, order_of_slot, gathered, precond_inv, func)
    recv = lax.all_to_all(values, "ord", 0, 0)
    part, energy, all_values = make_image(z, order_of_slot, ids, recv, tc, ts, func)
    gathered = lax.all_gather(part, "obs", axis=0)
    values, res, prec, sol = make_step(z, order_of_slot, gathered, precond_inv, func, (energy, res, direction))
    recv = lax.all_to_all(values, "ord", 0, 0)
    part, energy, direction, all_values = make_image(
        z, order_of_slot, ids, recv, tc, ts, func, (all_values, energy, prec, direction)
    )
    gathered = lax.all_gather(part, "obs", axis=0)
    return tuple(make_last(z, gathered, energy, res, sol, direction))


def solution(mesh):
    placed = (
        P("obs", None),
        P("obs", None),
        P("obs"),
        P("obs", None),
        P("obs", None),
        P("obs", "ord", None, None),
        P("ord", None, None),
        P("ord"),
    )
    return jax.shard_map(
        body,
        mesh=mesh,
        in_specs=placed,
        out_specs=(P("ord", None, None), P("ord", None, None)),
        check_vma=False,
    )
```

time: 733 us -> 136 us (0.19); the launches traced: 720 us -> 135 us
  blocking collectives: 239 us -> 32.1 us
  local copies, waits for them, and re-layouts: 183 us -> 2.06 us
  waiting for transfers between devices: 117 us -> 7.07 us
  matrix products: 99.8 us -> 0 us
  Pallas kernels: 0 us -> 78.8 us
  other arithmetic: 59.5 us -> 0.78 us
  between operations: 19.7 us -> 1.3 us
  starting transfers between devices: 0.08 us -> 13.3 us
    all_gather x5 -> x3, blocking collectives: 154 us -> 19.3 us  [body(): gathered = lax.all_gather(part, 'obs', axis=0)]
    psum x2 -> x0, waiting for transfers between devices: 117 us -> none  [body(): lax.psum(synthesize(coefficients, legendre_here, harmonic, cycle_ids), 'o...]
    dynamic_update_slice x32 -> x0, local copies, waits for them, and re-layouts: 110 us -> none  [spread_cycles(): pieces = lax.map(one_block, cycle_ids.reshape(blocks, block))]
    dot_general x47 -> x0, matrix products: 99.8 us -> none  [the longest x16 40.8 us: one_block(): jnp.dot(onehot, flat_cycles.T, precision=PRECISE, preferred_element_type=...]
    pallas_call x0 -> x8, Pallas kernels: none -> 78.8 us  [the longest x1 34.7 us: make_tables(): pl.pallas_call(functools.partial(tables_kernel, z), in_specs=[SMEM, SMEM]...]
    psum x5 -> x0, blocking collectives: 72.5 us -> none  [the longest x2 39.6 us: energy(): return lax.psum(jnp.sum(values * precond), 'ord')]
    dynamic_slice x64 -> x0, local copies, waits for them, and re-layouts: 47 us -> none  [collect_cycles(): lax.scan(add_block, jnp.zeros((rows, cycle_count), jnp.float32), (cycle_i...]
    cos x1 -> x0, other arithmetic: 33.9 us -> none  [body(): harmonic = jnp.stack([jnp.cos(angles), jnp.sin(angles)], axis=1)]
  transfers between devices with their start and end apart: 2 -> 2, of which waited for: 2 -> 1; matrix products, arithmetic and copies ran while one was open for 0% -> 1% of each run, Pallas kernels for 0% -> 26%
where the time goes in v1:
time: 136 us; the launch traced here: 135 us
  Pallas kernels  78.8 us (58%)
  blocking collectives  32.1 us (24%)
  starting transfers between devices  13.3 us (10%)
  waiting for transfers between devices  7.07 us (5%)
  local copies, waits for them, and re-layouts  2.06 us (2%)
    pallas_call x1, Pallas kernels, make_tables(): pl.pallas_call(functools.partial(tables_kernel, z), in_specs=[SMEM, SMEM]...  34.7 us
    all_gather x3, blocking collectives, body(): gathered = lax.all_gather(part, 'obs', axis=0)  19.3 us
    pallas_call x2, Pallas kernels, make_image(): pl.pallas_call(functools.partial(image_kernel, z, later), in_specs=[SMEM,...  16.1 us
    all_to_all x1, blocking collectives, body(): recv = lax.all_to_all(values, 'ord', 0, 0)  12.7 us
    pallas_call x2, Pallas kernels, make_step(): pl.pallas_call(functools.partial(step_kernel, z, later), in_specs=[SMEM]...  12.7 us
    all_to_all x1, starting transfers between devices, body(): recv = lax.all_to_all(seeds, 'ord', 0, 0)  7.31 us
    all_to_all x1, waiting for transfers between devices, body(): recv = lax.all_to_all(values, 'ord', 0, 0)  7.07 us
    all_to_all x1, starting transfers between devices, body(): recv = lax.all_to_all(values, 'ord', 0, 0)  6 us
  transfers between devices with their start and end apart: 2, of which 1 were waited for; matrix products, arithmetic and copies ran while one was open for 1% of the time, Pallas kernels for 26%

profile of v1, /device:TPU:0, one launch (start us, length us, event | category | flops | bytes accessed | tf_op | source)
XLA Modules:
  0.0 135.4 jit_solution(13294193367728153214)
XLA Ops:
  0.6 5.8 %seeds.1 = f32[8,48,256]{2,1,0:T(8,128)} custom-call(s32[1]{0:T(128)} %bitcast.first_ref, s32[9]{0:T(128)} %own_ref.13, f32[1,9,288,256]{3,2,1,0:T(8,128)} %leg_ref.1), custom_call_target="tpu_custom_call" | custom-call | tf_op jit(solution)/shard_map/seeds/pallas_call | solution.py:77
  6.5 7.3 %all-to-all-start = ((f32[8,48,256]{2,1,0:T(8,128)}), f32[8,48,256]{2,1,0:T(8,128)S(1)}, u32[]{:S(2)}, u32[]{:S(2)}) async-start(f32[8,48,256]{2,1,0:T(8,128)} %seeds.1), calls=%async_computation | async-start | bytes 786432 | tf_op jit(solution)/shard_map/all_to_all | solution.py:524
  14.4 34.7 %tables.1 = (f32[2,216,128]{2,1,0:T(8,128)}, f32[2,216,128]{2,1,0:T(8,128)}, f32[2,24,128]{2,1,0:T(8,128)}) custom-call(s32[1]{0:T(128)S(6)} %copy.10.count_ref, s32[9]{0:T(128)} %own_ref.13, f32[256,128]{1,0:T(8,128)} %bitcast.11, s32[256,128]{1,0:T(8,128)} %bitcast.12, f32[256,128]{1,0:T(8,128)} %bitcast.13, f32[256,128]{1,0:T(8,128)} %bitcast.14), custom_call_target="tpu_custom_call" | custom-call | tf_op jit(solution)/shard_map/tables/pallas_call | solution.py:199
  49.1 0.0 all-to-all-done.recv_ref
  49.1 0.0 copy-start
  49.1 0.8 copy-done
  49.9 5.4 %functions.1 = (f32[2,2592,128]{2,1,0:T(8,128)}, f32[6,8,128]{2,1,0:T(8,128)}) custom-call(s32[9]{0:T(128)} %own_ref.13, f32[8,48,256]{2,1,0:T(8,128)} %copy-done, f32[2,24,128]{2,1,0:T(8,128)} %get-tuple-element.20.ty_ref), custom_call_target="tpu_custom_call" | custom-call | tf_op jit(solution)/shard_map/functions/pallas_call | solution.py:297
  55.3 6.8 %all-gather = f32[24,8,128]{2,1,0:T(8,128)} all-gather(f32[6,8,128]{2,1,0:T(8,128)} %get-tuple-element.21), channel_id=2, replica_groups=mesh['obs'=4,'ord'=8] {'obs'}, dimensions={0}, use_global_device_ids=true | all-gather | bytes 122880 | tf_op jit(solution)/shard_map/all_gather | solution.py:530
  62.1 6.3 %step.2 = (f32[8,24,256]{2,1,0:T(8,128)}, f32[6,8,128]{2,1,0:T(8,128)}, f32[6,8,128]{2,1,0:T(8,128)}) custom-call(s32[9]{0:T(128)} %own_ref.13, f32[4,6,8,128]{3,2,1,0:T(8,128)} %bitcast.10, f32[9,288,288]{2,1,0:T(8,128)} %refs_1_.3, f32[2,2592,128]{2,1,0:T(8,128)} %get-tuple-element.22.refs_2_.func_ref), custom_call_target="tpu_custom_call" | custom-call | tf_op jit(solution)/shard_map/step/pallas_call | solution.py:397
  68.4 6.0 %all-to-all-start.1 = ((f32[8,24,256]{2,1,0:T(8,128)}), f32[8,24,256]{2,1,0:T(8,128)S(1)}, u32[]{:S(2)}, u32[]{:S(2)}) async-start(f32[8,24,256]{2,1,0:T(8,128)} %get-tuple-element.23), calls=%async_computation.1 | async-start | bytes 393216 | tf_op jit(solution)/shard_map/all_to_all | solution.py:532
  74.4 0.8 fusion
  75.2 0.6 convert_element_type.6.ids_ref
  75.8 7.1 %all-to-all-done.1.recv_ref = f32[8,24,256]{2,1,0:T(8,128)S(1)} async-done(((f32[8,24,256]{2,1,0:T(8,128)}), f32[8,24,256]{2,1,0:T(8,128)S(1)}, u32[]{:S(2)}, u32[]{:S(2)}) %all-to-all-start.1) | async-done | bytes 196640 | tf_op jit(solution)/shard_map/all_to_all | solution.py:532
  82.9 0.0 copy-start.1
  82.9 0.7 copy-done.1
  83.5 8.1 %image.2 = (f32[6,8,128]{2,1,0:T(8,128)}, f32[8,128]{1,0:T(8,128)}, f32[2,2,72,128]{3,2,1,0:T(8,128)}) custom-call(s32[9]{0:T(128)} %own_ref.13, s32[72]{0:T(128)} %convert_element_type.6.ids_ref, f32[8,24,256]{2,1,0:T(8,128)} %copy-done.1, f32[2,216,128]{2,1,0:T(8,128)} %get-tuple-element.24.tc_ref, f32[2,216,128]{2,1,0:T(8,128)} %get-tuple-element.25.ts_ref, ...), custom_call_target="tpu_custom_call" | custom-call | tf_op jit(solution)/shard_map/image/pallas_call | solution.py:468
  91.6 6.0 %all-gather.1 = f32[24,8,128]{2,1,0:T(8,128)} all-gather(f32[6,8,128]{2,1,0:T(8,128)} %get-tuple-element.26), channel_id=3, replica_groups=mesh['obs'=4,'ord'=8] {'obs'}, dimensions={0}, use_global_device_ids=true | all-gather | bytes 122880 | tf_op jit(solution)/shard_map/all_gather | solution.py:534
  97.6 6.4 %step.3 = (f32[8,24,256]{2,1,0:T(8,128)}, f32[6,8,128]{2,1,0:T(8,128)}, f32[6,8,128]{2,1,0:T(8,128)}, f32[6,8,128]{2,1,0:T(8,128)}) custom-call(s32[9]{0:T(128)} %own_ref.13, f32[4,6,8,128]{3,2,1,0:T(8,128)} %bitcast.9, f32[9,288,288]{2,1,0:T(8,128)} %refs_1_.3, f32[2,2592,128]{2,1,0:T(8,128)} %get-tuple-element.22.refs_2_.func_ref, ...), custom_call_target="tpu_custom_call" | custom-call | tf_op jit(solution)/shard_map/step/pallas_call | solution.py:397
  104.0 12.7 %all_to_all.15.recv_ref = f32[8,24,256]{2,1,0:T(8,128)} all-to-all(f32[8,24,256]{2,1,0:T(8,128)} %get-tuple-element.30), channel_id=1, replica_groups=mesh['obs'=4,'ord'=8] {'ord'}, dimensions={0} | all-to-all | bytes 393216 | tf_op jit(solution)/shard_map/all_to_all | solution.py:536
  116.8 8.0 %image.3 = (f32[6,8,128]{2,1,0:T(8,128)}, f32[8,128]{1,0:T(8,128)}, f32[6,8,128]{2,1,0:T(8,128)}, f32[2,2,72,128]{3,2,1,0:T(8,128)}) custom-call(s32[9]{0:T(128)} %own_ref.13, s32[72]{0:T(128)} %convert_element_type.6.ids_ref, f32[8,24,256]{2,1,0:T(8,128)} %all_to_all.15.recv_ref, f32[2,216,128]{2,1,0:T(8,128)} %get-tuple-element.24.tc_ref, ...), custom_call_target="tpu_custom_call" | custom-call | tf_op jit(solution)/shard_map/image/pallas_call | solution.py:468
  124.8 6.6 %all-gather.2 = f32[24,8,128]{2,1,0:T(8,128)} all-gather(f32[6,8,128]{2,1,0:T(8,128)} %get-tuple-element.33), channel_id=4, replica_groups=mesh['obs'=4,'ord'=8] {'obs'}, dimensions={0}, use_global_device_ids=true | all-gather | bytes 122880 | tf_op jit(solution)/shard_map/all_gather | solution.py:540
  131.4 4.0 %last.1 = (f32[9,2,288]{2,1,0:T(2,128)}, f32[9,2,288]{2,1,0:T(2,128)}) custom-call(f32[4,6,8,128]{3,2,1,0:T(8,128)} %bitcast.8, f32[8,128]{1,0:T(8,128)} %get-tuple-element.34.energy_ref, f32[6,8,128]{2,1,0:T(8,128)} %get-tuple-element.35.res_ref, f32[6,8,128]{2,1,0:T(8,128)} %get-tuple-element.36.sol_ref, f32[6,8,128]{2,1,0:T(8,128)} %get-tuple-element.37.dir_ref), custom_call_target="tpu_custom_call" | custom-call | tf_op jit(solution)/shard_map/last/pallas_call | solution.py:510
Async XLA Ops:
  6.5 42.7 %all-to-all-start = ((f32[8,48,256]{2,1,0:T(8,128)}), f32[8,48,256]{2,1,0:T(8,128)S(1)}, u32[]{:S(2)}, u32[]{:S(2)}) async-start(f32[8,48,256]{2,1,0:T(8,128)} %seeds.1), calls=%async_computation | async-start | bytes 786432 | tf_op jit(solution)/shard_map/all_to_all | solution.py:524
  49.1 0.8 copy-start
  68.4 14.5 %all-to-all-start.1 = ((f32[8,24,256]{2,1,0:T(8,128)}), f32[8,24,256]{2,1,0:T(8,128)S(1)}, u32[]{:S(2)}, u32[]{:S(2)}) async-start(f32[8,24,256]{2,1,0:T(8,128)} %get-tuple-element.23), calls=%async_computation.1 | async-start | bytes 393216 | tf_op jit(solution)/shard_map/all_to_all | solution.py:532
  82.9 0.7 copy-start.1

commit v2 on v1

--- a/solution.py
+++ b/solution.py
@@ -9,12 +9,16 @@
 
 ITERS = 2
 SEGMENTS = 2
+VMEM_LIMIT = 24 << 20
+WINDOW = 32
+UNROLL = 4
 CHUNK = 1024
 F32 = jnp.float32
 BF16 = jnp.bfloat16
 
 VMEM = pl.BlockSpec(memory_space=pltpu.VMEM)
 SMEM = pl.BlockSpec(memory_space=pltpu.SMEM)
+HBM = pl.BlockSpec(memory_space=pltpu.MemorySpace.HBM)
 
 
 def up(value, unit):
@@ -48,39 +52,75 @@
         self.seeds = up(self.id_row + 1, 8)
         self.pay = up(2 * self.cnt + 1, 8)
         self.off = up(self.no, 8)
-        self.freq = up(2 * self.no - 1, 16)
-        self.table = self.off + self.freq
-        self.own = up(self.cnt, 16)
-
-
-def seeds_kernel(z, first_ref, own_ref, leg_ref, out_ref, keep):
-    i = pl.program_id(0)
-    base = i * z.seed_rows
-    for s in range(z.seg):
-        for t in range(2):
-            keep[pl.ds(base + 2 * s + t, 1), :] = leg_ref[0, 0, s * z.seg_len + t : s * z.seg_len + t + 1, :]
-    order = first_ref[0] + i
-    keep[pl.ds(base + 2 * z.seg, 1), :] = leg_ref[0, 0, pl.ds(order, 1), :]
-
-    @pl.when(i == z.cnt - 1)
-    def _():
-        lane = iota((z.seeds - z.id_row, z.cyc), 1)
-        ids = jnp.zeros(lane.shape, F32)
-        for slot in range(z.cnt):
-            ids = jnp.where(lane == slot, own_ref[slot].astype(F32), ids)
-        keep[z.id_row :, :] = ids
-        for d in range(z.nord):
-            out_ref[d] = keep[...]
+        self.share = -(-(2 * self.no - 1) // self.nord)
+        self.freq = self.share * self.nord
+        self.table = up(self.off + self.freq, 8)
+        self.sums = up(2 * (self.share + self.cnt), 16)
+        self.pay_first = up(2 * self.cnt + 1 + 2 * self.share, 8)
+        self.width = min(CHUNK // 128, self.rows)
+        self.chunks = self.rows // self.width
+        self.windows = self.cyc // WINDOW
+        self.skew = self.rows + 1
+        self.seg_skew = self.seg_len + 1
+        self.func_rows = up(self.cnt * self.seg * self.seg_skew, 8)
+        self.pairs = up(self.chunks + self.windows - 1, UNROLL)
+        self.sum_lanes = up(2 * self.sums, 128)
+        self.limit = VMEM_LIMIT
+
+    def func_row(self, slot, a):
+        segment, at = divmod(8 * a, self.seg_len)
+        return (slot * self.seg + segment) * self.seg_skew + at
+
+
+def send_copies(z, source, out_ref, sems):
+    copies = [pltpu.make_async_copy(source, out_ref.at[d], sems.at[d]) for d in range(z.nord)]
+    for copy in copies:
+        copy.start()
+    for copy in copies:
+        copy.wait()
+
+
+def seeds_kernel(z, first_ref, own_ref, leg_ref, out_ref, stage, keep, sems, out_sems):
+    copies = []
+    for i in range(z.cnt):
+        aligned = pl.multiple_of((first_ref[0] + i) // 8 * 8, 8)
+        for s in range(z.seg + 1):
+            at = aligned if s == z.seg else s * z.seg_len
+            n = i * (z.seg + 1) + s
+            copies.append(pltpu.make_async_copy(leg_ref.at[0, i, pl.ds(at, 8), :], stage.at[n], sems.at[n]))
+    for copy in copies:
+        copy.start()
+    lane = iota((z.seeds - z.id_row, z.cyc), 1)
+    ids = jnp.zeros(lane.shape, F32)
+    for slot in range(z.cnt):
+        ids = jnp.where(lane == slot, own_ref[slot].astype(F32), ids)
+    keep[z.id_row :, :] = ids
+    for copy in copies:
+        copy.wait()
+    for i in range(z.cnt):
+        base = i * z.seed_rows
+        for s in range(z.seg):
+            keep[base + 2 * s : base + 2 * s + 2, :] = stage[i * (z.seg + 1) + s, 0:2, :]
+        order = first_ref[0] + i
+        block = stage[i * (z.seg + 1) + z.seg]
+        mine = iota((8, z.cyc), 0) == order - order // 8 * 8
+        keep[base + 2 * z.seg : base + 2 * z.seg + 1, :] = jnp.sum(jnp.where(mine, block, 0.0), axis=0, keepdims=True)
+    send_copies(z, keep, out_ref, out_sems)
 
 
 def make_seeds(z, first, own, legendre):
     return pl.pallas_call(
         functools.partial(seeds_kernel, z),
-        grid=(z.cnt,),
-        in_specs=[SMEM, SMEM, pl.BlockSpec((1, 1, z.nb, z.cyc), lambda i: (0, i, 0, 0))],
-        out_specs=pl.BlockSpec((z.nord, z.seeds, z.cyc), lambda i: (0, 0, 0)),
-        out_shape=jax.ShapeDtypeStruct((z.nord, z.seeds, z.cyc), F32),
-        scratch_shapes=[pltpu.VMEM((z.seeds, z.cyc), F32)],
+        in_specs=[SMEM, SMEM, HBM],
+        out_specs=HBM,
+        out_shape=pltpu.MemorySpace.HBM((z.nord, z.seeds, z.cyc), F32),
+        scratch_shapes=[
+            pltpu.VMEM((z.cnt * (z.seg + 1), 8, z.cyc), F32),
+            pltpu.VMEM((z.seeds, z.cyc), F32),
+            pltpu.SemaphoreType.DMA((z.cnt * (z.seg + 1),)),
+            pltpu.SemaphoreType.DMA((z.nord,)),
+        ],
+        compiler_params=pltpu.CompilerParams(vmem_limit_bytes=z.limit),
         name="seeds",
     )(first, own, legendre)
 
@@ -107,110 +147,117 @@
     return high, (value - high.astype(F32)).astype(BF16)
 
 
-def tables_kernel(z, count_ref, own_ref, lon_ref, cyc_ref, data_ref, weight_ref, tc_ref, ts_ref, ty_ref,
-                  bc, bs, yc, ys, c8, s8, lhs, hot, acc):
+def tables_kernel(z, base_ref, count_ref, own_ref, lon_ref, cyc_ref, data_ref, weight_ref,
+                  sum_ref, ty_ref, val, cyc_row, lhs, hot, acc, ids, pair_chunk, pair_window, sems):
+    scalars = pltpu.make_async_copy(cyc_ref, ids, sems.at[0])
+    scalars.start()
     total = z.slab * z.nobs
-    lon = lon_ref[...]
-    place = iota((z.rows, 128), 0) * 128 + iota((z.rows, 128), 1)
-    scale = weight_ref[...] * (place < count_ref[0]).astype(F32) / total
-    c1, s1 = sincos(lon)
-    cp, sp = c1, s1
-    bc[0 : z.rows, :] = scale
-    bs[0 : z.rows, :] = jnp.zeros_like(scale)
-    for p in range(1, 8):
-        bc[p * z.rows : (p + 1) * z.rows, :] = scale * cp
-        bs[p * z.rows : (p + 1) * z.rows, :] = scale * sp
-        cp, sp = cp * c1 - sp * s1, sp * c1 + cp * s1
-    c8[...] = cp
-    s8[...] = sp
-    scaled = scale * data_ref[...]
-
-    def own_order(i, carry):
-        c, s = sincos(own_ref[i].astype(F32) * lon_ref[...])
-        yc[pl.ds(pl.multiple_of(i * z.rows, 8), z.rows), :] = c * scaled
-        ys[pl.ds(pl.multiple_of(i * z.rows, 8), z.rows), :] = s * scaled
+    size = min(32, z.rows)
+
+    def block(i, carry):
+        at = pl.multiple_of(i * size, 8)
+        lon = lon_ref[pl.ds(at, size), :]
+        place = at * 128 + iota((size, 128), 0) * 128 + iota((size, 128), 1)
+        scale = weight_ref[pl.ds(at, size), :] * (place < count_ref[0]).astype(F32) / total
+        c1, s1 = sincos(lon)
+        c, s = sincos(base_ref[0].astype(F32) * lon)
+        c, s = c * scale, s * scale
+        for p in range(z.share):
+            val[pl.ds(p * z.skew + at, size), :] = c
+            val[pl.ds((z.share + p) * z.skew + at, size), :] = s
+            c, s = c * c1 - s * s1, s * c1 + c * s1
+        scaled = scale * data_ref[pl.ds(at, size), :]
+        for slot in range(z.cnt):
+            c, s = sincos(own_ref[slot].astype(F32) * lon)
+            val[pl.ds((2 * z.share + slot) * z.skew + at, size), :] = c * scaled
+            val[pl.ds((2 * z.share + z.cnt + slot) * z.skew + at, size), :] = s * scaled
+        for row in range(2 * (z.share + z.cnt), z.sums):
+            val[pl.ds(row * z.skew + at, size), :] = jnp.zeros((size, 128), F32)
+        cyc_row[pl.ds(at, size), :] = cyc_ref[pl.ds(at, size), :].astype(F32)
         return carry
 
-    lax.fori_loop(0, z.cnt, own_order, 0)
-    for i in range(z.cnt, z.own):
-        yc[i * z.rows : (i + 1) * z.rows, :] = jnp.zeros_like(lon)
-        ys[i * z.rows : (i + 1) * z.rows, :] = jnp.zeros_like(lon)
+    lax.fori_loop(0, z.rows // size, block, 0)
     acc[...] = jnp.zeros_like(acc)
-    cycle_id = iota((z.cyc, 128), 0)
-    top = 4 * z.freq
-    width = min(CHUNK, z.slab) // 128
-
-    def chunk(step, carry):
+    width = z.width
+
+    def fill(c, carry):
         for k in range(width):
-            r = step * width + k
+            r = c * width + k
             lanes = slice(k * 128, (k + 1) * 128)
-            c = bc[pl.ds(r, 8, stride=z.rows), :]
-            s = bs[pl.ds(r, 8, stride=z.rows), :]
-            cr = jnp.broadcast_to(c8[pl.ds(r, 1), :], (8, 128))
-            sr = jnp.broadcast_to(s8[pl.ds(r, 1), :], (8, 128))
-            for pair in range(z.freq // 16):
-                c2 = c * cr - s * sr
-                s2 = s * cr + c * sr
-                high, low = split(jnp.concatenate([c, c2], 0))
-                lhs[pair * 16 : pair * 16 + 16, lanes] = high
-                lhs[z.freq + pair * 16 : z.freq + pair * 16 + 16, lanes] = low
-                high, low = split(jnp.concatenate([s, s2], 0))
-                lhs[2 * z.freq + pair * 16 : 2 * z.freq + pair * 16 + 16, lanes] = high
-                lhs[3 * z.freq + pair * 16 : 3 * z.freq + pair * 16 + 16, lanes] = low
-                c = c2 * cr - s2 * sr
-                s = s2 * cr + c2 * sr
-            for part, table in enumerate((yc, ys)):
-                for block in range(z.own // 16):
-                    a = table[pl.ds(block * 16 * z.rows + r, 8, stride=z.rows), :]
-                    b = table[pl.ds((block * 16 + 8) * z.rows + r, 8, stride=z.rows), :]
-                    high, low = split(jnp.concatenate([a, b], 0))
-                    at = top + 2 * part * z.own + block * 16
-                    lhs[at : at + 16, lanes] = high
-                    lhs[at + z.own : at + z.own + 16, lanes] = low
-            hot[:, lanes] = jnp.where(cycle_id == cyc_ref[pl.ds(r, 1), :], 1.0, 0.0).astype(BF16)
-        acc[...] += lax.dot_general(lhs[...], hot[...], (((1,), (1,)), ((), ())), preferred_element_type=F32)
+            for pair in range(z.sums // 16):
+                first = val[pl.ds(pair * 16 * z.skew + r, 8, stride=z.skew), :]
+                second = val[pl.ds((pair * 16 + 8) * z.skew + r, 8, stride=z.skew), :]
+                high, low = split(jnp.concatenate([first, second], 0))
+                lhs[c, pair * 16 : pair * 16 + 16, lanes] = high
+                lhs[c, z.sums + pair * 16 : z.sums + pair * 16 + 16, lanes] = low
         return carry
 
-    lax.fori_loop(0, z.rows // width, chunk, 0)
+    lax.fori_loop(0, z.chunks, fill, 0)
+    scalars.wait()
+    for n in range(z.pairs):
+        pair_chunk[n] = 0
+        pair_window[n] = z.windows
+
+    def list_chunk(c, count):
+        low = ids[c * width, 0] // WINDOW
+        high = ids[c * width + width - 1, 127] // WINDOW
+
+        def add(w, at):
+            pair_chunk[at] = c
+            pair_window[at] = w
+            return at + 1
+
+        return lax.fori_loop(low, high + 1, add, count)
+
+    lax.fori_loop(0, z.chunks, list_chunk, 0)
+    cycle_id = iota((WINDOW, 128), 0).astype(F32)
+
+    def some(step, carry):
+        for u in range(UNROLL):
+            c = pair_chunk[step * UNROLL + u]
+            w = pair_window[step * UNROLL + u]
+            base = (w * WINDOW).astype(F32)
+            for k in range(width):
+                here = cyc_row[pl.ds(c * width + k, 1), :] - base
+                hot[u, :, k * 128 : (k + 1) * 128] = jnp.where(cycle_id == here, 1.0, 0.0).astype(BF16)
+            acc[w] += lax.dot_general(hot[u], lhs[c], (((1,), (1,)), ((), ())), preferred_element_type=F32)
+        return carry
+
+    lax.fori_loop(0, z.pairs // UNROLL, some, 0)
+    both = 2 * z.share
+    per_half = 128 // WINDOW
     for h in range(z.halves):
-        lanes = slice(h * 128, (h + 1) * 128)
-        tc_ref[h, z.off :, :] = acc[0 : z.freq, lanes] + acc[z.freq : 2 * z.freq, lanes]
-        ts_ref[h, z.off :, :] = acc[2 * z.freq : 3 * z.freq, lanes] + acc[3 * z.freq : 4 * z.freq, lanes]
-
-    def mirror(q, carry):
-        for h in range(z.halves):
-            tc_ref[h, pl.ds(z.off - q, 1), :] = tc_ref[h, pl.ds(z.off + q, 1), :]
-            ts_ref[h, pl.ds(z.off - q, 1), :] = -ts_ref[h, pl.ds(z.off + q, 1), :]
-        return carry
-
-    lax.fori_loop(1, z.no, mirror, 0)
-    for part in range(2):
-        at = top + 2 * part * z.own
-        for h in range(z.halves):
-            lanes = slice(h * 128, (h + 1) * 128)
-            ty_ref[h, part * z.cnt : (part + 1) * z.cnt, :] = (
-                acc[at : at + z.cnt, lanes] + acc[at + z.own : at + z.own + z.cnt, lanes]
-            )
-
-
-def make_tables(z, count, own, lon, cyc, data, weight):
-    lhs_rows = 4 * z.freq + 4 * z.own
-    table = jax.ShapeDtypeStruct((z.halves, z.table, 128), F32)
+        flat = jnp.concatenate([acc[h * per_half + w] for w in range(per_half)], 0)
+        flat = jnp.concatenate([flat[:, c * 128 : (c + 1) * 128].T for c in range(z.sum_lanes // 128)], 0)
+        sum_ref[h, 0:both, :] = flat[0:both] + flat[z.sums : z.sums + both]
+        ty_ref[h, 0 : 2 * z.cnt, :] = (
+            flat[both : both + 2 * z.cnt] + flat[z.sums + both : z.sums + both + 2 * z.cnt]
+        )
+
+
+def make_tables(z, base, count, own, lon, cyc, data, weight):
     return pl.pallas_call(
         functools.partial(tables_kernel, z),
-        in_specs=[SMEM, SMEM] + [VMEM] * 4,
-        out_specs=[VMEM] * 3,
-        out_shape=[table, table, jax.ShapeDtypeStruct((z.halves, z.pay, 128), F32)],
-        scratch_shapes=[pltpu.VMEM((8 * z.rows, 128), F32)] * 2
-        + [pltpu.VMEM((z.own * z.rows, 128), F32)] * 2
-        + [pltpu.VMEM((z.rows, 128), F32)] * 2
-        + [
-            pltpu.VMEM((lhs_rows, min(CHUNK, z.slab)), BF16),
-            pltpu.VMEM((z.cyc, min(CHUNK, z.slab)), BF16),
-            pltpu.VMEM((lhs_rows, z.cyc), F32),
+        in_specs=[SMEM, SMEM, SMEM] + [VMEM] * 4,
+        out_specs=[VMEM] * 2,
+        out_shape=[
+            jax.ShapeDtypeStruct((z.halves, up(2 * z.share, 8), 128), F32),
+            jax.ShapeDtypeStruct((z.halves, z.pay, 128), F32),
         ],
+        scratch_shapes=[
+            pltpu.VMEM((up(z.sums * z.skew, 8), 128), F32),
+            pltpu.VMEM((z.rows, 128), F32),
+            pltpu.VMEM((z.chunks, z.sum_lanes, z.width * 128), BF16),
+            pltpu.VMEM((UNROLL, WINDOW, z.width * 128), BF16),
+            pltpu.VMEM((z.windows + 1, WINDOW, z.sum_lanes), F32),
+            pltpu.SMEM((z.rows, 128), jnp.int32),
+            pltpu.SMEM((z.pairs,), jnp.int32),
+            pltpu.SMEM((z.pairs,), jnp.int32),
+            pltpu.SemaphoreType.DMA((1,)),
+        ],
+        compiler_params=pltpu.CompilerParams(vmem_limit_bytes=2 * z.limit),
         name="tables",
-    )(count, own, lon, cyc, data, weight)
+    )(base, count, own, lon, cyc, data, weight)
 
 
 def adjoint_into(z, func_ref, rows_ref, out_ref):
@@ -228,7 +275,7 @@
                 for k in range(2)
             ]
             for a in range(z.steps):
-                at = pl.multiple_of(slot * z.nb + 8 * a, 8)
+                at = z.func_row(slot, a)
                 f = [func_ref[h, pl.ds(at, 8), :] for h in range(z.halves)]
                 for k in range(2):
                     prod = f[0] * w[k][0]
@@ -287,7 +334,7 @@
                 else:
                     now = (rise[rows, t : t + 1] * x) * prev - fall[rows, t : t + 1] * before
                     now = jnp.where(starts[rows, t : t + 1] > 0.5, first[rows, lanes], now)
-                func_ref[h, pl.ds(tile * 8 * z.seg_len + t, left, stride=z.seg_len), :] = now[:left]
+                func_ref[h, pl.ds(tile * 8 * z.seg_skew + t, left, stride=z.seg_skew), :] = now[:left]
                 before, prev = prev, now
     adjoint_into(z, func_ref, ty_ref, out_ref)
 
@@ -299,10 +346,11 @@
         in_specs=[SMEM, VMEM, VMEM],
         out_specs=[VMEM] * 2,
         out_shape=[
-            jax.ShapeDtypeStruct((z.halves, z.cnt * z.nb, 128), F32),
+            jax.ShapeDtypeStruct((z.halves, z.func_rows, 128), F32),
             jax.ShapeDtypeStruct((z.tiles, 8, 128), F32),
         ],
         scratch_shapes=[pltpu.VMEM((padded, z.cyc), F32)] * 3,
+        compiler_params=pltpu.CompilerParams(vmem_limit_bytes=z.limit),
         name="functions",
     )(own, recv, ty)
 
@@ -325,10 +373,13 @@
 def step_kernel(z, later, own_ref, *refs):
     if later:
         gathered_ref, inv_ref, func_ref, energy_ref, res_ref, dir_ref = refs[:6]
-        out_ref, newres_ref, prec_ref, sol_ref, flat = refs[6:]
+        out_ref, newres_ref, prec_ref, sol_ref, flat, pay, inv_buf, sems, inv_sems = refs[6:]
     else:
-        gathered_ref, inv_ref, func_ref = refs[:3]
-        out_ref, newres_ref, prec_ref, flat = refs[3:]
+        gathered_ref, inv_ref, func_ref, sum_ref = refs[:4]
+        out_ref, newres_ref, prec_ref, flat, pay, inv_buf, sems, inv_sems = refs[4:]
+    fetches = [pltpu.make_async_copy(inv_ref.at[slot], inv_buf.at[slot], inv_sems.at[slot]) for slot in range(z.cnt)]
+    for fetch in fetches:
+        fetch.start()
     summed, curvature = total_of(z, gathered_ref)
     if later:
         step_size = energy_ref[0:1, 0:1] / curvature
@@ -344,9 +395,10 @@
     def apply(g, carry):
         for p in range(z.per):
             slot = g * z.per + p
+            pltpu.make_async_copy(inv_ref.at[slot], inv_buf.at[slot], inv_sems.at[slot]).wait()
             acc = [jnp.zeros((8, z.nb), F32)] * 2
             for a in range(z.steps):
-                block = inv_ref[slot, 8 * a : 8 * a + 8, :]
+                block = inv_buf[slot, 8 * a : 8 * a + 8, :]
                 for k in range(2):
                     col = newres_ref[k * z.groups + g][:, p * z.steps + a : p * z.steps + a + 1]
                     acc[k] = acc[k] + block * col
@@ -368,7 +420,7 @@
             slot = g * z.per + p
             acc = [[jnp.zeros((8, 128), F32)] * z.halves for k in range(2)]
             for a in range(z.steps):
-                f = [func_ref[h, slot * z.nb + 8 * a : slot * z.nb + 8 * a + 8, :] for h in range(z.halves)]
+                f = [func_ref[h, pl.ds(z.func_row(slot, a), 8), :] for h in range(z.halves)]
                 for k in range(2):
                     r = k * z.cnt + slot
                     col = jnp.broadcast_to(columns[8 * a : 8 * a + 8, r : r + 1], (8, 128))
@@ -378,38 +430,61 @@
             for k in range(2):
                 r = k * z.cnt + slot
                 for h in range(z.halves):
-                    out_ref[0, r : r + 1, h * 128 : (h + 1) * 128] = jnp.sum(acc[k][h], axis=0, keepdims=True)
+                    pay[r : r + 1, h * 128 : (h + 1) * 128] = jnp.sum(acc[k][h], axis=0, keepdims=True)
         for k in range(2):
             t = k * z.groups + g
             prec_ref[t] = tiles[k]
             energy = energy + tiles[k] * newres_ref[t]
-    rest = z.pay - 2 * z.cnt
-    out_ref[0, 2 * z.cnt :, :] = jnp.broadcast_to(full_sum(energy), (rest, z.cyc))
-    for d in range(1, z.nord):
-        out_ref[d] = out_ref[0]
-
-
-def make_step(z, own, gathered, inv, func, state=None):
-    later = state is not None
+    top = 2 * z.cnt + 1
+    pay[2 * z.cnt : top, :] = jnp.broadcast_to(full_sum(energy), (1, z.cyc))
+    if not later:
+        for h in range(z.halves):
+            pay[top : top + 2 * z.share, h * 128 : (h + 1) * 128] = sum_ref[h, 0 : 2 * z.share, :]
+    send_copies(z, pay, out_ref, sems)
+
+
+def make_step(z, own, gathered, inv, func, state, later):
     tile = jax.ShapeDtypeStruct((z.tiles, 8, 128), F32)
-    outs = [jax.ShapeDtypeStruct((z.nord, z.pay, z.cyc), F32), tile, tile] + [tile] * later
-    args = [own, gathered, inv, func] + (list(state) if later else [])
+    outs = [pltpu.MemorySpace.HBM((z.nord, z.pay if later else z.pay_first, z.cyc), F32), tile, tile] + [tile] * later
+    args = [own, gathered, inv, func] + list(state)
     return pl.pallas_call(
         functools.partial(step_kernel, z, later),
-        in_specs=[SMEM] + [VMEM] * (len(args) - 1),
-        out_specs=[VMEM] * len(outs),
+        in_specs=[SMEM, VMEM, HBM] + [VMEM] * (len(args) - 3),
+        out_specs=[HBM] + [VMEM] * (len(outs) - 1),
         out_shape=outs,
-        scratch_shapes=[pltpu.VMEM((up(z.nb, 128) // 128, up(2 * z.cnt, 8), 128), F32)],
+        scratch_shapes=[
+            pltpu.VMEM((up(z.nb, 128) // 128, up(2 * z.cnt, 8), 128), F32),
+            pltpu.VMEM(outs[0].shape[1:], F32),
+            pltpu.VMEM(inv.shape, F32),
+            pltpu.SemaphoreType.DMA((z.nord,)),
+            pltpu.SemaphoreType.DMA((z.cnt,)),
+        ],
+        compiler_params=pltpu.CompilerParams(vmem_limit_bytes=z.limit),
         name="step",
     )(*args)
 
 
-def image_kernel(z, later, own_ref, ids_ref, recv_ref, tc_ref, ts_ref, func_ref, *refs):
+def image_kernel(z, later, own_ref, ids_ref, recv_ref, func_ref, *refs):
     if later:
-        old_ref, old_energy_ref, prec_ref, old_dir_ref = refs[:4]
-        out_ref, energy_ref, dir_ref, val_ref, all_rows, rows = refs[4:]
+        tc_ref, ts_ref, old_ref, old_energy_ref, prec_ref, old_dir_ref = refs[:6]
+        out_ref, energy_ref, dir_ref, val_ref, all_rows, rows = refs[6:]
     else:
-        out_ref, energy_ref, val_ref, all_rows, rows = refs
+        out_ref, energy_ref, tc_ref, ts_ref, val_ref, all_rows, rows = refs
+        top = 2 * z.cnt + 1
+        for o in range(z.nord):
+            at = z.off + o * z.share
+            for h in range(z.halves):
+                lanes = slice(h * 128, (h + 1) * 128)
+                tc_ref[h, at : at + z.share, :] = recv_ref[o, top : top + z.share, lanes]
+                ts_ref[h, at : at + z.share, :] = recv_ref[o, top + z.share : top + 2 * z.share, lanes]
+
+        def mirror(q, carry):
+            for h in range(z.halves):
+                tc_ref[h, pl.ds(z.off - q, 1), :] = tc_ref[h, pl.ds(z.off + q, 1), :]
+                ts_ref[h, pl.ds(z.off - q, 1), :] = -ts_ref[h, pl.ds(z.off + q, 1), :]
+            return carry
+
+        lax.fori_loop(1, z.no, mirror, 0)
     energy = recv_ref[0, 2 * z.cnt : 2 * z.cnt + 1, 0:128]
     for o in range(1, z.nord):
         energy = energy + recv_ref[o, 2 * z.cnt : 2 * z.cnt + 1, 0:128]
@@ -459,12 +534,13 @@
     out_ref[0] = jnp.where(mark, full_sum(curvature), out_ref[0])
 
 
-def make_image(z, own, ids, recv, tc, ts, func, state=None):
-    later = state is not None
+def make_image(z, own, ids, recv, func, state=()):
+    later = len(state) > 0
     tile = jax.ShapeDtypeStruct((z.tiles, 8, 128), F32)
-    outs = [tile, jax.ShapeDtypeStruct((8, 128), F32)] + [tile] * later
+    table = jax.ShapeDtypeStruct((z.halves, z.table, 128), F32)
+    outs = [tile, jax.ShapeDtypeStruct((8, 128), F32)] + ([tile] if later else [table, table])
     outs.append(jax.ShapeDtypeStruct((2, z.halves, z.no, 128), F32))
-    args = [own, ids, recv, tc, ts, func] + (list(state) if later else [])
+    args = [own, ids, recv, func] + list(state)
     return pl.pallas_call(
         functools.partial(image_kernel, z, later),
         in_specs=[SMEM, SMEM] + [VMEM] * (len(args) - 2),
@@ -474,6 +550,7 @@
             pltpu.VMEM((2 * z.halves, z.no, 128), F32),
             pltpu.VMEM((z.halves, z.pay, 128), F32),
         ],
+        compiler_params=pltpu.CompilerParams(vmem_limit_bytes=z.limit),
         name="image",
     )(*args)
 
@@ -512,6 +589,7 @@
         in_specs=[VMEM] * 5,
         out_specs=[VMEM] * 2,
         out_shape=[out, out],
+        compiler_params=pltpu.CompilerParams(vmem_limit_bytes=z.limit),
         name="last",
     )(gathered, energy, res, sol, direction)
 
@@ -519,23 +597,26 @@
 def body(longitude, cycle_of, obs_count, observed, obs_weight, legendre, precond_inv, order_of_slot):
     z = Sizes(legendre, longitude.shape[1])
     dense = lambda value: value.reshape(z.rows, 128)
+    legendre = pltpu.with_memory_space_constraint(legendre, pltpu.MemorySpace.HBM)
+    inv = pltpu.with_memory_space_constraint(precond_inv, pltpu.MemorySpace.HBM)
     first = (lax.axis_index("ord") * z.cnt).astype(jnp.int32).reshape(1)
     seeds = make_seeds(z, first, order_of_slot, legendre)
     recv = lax.all_to_all(seeds, "ord", 0, 0)
-    tc, ts, ty = make_tables(
-        z, obs_count, order_of_slot, dense(longitude), dense(cycle_of), dense(observed), dense(obs_weight)
+    base = (lax.axis_index("ord") * z.share).astype(jnp.int32).reshape(1)
+    sums, ty = make_tables(
+        z, base, obs_count, order_of_slot, dense(longitude), dense(cycle_of), dense(observed), dense(obs_weight)
     )
     ids = recv[:, z.id_row, : z.cnt].reshape(z.no).astype(jnp.int32)
     func, part = make_functions(z, order_of_slot, recv, ty)
     gathered = lax.all_gather(part, "obs", axis=0)
-    values, res, direction = make_step(z, order_of_slot, gathered, precond_inv, func)
+    values, res, direction = make_step(z, order_of_slot, gathered, inv, func, (sums,), False)
     recv = lax.all_to_all(values, "ord", 0, 0)
-    part, energy, all_values = make_image(z, order_of_slot, ids, recv, tc, ts, func)
+    part, energy, tc, ts, all_values = make_image(z, order_of_slot, ids, recv, func)
     gathered = lax.all_gather(part, "obs", axis=0)
-    values, res, prec, sol = make_step(z, order_of_slot, gathered, precond_inv, func, (energy, res, direction))
+    values, res, prec, sol = make_step(z, order_of_slot, gathered, inv, func, (energy, res, direction), True)
     recv = lax.all_to_all(values, "ord", 0, 0)
     part, energy, direction, all_values = make_image(
-        z, order_of_slot, ids, recv, tc, ts, func, (all_values, energy, prec, direction)
+        z, order_of_slot, ids, recv, func, (tc, ts, all_values, energy, prec, direction)
     )
     gathered = lax.all_gather(part, "obs", axis=0)
     return tuple(make_last(z, gathered, energy, res, sol, direction))

time: 136 us -> 103 us (0.76)
  Pallas kernels: 78.8 us -> 43.7 us
  waiting for transfers between devices: 7.07 us -> 12.6 us
  blocking collectives: 32.1 us -> 28.1 us
    pallas_call x4, Pallas kernels: 53.3 us -> 24 us  [the longest x2 10.9 us: make_step(): pl.pallas_call(functools.partial(step_kernel, z, later), in_specs=[SMEM,...]
    all_to_all x1, waiting for transfers between devices: 7.07 us -> 12.2 us  [body(): recv = lax.all_to_all(values, 'ord', 0, 0)]
    all_gather x3, blocking collectives: 19.3 us -> 16 us  [body(): gathered = lax.all_gather(part, 'obs', axis=0)]
    pallas_call x2, Pallas kernels: 16.1 us -> 13.1 us  [make_image(): pl.pallas_call(functools.partial(image_kernel, z, later), in_specs=[SMEM,...]
    pallas_call x1, Pallas kernels: 5.41 us -> 3.57 us  [make_functions(): pl.pallas_call(functools.partial(functions_kernel, z), in_specs=[SMEM, VM...]
  transfers between devices with their start and end apart: 2 -> 2, of which waited for: 1 -> 2; matrix products, arithmetic and copies ran while one was open for 1% -> 1% of each run, Pallas kernels for 26% -> 10%
where the time goes in v2:
time: 103 us; the launch traced here: 102 us
  Pallas kernels  43.7 us (42%)
  blocking collectives  28.1 us (27%)
  starting transfers between devices  12.9 us (13%)
  waiting for transfers between devices  12.6 us (12%)
  local copies, waits for them, and re-layouts  2.76 us (3%)
  between operations  1.43 us (1%)
    all_gather x3, blocking collectives, body(): gathered = lax.all_gather(part, 'obs', axis=0)  16 us
    pallas_call x2, Pallas kernels, make_image(): pl.pallas_call(functools.partial(image_kernel, z, later), in_specs=[SMEM,...  13.1 us
    all_to_all x1, waiting for transfers between devices, body(): recv = lax.all_to_all(values, 'ord', 0, 0)  12.2 us
    all_to_all x1, blocking collectives, body(): recv = lax.all_to_all(values, 'ord', 0, 0)  12.1 us
    pallas_call x2, Pallas kernels, make_step(): pl.pallas_call(functools.partial(step_kernel, z, later), in_specs=[SMEM,...  10.9 us
    pallas_call x1, Pallas kernels, make_tables(): pl.pallas_call(functools.partial(tables_kernel, z), in_specs=[SMEM, SMEM,...  10.6 us
    all_to_all x1, starting transfers between devices, body(): recv = lax.all_to_all(seeds, 'ord', 0, 0)  7.32 us
    all_to_all x1, starting transfers between devices, body(): recv = lax.all_to_all(values, 'ord', 0, 0)  5.6 us
  transfers between devices with their start and end apart: 2, of which 2 were waited for; matrix products, arithmetic and copies ran while one was open for 1% of the time, Pallas kernels for 10%

profile of v2, /device:TPU:0, one launch (start us, length us, event | category | flops | bytes accessed | tf_op | source)
XLA Modules:
  0.0 102.1 jit_solution(5250781757904510589)
XLA Ops:
  0.6 0.0 copy-start.3
  0.6 0.0 copy-start.2
  0.7 0.0 copy-start.1
  0.7 0.0 copy-start
  0.7 0.0 copy-start.4
  0.7 0.7 copy-done.4
  1.4 0.0 copy-start.5
  1.4 2.6 %seeds.1 = f32[8,48,256]{2,1,0:T(8,128)} custom-call(s32[1]{0:T(128)} %bitcast.first_ref, s32[9]{0:T(128)S(1)} %copy-done.4, f32[1,9,288,256]{3,2,1,0:T(8,128)} %leg_ref.1), custom_call_target="tpu_custom_call" | custom-call | tf_op jit(solution)/shard_map/seeds/pallas_call | solution.py:112
  4.0 7.3 %all-to-all-start = ((f32[8,48,256]{2,1,0:T(8,128)}), f32[8,48,256]{2,1,0:T(8,128)S(1)}, u32[]{:S(2)}, u32[]{:S(2)}) async-start(f32[8,48,256]{2,1,0:T(8,128)} %seeds.1), calls=%async_computation | async-start | bytes 786432 | tf_op jit(solution)/shard_map/all_to_all | solution.py:604
  11.9 0.0 copy-done.3
  12.0 0.0 copy-done.2
  12.0 0.0 copy-done.1
  12.0 0.0 copy-done
  12.0 0.0 copy-done.5
  12.0 10.6 %tables.1 = (f32[2,40,128]{2,1,0:T(8,128)S(1)}, f32[2,24,128]{2,1,0:T(8,128)S(1)}) custom-call(s32[1]{0:T(128)} %bitcast.1.base_ref, s32[1]{0:T(128)S(6)} %copy.10.count_ref, s32[9]{0:T(128)S(1)} %copy-done.5, f32[256,128]{1,0:T(8,128)S(1)} %bitcast.12, s32[256,128]{1,0:T(8,128)S(1)} %bitcast.13, f32[256,128]{1,0:T(8,128)S(1)} %bitcast.14, ...), custom_call_target="tpu_custom_call" | custom-call | tf_op jit(solution)/shard_map/tables/pallas_call | solution.py:239
  22.6 0.4 all-to-all-done.recv_ref
  23.0 3.6 %functions.1 = (f32[2,2616,128]{2,1,0:T(8,128)S(1)}, f32[6,8,128]{2,1,0:T(8,128)S(1)}) custom-call(s32[9]{0:T(128)S(1)} %copy-done.5, f32[8,48,256]{2,1,0:T(8,128)S(1)} %all-to-all-done.recv_ref, f32[2,24,128]{2,1,0:T(8,128)S(1)} %get-tuple-element.21.ty_ref), custom_call_target="tpu_custom_call" | custom-call | tf_op jit(solution)/shard_map/functions/pallas_call | solution.py:344
  26.5 5.3 %all-gather = f32[24,8,128]{2,1,0:T(8,128)S(1)} all-gather(f32[6,8,128]{2,1,0:T(8,128)S(1)} %get-tuple-element.22), channel_id=2, replica_groups=mesh['obs'=4,'ord'=8] {'obs'}, dimensions={0}, use_global_device_ids=true | all-gather | bytes 122880 | tf_op jit(solution)/shard_map/all_gather | solution.py:611
  31.9 5.5 %step.2 = (f32[8,56,256]{2,1,0:T(8,128)}, f32[6,8,128]{2,1,0:T(8,128)S(1)}, f32[6,8,128]{2,1,0:T(8,128)S(1)}) custom-call(s32[9]{0:T(128)S(1)} %copy-done.5, f32[4,6,8,128]{3,2,1,0:T(8,128)S(1)} %bitcast.10, f32[9,288,288]{2,1,0:T(8,128)} %refs_1_.3, f32[2,2616,128]{2,1,0:T(8,128)S(1)} %get-tuple-element.23.refs_2_.func_ref, ...), custom_call_target="tpu_custom_call" | custom-call | tf_op jit(solution)/shard_map/step/pallas_call | solution.py:450
  37.4 0.0 copy-start.7
  37.4 0.6 copy-done.7
  38.0 5.6 %all-to-all-start.1 = ((f32[8,56,256]{2,1,0:T(8,128)}), f32[8,56,256]{2,1,0:T(8,128)S(1)}, u32[]{:S(2)}, u32[]{:S(2)}) async-start(f32[8,56,256]{2,1,0:T(8,128)} %get-tuple-element.25), calls=%async_computation.1 | async-start | bytes 917504 | tf_op jit(solution)/shard_map/all_to_all | solution.py:613
  43.6 0.6 fusion
  44.2 0.8 convert_element_type.6.ids_ref
  45.0 12.2 %all-to-all-done.1.recv_ref = f32[8,56,256]{2,1,0:T(8,128)S(1)} async-done(((f32[8,56,256]{2,1,0:T(8,128)}), f32[8,56,256]{2,1,0:T(8,128)S(1)}, u32[]{:S(2)}, u32[]{:S(2)}) %all-to-all-start.1) | async-done | bytes 458784 | tf_op jit(solution)/shard_map/all_to_all | solution.py:613
  57.2 0.0 copy-start.6
  57.2 0.7 copy-done.6
  57.8 0.0 copy-start.8
  57.8 6.9 %image.2 = (f32[6,8,128]{2,1,0:T(8,128)S(1)}, f32[8,128]{1,0:T(8,128)S(1)}, f32[2,216,128]{2,1,0:T(8,128)S(1)}, f32[2,216,128]{2,1,0:T(8,128)S(1)}, f32[2,2,72,128]{3,2,1,0:T(8,128)S(1)}) custom-call(s32[9]{0:T(128)S(1)} %copy-done.6, s32[72]{0:T(128)S(1)} %convert_element_type.6.ids_ref, f32[8,56,256]{2,1,0:T(8,128)S(1)} %all-to-all-done.1.recv_ref, ...), custom_call_target="tpu_custom_call" | custom-call | tf_op jit(solution)/shard_map/image/pallas_call | solution.py:544
  64.7 5.3 %all-gather.1 = f32[24,8,128]{2,1,0:T(8,128)S(1)} all-gather(f32[6,8,128]{2,1,0:T(8,128)S(1)} %get-tuple-element.26), channel_id=3, replica_groups=mesh['obs'=4,'ord'=8] {'obs'}, dimensions={0}, use_global_device_ids=true | all-gather | bytes 122880 | tf_op jit(solution)/shard_map/all_gather | solution.py:615
  70.0 0.0 copy-done.8
  70.0 5.4 %step.3 = (f32[8,24,256]{2,1,0:T(8,128)}, f32[6,8,128]{2,1,0:T(8,128)S(1)}, f32[6,8,128]{2,1,0:T(8,128)S(1)}, f32[6,8,128]{2,1,0:T(8,128)S(1)}) custom-call(s32[9]{0:T(128)S(1)} %copy-done.6, f32[4,6,8,128]{3,2,1,0:T(8,128)S(1)} %bitcast.11, f32[9,288,288]{2,1,0:T(8,128)} %refs_1_.3, f32[2,2616,128]{2,1,0:T(8,128)S(1)} %get-tuple-element.23.refs_2_.func_ref, ...), custom_call_target="tpu_custom_call" | custom-call | tf_op jit(solution)/shard_map/step/pallas_call | solution.py:450
  75.4 12.1 %all_to_all.15.recv_ref = f32[8,24,256]{2,1,0:T(8,128)S(1)} all-to-all(f32[8,24,256]{2,1,0:T(8,128)} %get-tuple-element.30), channel_id=1, replica_groups=mesh['obs'=4,'ord'=8] {'ord'}, dimensions={0} | all-to-all | bytes 393216 | tf_op jit(solution)/shard_map/all_to_all | solution.py:617
  87.5 6.2 %image.3 = (f32[6,8,128]{2,1,0:T(8,128)S(1)}, f32[8,128]{1,0:T(8,128)S(1)}, f32[6,8,128]{2,1,0:T(8,128)S(1)}, f32[2,2,72,128]{3,2,1,0:T(8,128)}) custom-call(s32[9]{0:T(128)S(1)} %copy-done.6, s32[72]{0:T(128)S(1)} %convert_element_type.6.ids_ref, f32[8,24,256]{2,1,0:T(8,128)S(1)} %all_to_all.15.recv_ref, ...), custom_call_target="tpu_custom_call" | custom-call | tf_op jit(solution)/shard_map/image/pallas_call | solution.py:544
  93.7 5.3 %all-gather.2 = f32[24,8,128]{2,1,0:T(8,128)S(1)} all-gather(f32[6,8,128]{2,1,0:T(8,128)S(1)} %get-tuple-element.35), channel_id=4, replica_groups=mesh['obs'=4,'ord'=8] {'obs'}, dimensions={0}, use_global_device_ids=true | all-gather | bytes 122880 | tf_op jit(solution)/shard_map/all_gather | solution.py:621
  99.0 3.1 %last.1 = (f32[9,2,288]{2,1,0:T(2,128)}, f32[9,2,288]{2,1,0:T(2,128)}) custom-call(f32[4,6,8,128]{3,2,1,0:T(8,128)S(1)} %bitcast.9, f32[8,128]{1,0:T(8,128)S(1)} %get-tuple-element.36.energy_ref, f32[6,8,128]{2,1,0:T(8,128)S(1)} %get-tuple-element.37.res_ref, f32[6,8,128]{2,1,0:T(8,128)S(1)} %get-tuple-element.38.sol_ref, ...), custom_call_target="tpu_custom_call" | custom-call | tf_op jit(solution)/shard_map/last/pallas_call | solution.py:587
Async XLA Ops:
  0.6 11.3 %copy-start.3 = (f32[1,32768]{1,0:T(1,128)S(1)}, f32[1,32768]{1,0:T(1,128)}, u32[]{:S(2)}) copy-start(f32[1,32768]{1,0:T(1,128)} %param.12) | copy-start | bytes 393220
  0.6 11.3 %copy-start.2 = (f32[1,32768]{1,0:T(1,128)S(1)}, f32[1,32768]{1,0:T(1,128)}, u32[]{:S(2)}) copy-start(f32[1,32768]{1,0:T(1,128)} %param.11) | copy-start | bytes 393220
  0.7 11.3 %copy-start.1 = (s32[1,32768]{1,0:T(1,128)S(1)}, s32[1,32768]{1,0:T(1,128)}, u32[]{:S(2)}) copy-start(s32[1,32768]{1,0:T(1,128)} %param.9) | copy-start | bytes 393220
  0.7 11.3 %copy-start = (f32[1,32768]{1,0:T(1,128)S(1)}, f32[1,32768]{1,0:T(1,128)}, u32[]{:S(2)}) copy-start(f32[1,32768]{1,0:T(1,128)} %param.8) | copy-start | bytes 393220
  0.7 0.7 copy-start.4
  1.4 10.6 %copy-start.5 = (s32[9]{0:T(128)S(1)}, s32[9]{0:T(128)}, u32[]{:S(2)}) copy-start(s32[9]{0:T(128)} %own_ref.13) | copy-start | bytes 112
  4.0 19.0 %all-to-all-start = ((f32[8,48,256]{2,1,0:T(8,128)}), f32[8,48,256]{2,1,0:T(8,128)S(1)}, u32[]{:S(2)}, u32[]{:S(2)}) async-start(f32[8,48,256]{2,1,0:T(8,128)} %seeds.1), calls=%async_computation | async-start | bytes 786432 | tf_op jit(solution)/shard_map/all_to_all | solution.py:604
  37.4 0.6 copy-start.7
  38.0 19.2 %all-to-all-start.1 = ((f32[8,56,256]{2,1,0:T(8,128)}), f32[8,56,256]{2,1,0:T(8,128)S(1)}, u32[]{:S(2)}, u32[]{:S(2)}) async-start(f32[8,56,256]{2,1,0:T(8,128)} %get-tuple-element.25), calls=%async_computation.1 | async-start | bytes 917504 | tf_op jit(solution)/shard_map/all_to_all | solution.py:613
  57.2 0.7 copy-start.6
  57.8 12.2 %copy-start.8 = (f32[6,8,128]{2,1,0:T(8,128)S(1)}, f32[6,8,128]{2,1,0:T(8,128)}, u32[]{:S(2)}) copy-start(f32[6,8,128]{2,1,0:T(8,128)} %copy-done.7) | copy-start | bytes 73732

commit v3 on v2

--- a/solution.py
+++ b/solution.py
@@ -12,6 +12,7 @@
 VMEM_LIMIT = 24 << 20
 WINDOW = 32
 UNROLL = 4
+ORDERS_AT_ONCE = 2
 CHUNK = 1024
 F32 = jnp.float32
 BF16 = jnp.bfloat16
@@ -39,16 +40,12 @@
         self.rows = slab // 128
         self.halves = self.cyc // 128
         self.steps = self.nb // 8
-        per = 128 // self.steps
-        while self.cnt % per or per * self.steps == 128:
-            per -= 1
-        self.per = per
-        self.groups = self.cnt // per
-        self.tiles = 2 * self.groups
+        self.state = (up(2 * self.cnt + 1, 8), up(self.nb, 128))
         self.seg = SEGMENTS
         self.seg_len = self.nb // SEGMENTS
-        self.seed_rows = 2 * self.seg + 1
-        self.id_row = self.cnt * self.seed_rows
+        self.seed_rows = 2 * self.seg - 1
+        self.cos_row = self.cnt * self.seed_rows
+        self.id_row = self.cos_row + 1
         self.seeds = up(self.id_row + 1, 8)
         self.pay = up(2 * self.cnt + 1, 8)
         self.off = up(self.no, 8)
@@ -82,12 +79,16 @@
 
 def seeds_kernel(z, first_ref, own_ref, leg_ref, out_ref, stage, keep, sems, out_sems):
     copies = []
+
+    def fetch(i, at):
+        n = len(copies)
+        copies.append(pltpu.make_async_copy(leg_ref.at[0, i, pl.ds(at, 8), :], stage.at[n], sems.at[n]))
+
     for i in range(z.cnt):
-        aligned = pl.multiple_of((first_ref[0] + i) // 8 * 8, 8)
-        for s in range(z.seg + 1):
-            at = aligned if s == z.seg else s * z.seg_len
-            n = i * (z.seg + 1) + s
-            copies.append(pltpu.make_async_copy(leg_ref.at[0, i, pl.ds(at, 8), :], stage.at[n], sems.at[n]))
+        for s in range(1, z.seg):
+            fetch(i, s * z.seg_len)
+        fetch(i, pl.multiple_of((first_ref[0] + i) // 8 * 8, 8))
+    fetch(0, 0)
     for copy in copies:
         copy.start()
     lane = iota((z.seeds - z.id_row, z.cyc), 1)
@@ -99,25 +100,28 @@
         copy.wait()
     for i in range(z.cnt):
         base = i * z.seed_rows
-        for s in range(z.seg):
-            keep[base + 2 * s : base + 2 * s + 2, :] = stage[i * (z.seg + 1) + s, 0:2, :]
+        for s in range(z.seg - 1):
+            keep[base + 2 * s : base + 2 * s + 2, :] = stage[i * z.seg + s, 0:2, :]
         order = first_ref[0] + i
-        block = stage[i * (z.seg + 1) + z.seg]
+        block = stage[i * z.seg + z.seg - 1]
         mine = iota((8, z.cyc), 0) == order - order // 8 * 8
-        keep[base + 2 * z.seg : base + 2 * z.seg + 1, :] = jnp.sum(jnp.where(mine, block, 0.0), axis=0, keepdims=True)
+        top = base + z.seed_rows - 1
+        keep[top : top + 1, :] = jnp.sum(jnp.where(mine, block, 0.0), axis=0, keepdims=True)
+    keep[z.cos_row : z.cos_row + 1, :] = stage[z.cnt * z.seg, 1:2, :]
     send_copies(z, keep, out_ref, out_sems)
 
 
 def make_seeds(z, first, own, legendre):
+    slabs = z.cnt * z.seg + 1
     return pl.pallas_call(
         functools.partial(seeds_kernel, z),
         in_specs=[SMEM, SMEM, HBM],
         out_specs=HBM,
         out_shape=pltpu.MemorySpace.HBM((z.nord, z.seeds, z.cyc), F32),
         scratch_shapes=[
-            pltpu.VMEM((z.cnt * (z.seg + 1), 8, z.cyc), F32),
+            pltpu.VMEM((slabs, 8, z.cyc), F32),
             pltpu.VMEM((z.seeds, z.cyc), F32),
-            pltpu.SemaphoreType.DMA((z.cnt * (z.seg + 1),)),
+            pltpu.SemaphoreType.DMA((slabs,)),
             pltpu.SemaphoreType.DMA((z.nord,)),
         ],
         compiler_params=pltpu.CompilerParams(vmem_limit_bytes=z.limit),
@@ -260,36 +264,33 @@
     )(base, count, own, lon, cyc, data, weight)
 
 
-def adjoint_into(z, func_ref, rows_ref, out_ref):
-    lane = iota((8, 128), 1)
-
-    def group(g, carry):
-        tiles = [jnp.zeros((8, 128), F32)] * 2
-        for p in range(z.per):
-            slot = g * z.per + p
-            w = [
-                [
-                    jnp.broadcast_to(rows_ref[h, pl.ds(k * z.cnt + slot, 1), :], (8, 128))
-                    for h in range(z.halves)
-                ]
-                for k in range(2)
+def flip(z, cols_ref, out_ref):
+    for c in range(z.state[1] // 128):
+        out_ref[:, c * 128 : (c + 1) * 128] = cols_ref[c * 128 : (c + 1) * 128, :].T[0 : z.state[0]]
+
+
+def adjoint_into(z, func_ref, rows_ref, cols_ref, out_ref):
+    cols_ref[...] = jnp.zeros_like(cols_ref)
+    for slot in range(z.cnt):
+        w = [
+            [
+                jnp.broadcast_to(rows_ref[h, k * z.cnt + slot : k * z.cnt + slot + 1, :], (8, 128))
+                for h in range(z.halves)
             ]
-            for a in range(z.steps):
-                at = z.func_row(slot, a)
-                f = [func_ref[h, pl.ds(at, 8), :] for h in range(z.halves)]
-                for k in range(2):
-                    prod = f[0] * w[k][0]
-                    for h in range(1, z.halves):
-                        prod = prod + f[h] * w[k][h]
-                    tiles[k] = jnp.where(lane == p * z.steps + a, jnp.sum(prod, axis=1, keepdims=True), tiles[k])
-        for k in range(2):
-            out_ref[k * z.groups + g] = tiles[k]
-        return carry
-
-    lax.fori_loop(0, z.groups, group, 0)
-
-
-def functions_kernel(z, own_ref, recv_ref, ty_ref, func_ref, out_ref, seed0, seed1, first):
+            for k in range(2)
+        ]
+        for a in range(z.steps):
+            f = [func_ref[h, pl.ds(z.func_row(slot, a), 8), :] for h in range(z.halves)]
+            for k in range(2):
+                prod = f[0] * w[k][0]
+                for h in range(1, z.halves):
+                    prod = prod + f[h] * w[k][h]
+                r = k * z.cnt + slot
+                cols_ref[8 * a : 8 * a + 8, r : r + 1] = jnp.sum(prod, axis=1, keepdims=True)
+    flip(z, cols_ref, out_ref)
+
+
+def functions_kernel(z, own_ref, recv_ref, ty_ref, func_ref, out_ref, seed0, seed1, first, cols):
     total = z.seg * z.cnt
     padded = up(total, 8)
     for slot in range(z.cnt):
@@ -298,19 +299,25 @@
         base = (order - block * z.cnt) * z.seed_rows
         for s in range(z.seg):
             r = slot * z.seg + s
-            seed0[r : r + 1, :] = recv_ref[block, pl.ds(base + 2 * s, 1), :]
-            seed1[r : r + 1, :] = recv_ref[block, pl.ds(base + 2 * s + 1, 1), :]
-            first[r : r + 1, :] = recv_ref[block, pl.ds(base + 2 * z.seg, 1), :]
-    cosine = recv_ref[0, 1:2, :] / (recv_ref[0, 0:1, :] * 1.7320508075688772)
+            if s > 0:
+                seed0[r : r + 1, :] = recv_ref[block, pl.ds(base + 2 * s - 2, 1), :]
+                seed1[r : r + 1, :] = recv_ref[block, pl.ds(base + 2 * s - 1, 1), :]
+            else:
+                seed0[r : r + 1, :] = jnp.zeros((1, z.cyc), F32)
+                seed1[r : r + 1, :] = jnp.zeros((1, z.cyc), F32)
+            first[r : r + 1, :] = recv_ref[block, pl.ds(base + z.seed_rows - 1, 1), :]
+    ground = recv_ref[0, z.seed_rows - 1 : z.seed_rows, :]
+    cosine = recv_ref[0, z.cos_row : z.cos_row + 1, :] / (ground * 1.7320508075688772)
     lanes_len = up(z.seg_len, 128)
     row = iota((padded, lanes_len), 0)
     order_of = jnp.zeros(row.shape, F32)
-    degree = jnp.zeros(row.shape, F32) + iota(row.shape, 1).astype(F32)
+    start_of = jnp.zeros(row.shape, F32)
     for slot in range(z.cnt):
         for s in range(z.seg):
             hit = row == slot * z.seg + s
             order_of = jnp.where(hit, own_ref[slot].astype(F32), order_of)
-            degree = jnp.where(hit, degree + float(s * z.seg_len), degree)
+            start_of = jnp.where(hit, float(s * z.seg_len), start_of)
+    degree = start_of + iota(row.shape, 1).astype(F32)
     minus = jnp.maximum(degree - order_of, 1.0)
     plus = jnp.maximum(degree + order_of, 1.0)
     rise = jnp.sqrt(jnp.maximum((2.0 * degree - 1.0) * (2.0 * degree + 1.0), 0.0) / (minus * plus))
@@ -318,25 +325,30 @@
     top = jnp.maximum((2.0 * degree + 1.0) * (degree + order_of - 1.0) * (degree - order_of - 1.0), 0.0)
     fall = jnp.sqrt(top / (minus * plus * jnp.maximum(2.0 * degree - 3.0, 1.0)))
     fall = jnp.where(degree > order_of + 1.0, fall, 0.0)
-    starts = (degree == order_of).astype(F32)
-    for h in range(z.halves):
-        lanes = slice(h * 128, (h + 1) * 128)
-        x = jnp.broadcast_to(cosine[:, lanes], (8, 128))
-        for tile in range(padded // 8):
-            rows = slice(tile * 8, tile * 8 + 8)
-            left = min(8, total - tile * 8)
-            before, prev = None, None
-            for t in range(z.seg_len):
+    for tile in range(padded // 8):
+        rows = slice(tile * 8, tile * 8 + 8)
+        left = min(8, total - tile * 8)
+        entry = order_of[rows, 0:128] - start_of[rows, 0:128]
+        lowest = start_of[rows, 0:128] == 0.0
+        now, prev, before = [None] * z.halves, [None] * z.halves, [None] * z.halves
+        for t in range(z.seg_len):
+            if t > 0:
+                up_by = jnp.broadcast_to(rise[rows, t : t + 1], (8, 128))
+                down_by = jnp.broadcast_to(fall[rows, t : t + 1], (8, 128))
+            here = entry == float(t)
+            for h in range(z.halves):
+                lanes = slice(h * 128, (h + 1) * 128)
+                x = jnp.broadcast_to(cosine[:, lanes], (8, 128))
                 if t == 0:
-                    now = seed0[rows, lanes]
+                    value = seed0[rows, lanes]
                 elif t == 1:
-                    now = seed1[rows, lanes]
+                    value = jnp.where(lowest, (up_by * x) * prev[h], seed1[rows, lanes])
                 else:
-                    now = (rise[rows, t : t + 1] * x) * prev - fall[rows, t : t + 1] * before
-                    now = jnp.where(starts[rows, t : t + 1] > 0.5, first[rows, lanes], now)
-                func_ref[h, pl.ds(tile * 8 * z.seg_skew + t, left, stride=z.seg_skew), :] = now[:left]
-                before, prev = prev, now
-    adjoint_into(z, func_ref, ty_ref, out_ref)
+                    value = (up_by * x) * prev[h] - down_by * before[h]
+                now[h] = jnp.where(here, first[rows, lanes], value)
+                func_ref[h, pl.ds(tile * 8 * z.seg_skew + t, left, stride=z.seg_skew), :] = now[h][:left]
+            before, prev, now = prev, now, [None] * z.halves
+    adjoint_into(z, func_ref, ty_ref, cols, out_ref)
 
 
 def make_functions(z, own, recv, ty):
@@ -347,23 +359,19 @@
         out_specs=[VMEM] * 2,
         out_shape=[
             jax.ShapeDtypeStruct((z.halves, z.func_rows, 128), F32),
-            jax.ShapeDtypeStruct((z.tiles, 8, 128), F32),
+            jax.ShapeDtypeStruct(z.state, F32),
         ],
-        scratch_shapes=[pltpu.VMEM((padded, z.cyc), F32)] * 3,
+        scratch_shapes=[pltpu.VMEM((padded, z.cyc), F32)] * 3 + [pltpu.VMEM((z.state[1], 128), F32)],
         compiler_params=pltpu.CompilerParams(vmem_limit_bytes=z.limit),
         name="functions",
     )(own, recv, ty)
 
 
 def total_of(z, gathered_ref):
-    summed = [gathered_ref[0, t] for t in range(z.tiles)]
+    summed = gathered_ref[0]
     for b in range(1, z.nobs):
-        summed = [summed[t] + gathered_ref[b, t] for t in range(z.tiles)]
-    lane = iota((8, 128), 1)
-    curvature = jnp.max(jnp.where((lane == 127) & (iota((8, 128), 0) == 0), summed[0], -jnp.inf), axis=1, keepdims=True)
-    curvature = jnp.max(curvature, axis=0, keepdims=True)
-    used = lane < z.per * z.steps
-    return [jnp.where(used, s, 0.0) for s in summed], curvature
+        summed = summed + gathered_ref[b]
+    return summed, summed[2 * z.cnt : 2 * z.cnt + 1, 0:1]
 
 
 def full_sum(value):
@@ -373,70 +381,46 @@
 def step_kernel(z, later, own_ref, *refs):
     if later:
         gathered_ref, inv_ref, func_ref, energy_ref, res_ref, dir_ref = refs[:6]
-        out_ref, newres_ref, prec_ref, sol_ref, flat, pay, inv_buf, sems, inv_sems = refs[6:]
+        out_ref, newres_ref, prec_ref, sol_ref, cols, pay, inv_buf, sems, inv_sems = refs[6:]
     else:
         gathered_ref, inv_ref, func_ref, sum_ref = refs[:4]
-        out_ref, newres_ref, prec_ref, flat, pay, inv_buf, sems, inv_sems = refs[4:]
+        out_ref, newres_ref, prec_ref, cols, pay, inv_buf, sems, inv_sems = refs[4:]
     fetches = [pltpu.make_async_copy(inv_ref.at[slot], inv_buf.at[slot], inv_sems.at[slot]) for slot in range(z.cnt)]
     for fetch in fetches:
         fetch.start()
     summed, curvature = total_of(z, gathered_ref)
     if later:
         step_size = energy_ref[0:1, 0:1] / curvature
-        for t in range(z.tiles):
-            sol_ref[t] = step_size * dir_ref[t]
-            newres_ref[t] = res_ref[t] - step_size * summed[t]
+        sol_ref[...] = step_size * dir_ref[...]
+        newres_ref[...] = res_ref[...] - step_size * summed
     else:
-        for t in range(z.tiles):
-            newres_ref[t] = summed[t]
-    lane = iota((8, 128), 1)
-    wide = up(z.nb, 128)
-
-    def apply(g, carry):
-        for p in range(z.per):
-            slot = g * z.per + p
-            pltpu.make_async_copy(inv_ref.at[slot], inv_buf.at[slot], inv_sems.at[slot]).wait()
-            acc = [jnp.zeros((8, z.nb), F32)] * 2
-            for a in range(z.steps):
-                block = inv_buf[slot, 8 * a : 8 * a + 8, :]
-                for k in range(2):
-                    col = newres_ref[k * z.groups + g][:, p * z.steps + a : p * z.steps + a + 1]
-                    acc[k] = acc[k] + block * col
-            live = iota((1, z.nb), 1) >= own_ref[slot]
-            for k in range(2):
-                value = jnp.where(live, jnp.sum(acc[k], axis=0, keepdims=True), 0.0)
-                for c in range(wide // 128):
-                    size = min(128, z.nb - c * 128)
-                    flat[c, pl.ds(k * z.cnt + slot, 1), 0:size] = value[:, c * 128 : c * 128 + size]
-        return carry
-
-    flat[...] = jnp.zeros_like(flat)
-    lax.fori_loop(0, z.groups, apply, 0)
-    columns = jnp.concatenate([flat[c].T for c in range(wide // 128)], 0)
-    energy = jnp.zeros((8, 128), F32)
-    for g in range(z.groups):
-        tiles = [jnp.zeros((8, 128), F32)] * 2
-        for p in range(z.per):
-            slot = g * z.per + p
-            acc = [[jnp.zeros((8, 128), F32)] * z.halves for k in range(2)]
-            for a in range(z.steps):
-                f = [func_ref[h, pl.ds(z.func_row(slot, a), 8), :] for h in range(z.halves)]
-                for k in range(2):
-                    r = k * z.cnt + slot
-                    col = jnp.broadcast_to(columns[8 * a : 8 * a + 8, r : r + 1], (8, 128))
-                    tiles[k] = jnp.where(lane == p * z.steps + a, col, tiles[k])
-                    for h in range(z.halves):
-                        acc[k][h] = acc[k][h] + f[h] * col
+        newres_ref[...] = summed
+    cols[...] = jnp.zeros_like(cols)
+    height = iota((8, 128), 0)
+    for slot in range(z.cnt):
+        fetches[slot].wait()
+        vec = [
+            jnp.broadcast_to(newres_ref[k * z.cnt + slot : k * z.cnt + slot + 1, 0 : z.nb], (8, z.nb)) for k in range(2)
+        ]
+        acc = [[jnp.zeros((8, 128), F32)] * z.halves for k in range(2)]
+        for a in range(z.steps):
+            block = inv_buf[slot, 8 * a : 8 * a + 8, :]
+            live = height >= own_ref[slot] - 8 * a
+            f = [func_ref[h, pl.ds(z.func_row(slot, a), 8), :] for h in range(z.halves)]
             for k in range(2):
                 r = k * z.cnt + slot
+                col = jnp.broadcast_to(jnp.sum(block * vec[k], axis=1, keepdims=True), (8, 128))
+                col = jnp.where(live, col, 0.0)
+                cols[8 * a : 8 * a + 8, r : r + 1] = col[:, r : r + 1]
                 for h in range(z.halves):
-                    pay[r : r + 1, h * 128 : (h + 1) * 128] = jnp.sum(acc[k][h], axis=0, keepdims=True)
+                    acc[k][h] = acc[k][h] + f[h] * col
         for k in range(2):
-            t = k * z.groups + g
-            prec_ref[t] = tiles[k]
-            energy = energy + tiles[k] * newres_ref[t]
+            r = k * z.cnt + slot
+            for h in range(z.halves):
+                pay[r : r + 1, h * 128 : (h + 1) * 128] = jnp.sum(acc[k][h], axis=0, keepdims=True)
+    flip(z, cols, prec_ref)
     top = 2 * z.cnt + 1
-    pay[2 * z.cnt : top, :] = jnp.broadcast_to(full_sum(energy), (1, z.cyc))
+    pay[2 * z.cnt : top, :] = jnp.broadcast_to(full_sum(newres_ref[...] * prec_ref[...]), (1, z.cyc))
     if not later:
         for h in range(z.halves):
             pay[top : top + 2 * z.share, h * 128 : (h + 1) * 128] = sum_ref[h, 0 : 2 * z.share, :]
@@ -444,8 +428,8 @@
 
 
 def make_step(z, own, gathered, inv, func, state, later):
-    tile = jax.ShapeDtypeStruct((z.tiles, 8, 128), F32)
-    outs = [pltpu.MemorySpace.HBM((z.nord, z.pay if later else z.pay_first, z.cyc), F32), tile, tile] + [tile] * later
+    vector = jax.ShapeDtypeStruct(z.state, F32)
+    outs = [pltpu.MemorySpace.HBM((z.nord, z.pay if later else z.pay_first, z.cyc), F32)] + [vector] * (2 + later)
     args = [own, gathered, inv, func] + list(state)
     return pl.pallas_call(
         functools.partial(step_kernel, z, later),
@@ -453,7 +437,7 @@
         out_specs=[HBM] + [VMEM] * (len(outs) - 1),
         out_shape=outs,
         scratch_shapes=[
-            pltpu.VMEM((up(z.nb, 128) // 128, up(2 * z.cnt, 8), 128), F32),
+            pltpu.VMEM((z.state[1], 128), F32),
             pltpu.VMEM(outs[0].shape[1:], F32),
             pltpu.VMEM(inv.shape, F32),
             pltpu.SemaphoreType.DMA((z.nord,)),
@@ -467,9 +451,9 @@
 def image_kernel(z, later, own_ref, ids_ref, recv_ref, func_ref, *refs):
     if later:
         tc_ref, ts_ref, old_ref, old_energy_ref, prec_ref, old_dir_ref = refs[:6]
-        out_ref, energy_ref, dir_ref, val_ref, all_rows, rows = refs[6:]
+        out_ref, energy_ref, dir_ref, val_ref, all_rows, rows, cols = refs[6:]
     else:
-        out_ref, energy_ref, tc_ref, ts_ref, val_ref, all_rows, rows = refs
+        out_ref, energy_ref, tc_ref, ts_ref, val_ref, all_rows, rows, cols = refs
         top = 2 * z.cnt + 1
         for o in range(z.nord):
             at = z.off + o * z.share
@@ -494,8 +478,9 @@
         for i in range(z.cnt):
             order = ids_ref[o * z.cnt + i]
             for k in range(2):
+                r = k * z.cnt + i
                 for h in range(z.halves):
-                    val_ref[k, h, pl.ds(order, 1), :] = recv_ref[o, k * z.cnt + i : k * z.cnt + i + 1, h * 128 : (h + 1) * 128]
+                    val_ref[k, h, pl.ds(order, 1), :] = recv_ref[o, r : r + 1, h * 128 : (h + 1) * 128]
         return carry
 
     lax.fori_loop(0, z.nord, place, 0)
@@ -504,41 +489,46 @@
         for k in range(2):
             for h in range(z.halves):
                 val_ref[k, h] = val_ref[k, h] + ratio * old_ref[k, h]
-        for t in range(z.tiles):
-            dir_ref[t] = prec_ref[t] + ratio * old_dir_ref[t]
-
-    def one_order(m, total):
+        dir_ref[...] = prec_ref[...] + ratio[:, 0:1] * old_dir_ref[...]
+
+    def some_orders(step, carry):
         for h in range(z.halves):
-            vc, vs = val_ref[0, h], val_ref[1, h]
-            near, far = tc_ref[h, pl.ds(z.off - m, z.no), :], tc_ref[h, pl.ds(z.off + m, z.no), :]
-            snear, sfar = ts_ref[h, pl.ds(z.off - m, z.no), :], ts_ref[h, pl.ds(z.off + m, z.no), :]
-            wc = 0.5 * jnp.sum((near + far) * vc + (sfar + snear) * vs, axis=0, keepdims=True)
-            ws = 0.5 * jnp.sum((sfar - snear) * vc + (near - far) * vs, axis=0, keepdims=True)
-            all_rows[h, pl.ds(m, 1), :] = wc
-            all_rows[z.halves + h, pl.ds(m, 1), :] = ws
-        return total
-
-    lax.fori_loop(0, z.no, one_order, 0)
+            sums = [[None] * 2 for _ in range(ORDERS_AT_ONCE)]
+            for tile in range(z.no // 8):
+                vc, vs = val_ref[0, h, tile * 8 : tile * 8 + 8, :], val_ref[1, h, tile * 8 : tile * 8 + 8, :]
+                for u in range(ORDERS_AT_ONCE):
+                    m = step * ORDERS_AT_ONCE + u
+                    low, high = pl.ds(z.off + tile * 8 - m, 8), pl.ds(z.off + tile * 8 + m, 8)
+                    near, far = tc_ref[h, low, :], tc_ref[h, high, :]
+                    snear, sfar = ts_ref[h, low, :], ts_ref[h, high, :]
+                    wc = (near + far) * vc + (sfar + snear) * vs
+                    ws = (sfar - snear) * vc + (near - far) * vs
+                    sums[u] = [wc, ws] if tile == 0 else [sums[u][0] + wc, sums[u][1] + ws]
+            for u in range(ORDERS_AT_ONCE):
+                m = step * ORDERS_AT_ONCE + u
+                for k in range(2):
+                    all_rows[k * z.halves + h, pl.ds(m, 1), :] = 0.5 * jnp.sum(sums[u][k], axis=0, keepdims=True)
+        return carry
+
+    lax.fori_loop(0, z.no // ORDERS_AT_ONCE, some_orders, 0)
     curvature = jnp.zeros((z.no, 128), F32)
     for k in range(2):
         for h in range(z.halves):
             curvature = curvature + all_rows[k * z.halves + h] * val_ref[k, h]
     for i in range(z.cnt):
         for k in range(2):
+            r = k * z.cnt + i
             for h in range(z.halves):
-                rows[h, k * z.cnt + i : k * z.cnt + i + 1, :] = all_rows[
-                    k * z.halves + h, pl.ds(own_ref[i], 1), :
-                ]
-    adjoint_into(z, func_ref, rows, out_ref)
-    mark = (iota((8, 128), 1) == 127) & (iota((8, 128), 0) == 0)
-    out_ref[0] = jnp.where(mark, full_sum(curvature), out_ref[0])
+                rows[h, r : r + 1, :] = all_rows[k * z.halves + h, pl.ds(own_ref[i], 1), :]
+    adjoint_into(z, func_ref, rows, cols, out_ref)
+    out_ref[2 * z.cnt : 2 * z.cnt + 1, :] = jnp.broadcast_to(full_sum(curvature), (1, z.state[1]))
 
 
 def make_image(z, own, ids, recv, func, state=()):
     later = len(state) > 0
-    tile = jax.ShapeDtypeStruct((z.tiles, 8, 128), F32)
+    vector = jax.ShapeDtypeStruct(z.state, F32)
     table = jax.ShapeDtypeStruct((z.halves, z.table, 128), F32)
-    outs = [tile, jax.ShapeDtypeStruct((8, 128), F32)] + ([tile] if later else [table, table])
+    outs = [vector, jax.ShapeDtypeStruct((8, 128), F32)] + ([vector] if later else [table, table])
     outs.append(jax.ShapeDtypeStruct((2, z.halves, z.no, 128), F32))
     args = [own, ids, recv, func] + list(state)
     return pl.pallas_call(
@@ -549,6 +539,7 @@
         scratch_shapes=[
             pltpu.VMEM((2 * z.halves, z.no, 128), F32),
             pltpu.VMEM((z.halves, z.pay, 128), F32),
+            pltpu.VMEM((z.state[1], 128), F32),
         ],
         compiler_params=pltpu.CompilerParams(vmem_limit_bytes=z.limit),
         name="image",
@@ -558,28 +549,13 @@
 def last_kernel(z, gathered_ref, energy_ref, res_ref, sol_ref, dir_ref, out_sol, out_res):
     summed, curvature = total_of(z, gathered_ref)
     step_size = energy_ref[0:1, 0:1] / curvature
-    lane = iota((8, 128), 1)
-    finals = (
-        [sol_ref[t] + step_size * dir_ref[t] for t in range(z.tiles)],
-        [res_ref[t] - step_size * summed[t] for t in range(z.tiles)],
-    )
-    wide = up(z.nb, 128)
-    for tiles, out in zip(finals, (out_sol, out_res)):
-        columns = []
-        for a in range(z.steps):
-            tile = jnp.zeros((8, 128), F32)
-            for slot in range(z.cnt):
-                g, p = divmod(slot, z.per)
-                for k in range(2):
-                    col = tiles[k * z.groups + g][:, p * z.steps + a : p * z.steps + a + 1]
-                    tile = jnp.where(lane == 2 * slot + k, col, tile)
-            columns.append(tile)
-        columns += [jnp.zeros((8, 128), F32)] * ((wide - z.nb) // 8)
-        for c in range(wide // 128):
-            flat = jnp.concatenate(columns[16 * c : 16 * c + 16], 0).T
-            size = min(128, z.nb - c * 128)
-            for slot in range(z.cnt):
-                out[slot, :, c * 128 : c * 128 + size] = flat[2 * slot : 2 * slot + 2, 0:size]
+    sol = sol_ref[...] + step_size * dir_ref[...]
+    res = res_ref[...] - step_size * summed
+    for slot in range(z.cnt):
+        for k in range(2):
+            r = k * z.cnt + slot
+            out_sol[slot, k : k + 1, :] = sol[r : r + 1, 0 : z.nb]
+            out_res[slot, k : k + 1, :] = res[r : r + 1, 0 : z.nb]
 
 
 def make_last(z, gathered, energy, res, sol, direction):

time: 103 us -> 94.3 us (0.916)
  Pallas kernels: 43.7 us -> 36.2 us
  local copies, waits for them, and re-layouts: 2.76 us -> 0.81 us
    pallas_call x2, Pallas kernels: 10.9 us -> 8.19 us  [make_step(): pl.pallas_call(functools.partial(step_kernel, z, later), in_specs=[SMEM,...]
    pallas_call x1, Pallas kernels: 3.07 us -> 0.69 us  [make_last(): pl.pallas_call(functools.partial(last_kernel, z), in_specs=[VMEM] * 5, ou...]
    pallas_call x2, Pallas kernels: 13.1 us -> 11.4 us  [make_image(): pl.pallas_call(functools.partial(image_kernel, z, later), in_specs=[SMEM,...]
    all_to_all x1, waiting for transfers between devices: 12.2 us -> 13.5 us  [body(): recv = lax.all_to_all(values, 'ord', 0, 0)]
    unnamed x18 -> x12, local copies, waits for them, and re-layouts: 2 us -> 0.73 us
  transfers between devices with their start and end apart: 2 -> 2, of which waited for: 2 -> 1; matrix products, arithmetic and copies ran while one was open for 1% -> 0% of each run, Pallas kernels for 10% -> 11%
where the time goes in v3:
time: 94.3 us; the launch traced here: 93.8 us
  Pallas kernels  36.2 us (38%)
  blocking collectives  28.5 us (30%)
  waiting for transfers between devices  13.5 us (14%)
  starting transfers between devices  13.3 us (14%)
  between operations  1.42 us (2%)
    all_gather x3, blocking collectives, body(): gathered = lax.all_gather(part, 'obs', axis=0)  16.4 us
    all_to_all x1, waiting for transfers between devices, body(): recv = lax.all_to_all(values, 'ord', 0, 0)  13.5 us
    all_to_all x1, blocking collectives, body(): recv = lax.all_to_all(values, 'ord', 0, 0)  12.1 us
    pallas_call x2, Pallas kernels, make_image(): pl.pallas_call(functools.partial(image_kernel, z, later), in_specs=[SMEM,...  11.4 us
    pallas_call x1, Pallas kernels, make_tables(): pl.pallas_call(functools.partial(tables_kernel, z), in_specs=[SMEM, SMEM,...  10.6 us
    pallas_call x2, Pallas kernels, make_step(): pl.pallas_call(functools.partial(step_kernel, z, later), in_specs=[SMEM,...  8.19 us
    all_to_all x1, starting transfers between devices, body(): recv = lax.all_to_all(seeds, 'ord', 0, 0)  7.32 us
    all_to_all x1, starting transfers between devices, body(): recv = lax.all_to_all(values, 'ord', 0, 0)  6.01 us
  transfers between devices with their start and end apart: 2, of which 1 were waited for; matrix products, arithmetic and copies ran while one was open for 0% of the time, Pallas kernels for 11%

profile of v3, /device:TPU:0, one launch (start us, length us, event | category | flops | bytes accessed | tf_op | source)
XLA Modules:
  0.0 93.8 jit_solution(2618313067746094982)
XLA Ops:
  0.6 0.0 copy-start.3
  0.6 0.0 copy-start.2
  0.7 0.0 copy-start.1
  0.7 0.0 copy-start
  0.7 0.0 copy-start.4
  0.7 0.7 copy-done.4
  1.4 0.0 copy-start.5
  1.4 2.4 %seeds.1 = f32[8,32,256]{2,1,0:T(8,128)} custom-call(s32[1]{0:T(128)} %bitcast.first_ref, s32[9]{0:T(128)S(1)} %copy-done.4, f32[1,9,288,256]{3,2,1,0:T(8,128)} %leg_ref.1), custom_call_target="tpu_custom_call" | custom-call | tf_op jit(solution)/shard_map/seeds/pallas_call | solution.py:116
  3.8 7.3 %all-to-all-start = ((f32[8,32,256]{2,1,0:T(8,128)}), f32[8,32,256]{2,1,0:T(8,128)S(1)}, u32[]{:S(2)}, u32[]{:S(2)}) async-start(f32[8,32,256]{2,1,0:T(8,128)} %seeds.1), calls=%async_computation | async-start | bytes 524288 | tf_op jit(solution)/shard_map/all_to_all | solution.py:580
  11.8 0.0 copy-done.3
  11.8 0.0 copy-done.2
  11.8 0.0 copy-done.1
  11.8 0.0 copy-done
  11.8 0.0 copy-done.5
  11.8 10.6 %tables.1 = (f32[2,40,128]{2,1,0:T(8,128)S(1)}, f32[2,24,128]{2,1,0:T(8,128)S(1)}) custom-call(s32[1]{0:T(128)} %bitcast.1.base_ref, s32[1]{0:T(128)S(6)} %copy.10.count_ref, s32[9]{0:T(128)S(1)} %copy-done.5, f32[256,128]{1,0:T(8,128)S(1)} %bitcast.12, s32[256,128]{1,0:T(8,128)S(1)} %bitcast.13, f32[256,128]{1,0:T(8,128)S(1)} %bitcast.14, ...), custom_call_target="tpu_custom_call" | custom-call | tf_op jit(solution)/shard_map/tables/pallas_call | solution.py:243
  22.4 0.0 all-to-all-done.recv_ref
  22.4 3.0 %functions.1 = (f32[2,2616,128]{2,1,0:T(8,128)S(1)}, f32[24,384]{1,0:T(8,128)S(1)}) custom-call(s32[9]{0:T(128)S(1)} %copy-done.5, f32[8,32,256]{2,1,0:T(8,128)S(1)} %all-to-all-done.recv_ref, f32[2,24,128]{2,1,0:T(8,128)S(1)} %get-tuple-element.21.ty_ref), custom_call_target="tpu_custom_call" | custom-call | tf_op jit(solution)/shard_map/functions/pallas_call | solution.py:356
  25.4 5.5 %all-gather = f32[96,384]{1,0:T(8,128)S(1)} all-gather(f32[24,384]{1,0:T(8,128)S(1)} %get-tuple-element.22), channel_id=2, replica_groups=mesh['obs'=4,'ord'=8] {'obs'}, dimensions={0}, use_global_device_ids=true | all-gather | bytes 184320 | tf_op jit(solution)/shard_map/all_gather | solution.py:587
  30.9 4.1 %step.2 = (f32[8,56,256]{2,1,0:T(8,128)}, f32[24,384]{1,0:T(8,128)S(1)}, f32[24,384]{1,0:T(8,128)S(1)}) custom-call(s32[9]{0:T(128)S(1)} %copy-done.5, f32[4,24,384]{2,1,0:T(8,128)S(1)} %bitcast.9, f32[9,288,288]{2,1,0:T(8,128)} %refs_1_.3, f32[2,2616,128]{2,1,0:T(8,128)S(1)} %get-tuple-element.23.refs_2_.func_ref, f32[2,40,128]{2,1,0:T(8,128)S(1)} %get-tuple-element.24.refs_3_), custom_call_target="tpu_custom_call" | custom-call | tf_op jit(solution)/shard_map/step/pallas_call | solution.py:434
  35.0 6.0 %all-to-all-start.1 = ((f32[8,56,256]{2,1,0:T(8,128)}), f32[8,56,256]{2,1,0:T(8,128)S(1)}, u32[]{:S(2)}, u32[]{:S(2)}) async-start(f32[8,56,256]{2,1,0:T(8,128)} %get-tuple-element.25), calls=%async_computation.1 | async-start | bytes 917504 | tf_op jit(solution)/shard_map/all_to_all | solution.py:589
  41.0 0.1 convert_element_type.6.ids_ref
  41.1 13.5 %all-to-all-done.1.recv_ref = f32[8,56,256]{2,1,0:T(8,128)S(1)} async-done(((f32[8,56,256]{2,1,0:T(8,128)}), f32[8,56,256]{2,1,0:T(8,128)S(1)}, u32[]{:S(2)}, u32[]{:S(2)}) %all-to-all-start.1) | async-done | bytes 458784 | tf_op jit(solution)/shard_map/all_to_all | solution.py:589
  54.6 5.9 %image.2 = (f32[24,384]{1,0:T(8,128)S(1)}, f32[8,128]{1,0:T(8,128)S(1)}, f32[2,216,128]{2,1,0:T(8,128)S(1)}, f32[2,216,128]{2,1,0:T(8,128)S(1)}, f32[2,2,72,128]{3,2,1,0:T(8,128)S(1)}) custom-call(s32[9]{0:T(128)S(1)} %copy-done.5, s32[72]{0:T(128)S(1)} %convert_element_type.6.ids_ref, f32[8,56,256]{2,1,0:T(8,128)S(1)} %all-to-all-done.1.recv_ref, ...), custom_call_target="tpu_custom_call" | custom-call | tf_op jit(solution)/shard_map/image/pallas_call | solution.py:534
  60.5 5.5 %all-gather.1 = f32[96,384]{1,0:T(8,128)S(1)} all-gather(f32[24,384]{1,0:T(8,128)S(1)} %get-tuple-element.26), channel_id=3, replica_groups=mesh['obs'=4,'ord'=8] {'obs'}, dimensions={0}, use_global_device_ids=true | all-gather | bytes 184320 | tf_op jit(solution)/shard_map/all_gather | solution.py:591
  66.0 4.0 %step.3 = (f32[8,24,256]{2,1,0:T(8,128)}, f32[24,384]{1,0:T(8,128)S(1)}, f32[24,384]{1,0:T(8,128)S(1)}, f32[24,384]{1,0:T(8,128)S(1)}) custom-call(s32[9]{0:T(128)S(1)} %copy-done.5, f32[4,24,384]{2,1,0:T(8,128)S(1)} %bitcast.10, f32[9,288,288]{2,1,0:T(8,128)} %refs_1_.3, f32[2,2616,128]{2,1,0:T(8,128)S(1)} %get-tuple-element.23.refs_2_.func_ref, ...), custom_call_target="tpu_custom_call" | custom-call | tf_op jit(solution)/shard_map/step/pallas_call | solution.py:434
  70.0 12.1 %all_to_all.15.recv_ref = f32[8,24,256]{2,1,0:T(8,128)S(1)} all-to-all(f32[8,24,256]{2,1,0:T(8,128)} %get-tuple-element.30), channel_id=1, replica_groups=mesh['obs'=4,'ord'=8] {'ord'}, dimensions={0} | all-to-all | bytes 393216 | tf_op jit(solution)/shard_map/all_to_all | solution.py:593
  82.2 5.5 %image.3 = (f32[24,384]{1,0:T(8,128)S(1)}, f32[8,128]{1,0:T(8,128)S(1)}, f32[24,384]{1,0:T(8,128)S(1)}, f32[2,2,72,128]{3,2,1,0:T(8,128)}) custom-call(s32[9]{0:T(128)S(1)} %copy-done.5, s32[72]{0:T(128)S(1)} %convert_element_type.6.ids_ref, f32[8,24,256]{2,1,0:T(8,128)S(1)} %all_to_all.15.recv_ref, f32[2,2616,128]{2,1,0:T(8,128)S(1)} %get-tuple-element.23.refs_2_.func_ref, ...), custom_call_target="tpu_custom_call" | custom-call | tf_op jit(solution)/shard_map/image/pallas_call | solution.py:534
  87.7 5.4 %all-gather.2 = f32[96,384]{1,0:T(8,128)S(1)} all-gather(f32[24,384]{1,0:T(8,128)S(1)} %get-tuple-element.35), channel_id=4, replica_groups=mesh['obs'=4,'ord'=8] {'obs'}, dimensions={0}, use_global_device_ids=true | all-gather | bytes 184320 | tf_op jit(solution)/shard_map/all_gather | solution.py:597
  93.1 0.7 last.1
  (1 shorter events, 0.0 us)
Async XLA Ops:
  0.6 11.2 %copy-start.3 = (f32[1,32768]{1,0:T(1,128)S(1)}, f32[1,32768]{1,0:T(1,128)}, u32[]{:S(2)}) copy-start(f32[1,32768]{1,0:T(1,128)} %param.12) | copy-start | bytes 393220
  0.6 11.2 %copy-start.2 = (f32[1,32768]{1,0:T(1,128)S(1)}, f32[1,32768]{1,0:T(1,128)}, u32[]{:S(2)}) copy-start(f32[1,32768]{1,0:T(1,128)} %param.11) | copy-start | bytes 393220
  0.7 11.2 %copy-start.1 = (s32[1,32768]{1,0:T(1,128)S(1)}, s32[1,32768]{1,0:T(1,128)}, u32[]{:S(2)}) copy-start(s32[1,32768]{1,0:T(1,128)} %param.9) | copy-start | bytes 393220
  0.7 11.2 %copy-start = (f32[1,32768]{1,0:T(1,128)S(1)}, f32[1,32768]{1,0:T(1,128)}, u32[]{:S(2)}) copy-start(f32[1,32768]{1,0:T(1,128)} %param.8) | copy-start | bytes 393220
  0.7 0.7 copy-start.4
  1.4 10.4 %copy-start.5 = (s32[9]{0:T(128)S(1)}, s32[9]{0:T(128)}, u32[]{:S(2)}) copy-start(s32[9]{0:T(128)} %own_ref.13) | copy-start | bytes 112
  3.8 18.6 %all-to-all-start = ((f32[8,32,256]{2,1,0:T(8,128)}), f32[8,32,256]{2,1,0:T(8,128)S(1)}, u32[]{:S(2)}, u32[]{:S(2)}) async-start(f32[8,32,256]{2,1,0:T(8,128)} %seeds.1), calls=%async_computation | async-start | bytes 524288 | tf_op jit(solution)/shard_map/all_to_all | solution.py:580
  35.0 19.6 %all-to-all-start.1 = ((f32[8,56,256]{2,1,0:T(8,128)}), f32[8,56,256]{2,1,0:T(8,128)S(1)}, u32[]{:S(2)}, u32[]{:S(2)}) async-start(f32[8,56,256]{2,1,0:T(8,128)} %get-tuple-element.25), calls=%async_computation.1 | async-start | bytes 917504 | tf_op jit(solution)/shard_map/all_to_all | solution.py:589

commit v4 on v3

--- a/solution.py
+++ b/solution.py
@@ -12,7 +12,6 @@
 VMEM_LIMIT = 24 << 20
 WINDOW = 32
 UNROLL = 4
-ORDERS_AT_ONCE = 2
 CHUNK = 1024
 F32 = jnp.float32
 BF16 = jnp.bfloat16
@@ -152,9 +151,14 @@
 
 
 def tables_kernel(z, base_ref, count_ref, own_ref, lon_ref, cyc_ref, data_ref, weight_ref,
-                  sum_ref, ty_ref, val, cyc_row, lhs, hot, acc, ids, pair_chunk, pair_window, sems):
-    scalars = pltpu.make_async_copy(cyc_ref, ids, sems.at[0])
-    scalars.start()
+                  sum_ref, ty_ref, val, powers, eights, cyc_row, lhs, hot, acc, ids, pair_chunk, pair_window, sems):
+    width = z.width
+    scalars = [
+        pltpu.make_async_copy(cyc_ref.at[pl.ds(c * width, 1), :], ids.at[pl.ds(c, 1), :], sems.at[c])
+        for c in range(z.chunks)
+    ]
+    for copy in scalars:
+        copy.start()
     total = z.slab * z.nobs
     size = min(32, z.rows)
 
@@ -171,10 +175,25 @@
             val[pl.ds((z.share + p) * z.skew + at, size), :] = s
             c, s = c * c1 - s * s1, s * c1 + c * s1
         scaled = scale * data_ref[pl.ds(at, size), :]
+        ones, none = jnp.ones((size, 128), F32), jnp.zeros((size, 128), F32)
+        c, s = ones, none
+        for p in range(8):
+            powers[0, p * size : p * size + size, :] = scaled * c
+            powers[1, p * size : p * size + size, :] = scaled * s
+            c, s = (c1, s1) if p == 0 else (c * c1 - s * s1, s * c1 + c * s1)
+        c8, s8 = c, s
+        c, s = ones, none
+        for p in range(z.no // 8):
+            eights[0, p * size : p * size + size, :] = c
+            eights[1, p * size : p * size + size, :] = s
+            c, s = (c8, s8) if p == 0 else (c * c8 - s * s8, s * c8 + c * s8)
         for slot in range(z.cnt):
-            c, s = sincos(own_ref[slot].astype(F32) * lon)
-            val[pl.ds((2 * z.share + slot) * z.skew + at, size), :] = c * scaled
-            val[pl.ds((2 * z.share + z.cnt + slot) * z.skew + at, size), :] = s * scaled
+            tens = own_ref[slot] // 8
+            small = pl.ds(pl.multiple_of((own_ref[slot] - tens * 8) * size, 8), size)
+            large = pl.ds(pl.multiple_of(tens * size, 8), size)
+            ca, sa, cb, sb = powers[0, small, :], powers[1, small, :], eights[0, large, :], eights[1, large, :]
+            val[pl.ds((2 * z.share + slot) * z.skew + at, size), :] = ca * cb - sa * sb
+            val[pl.ds((2 * z.share + z.cnt + slot) * z.skew + at, size), :] = sa * cb + ca * sb
         for row in range(2 * (z.share + z.cnt), z.sums):
             val[pl.ds(row * z.skew + at, size), :] = jnp.zeros((size, 128), F32)
         cyc_row[pl.ds(at, size), :] = cyc_ref[pl.ds(at, size), :].astype(F32)
@@ -182,7 +201,6 @@
 
     lax.fori_loop(0, z.rows // size, block, 0)
     acc[...] = jnp.zeros_like(acc)
-    width = z.width
 
     def fill(c, carry):
         for k in range(width):
@@ -197,14 +215,16 @@
         return carry
 
     lax.fori_loop(0, z.chunks, fill, 0)
-    scalars.wait()
+    for copy in scalars:
+        copy.wait()
     for n in range(z.pairs):
         pair_chunk[n] = 0
         pair_window[n] = z.windows
 
     def list_chunk(c, count):
-        low = ids[c * width, 0] // WINDOW
-        high = ids[c * width + width - 1, 127] // WINDOW
+        low = ids[c, 0] // WINDOW
+        following = ids[jnp.minimum(c + 1, z.chunks - 1), 0] // WINDOW
+        high = jnp.where(c + 1 < z.chunks, following, z.windows - 1)
 
         def add(w, at):
             pair_chunk[at] = c
@@ -250,14 +270,16 @@
         ],
         scratch_shapes=[
             pltpu.VMEM((up(z.sums * z.skew, 8), 128), F32),
+            pltpu.VMEM((2, 8 * min(32, z.rows), 128), F32),
+            pltpu.VMEM((2, z.no // 8 * min(32, z.rows), 128), F32),
             pltpu.VMEM((z.rows, 128), F32),
             pltpu.VMEM((z.chunks, z.sum_lanes, z.width * 128), BF16),
             pltpu.VMEM((UNROLL, WINDOW, z.width * 128), BF16),
             pltpu.VMEM((z.windows + 1, WINDOW, z.sum_lanes), F32),
-            pltpu.SMEM((z.rows, 128), jnp.int32),
+            pltpu.SMEM((z.chunks, 128), jnp.int32),
             pltpu.SMEM((z.pairs,), jnp.int32),
             pltpu.SMEM((z.pairs,), jnp.int32),
-            pltpu.SemaphoreType.DMA((1,)),
+            pltpu.SemaphoreType.DMA((z.chunks,)),
         ],
         compiler_params=pltpu.CompilerParams(vmem_limit_bytes=2 * z.limit),
         name="tables",
@@ -451,9 +473,9 @@
 def image_kernel(z, later, own_ref, ids_ref, recv_ref, func_ref, *refs):
     if later:
         tc_ref, ts_ref, old_ref, old_energy_ref, prec_ref, old_dir_ref = refs[:6]
-        out_ref, energy_ref, dir_ref, val_ref, all_rows, rows, cols = refs[6:]
+        out_ref, energy_ref, dir_ref, val_ref, rows, cols = refs[6:]
     else:
-        out_ref, energy_ref, tc_ref, ts_ref, val_ref, all_rows, rows, cols = refs
+        out_ref, energy_ref, tc_ref, ts_ref, val_ref, rows, cols = refs
         top = 2 * z.cnt + 1
         for o in range(z.nord):
             at = z.off + o * z.share
@@ -491,35 +513,48 @@
                 val_ref[k, h] = val_ref[k, h] + ratio * old_ref[k, h]
         dir_ref[...] = prec_ref[...] + ratio[:, 0:1] * old_dir_ref[...]
 
-    def some_orders(step, carry):
+    tiles = z.no // 8
+
+    def sums_of(m, h, chosen):
+        both = None
+        for tile in chosen:
+            vc, vs = val_ref[0, h, tile * 8 : tile * 8 + 8, :], val_ref[1, h, tile * 8 : tile * 8 + 8, :]
+            low, high = pl.ds(z.off + tile * 8 - m, 8), pl.ds(z.off + tile * 8 + m, 8)
+            near, far = tc_ref[h, low, :], tc_ref[h, high, :]
+            snear, sfar = ts_ref[h, low, :], ts_ref[h, high, :]
+            wc = (near + far) * vc + (sfar + snear) * vs
+            ws = (sfar - snear) * vc + (near - far) * vs
+            both = (wc, ws) if both is None else (both[0] + wc, both[1] + ws)
+        return both
+
+    for i in range(z.cnt):
         for h in range(z.halves):
-            sums = [[None] * 2 for _ in range(ORDERS_AT_ONCE)]
-            for tile in range(z.no // 8):
-                vc, vs = val_ref[0, h, tile * 8 : tile * 8 + 8, :], val_ref[1, h, tile * 8 : tile * 8 + 8, :]
-                for u in range(ORDERS_AT_ONCE):
-                    m = step * ORDERS_AT_ONCE + u
-                    low, high = pl.ds(z.off + tile * 8 - m, 8), pl.ds(z.off + tile * 8 + m, 8)
-                    near, far = tc_ref[h, low, :], tc_ref[h, high, :]
-                    snear, sfar = ts_ref[h, low, :], ts_ref[h, high, :]
-                    wc = (near + far) * vc + (sfar + snear) * vs
-                    ws = (sfar - snear) * vc + (near - far) * vs
-                    sums[u] = [wc, ws] if tile == 0 else [sums[u][0] + wc, sums[u][1] + ws]
-            for u in range(ORDERS_AT_ONCE):
-                m = step * ORDERS_AT_ONCE + u
-                for k in range(2):
-                    all_rows[k * z.halves + h, pl.ds(m, 1), :] = 0.5 * jnp.sum(sums[u][k], axis=0, keepdims=True)
-        return carry
-
-    lax.fori_loop(0, z.no // ORDERS_AT_ONCE, some_orders, 0)
-    curvature = jnp.zeros((z.no, 128), F32)
-    for k in range(2):
-        for h in range(z.halves):
-            curvature = curvature + all_rows[k * z.halves + h] * val_ref[k, h]
-    for i in range(z.cnt):
-        for k in range(2):
-            r = k * z.cnt + i
+            for k, value in enumerate(sums_of(own_ref[i], h, range(tiles))):
+                r = k * z.cnt + i
+                rows[h, r : r + 1, :] = 0.5 * jnp.sum(value, axis=0, keepdims=True)
+
+    def times_row(m, h, value):
+        at = pl.ds(m, 1)
+        return val_ref[0, h, at, :] * value[0] + val_ref[1, h, at, :] * value[1]
+
+    curvature = jnp.zeros((8, 128), F32)
+    if z.no <= 128:
+        for m in range(z.no):
             for h in range(z.halves):
-                rows[h, r : r + 1, :] = all_rows[k * z.halves + h, pl.ds(own_ref[i], 1), :]
+                value = sums_of(m, h, [m // 8])
+                if m // 8 + 1 < tiles:
+                    above = sums_of(m, h, range(m // 8 + 1, tiles))
+                    value = [v + 2.0 * w for v, w in zip(value, above)]
+                curvature = curvature + times_row(m, h, value)
+    else:
+
+        def one_order(m, total):
+            for h in range(z.halves):
+                total = total + times_row(m, h, sums_of(m, h, range(tiles)))
+            return total
+
+        curvature = lax.fori_loop(0, z.no, one_order, curvature)
+    curvature = 0.5 * curvature
     adjoint_into(z, func_ref, rows, cols, out_ref)
     out_ref[2 * z.cnt : 2 * z.cnt + 1, :] = jnp.broadcast_to(full_sum(curvature), (1, z.state[1]))
 
@@ -537,7 +572,6 @@
         out_specs=[VMEM] * len(outs),
         out_shape=outs,
         scratch_shapes=[
-            pltpu.VMEM((2 * z.halves, z.no, 128), F32),
             pltpu.VMEM((z.halves, z.pay, 128), F32),
             pltpu.VMEM((z.state[1], 128), F32),
         ],

time: 94.3 us -> 90.2 us (0.957)
  Pallas kernels: 36.2 us -> 32.2 us
    pallas_call x2, Pallas kernels: 11.4 us -> 7.57 us  [make_image(): pl.pallas_call(functools.partial(image_kernel, z, later), in_specs=[SMEM,...]
  transfers between devices with their start and end apart: 2 -> 2, of which waited for: 1 -> 1; matrix products, arithmetic and copies ran while one was open for 0% -> 0% of each run, Pallas kernels for 11% -> 12%
where the time goes in v4:
time: 90.2 us; the launch traced here: 89.7 us
  Pallas kernels  32.2 us (36%)
  blocking collectives  28.5 us (32%)
  waiting for transfers between devices  13.5 us (15%)
  starting transfers between devices  13.3 us (15%)
  between operations  1.42 us (2%)
    all_gather x3, blocking collectives, body(): gathered = lax.all_gather(part, 'obs', axis=0)  16.4 us
    all_to_all x1, waiting for transfers between devices, body(): recv = lax.all_to_all(values, 'ord', 0, 0)  13.5 us
    all_to_all x1, blocking collectives, body(): recv = lax.all_to_all(values, 'ord', 0, 0)  12.1 us
    pallas_call x1, Pallas kernels, make_tables(): pl.pallas_call(functools.partial(tables_kernel, z), in_specs=[SMEM, SMEM,...  10.3 us
    pallas_call x2, Pallas kernels, make_step(): pl.pallas_call(functools.partial(step_kernel, z, later), in_specs=[SMEM,...  8.19 us
    pallas_call x2, Pallas kernels, make_image(): pl.pallas_call(functools.partial(image_kernel, z, later), in_specs=[SMEM,...  7.57 us
    all_to_all x1, starting transfers between devices, body(): recv = lax.all_to_all(seeds, 'ord', 0, 0)  7.32 us
    all_to_all x1, starting transfers between devices, body(): recv = lax.all_to_all(values, 'ord', 0, 0)  6.01 us
  transfers between devices with their start and end apart: 2, of which 1 were waited for; matrix products, arithmetic and copies ran while one was open for 0% of the time, Pallas kernels for 12%

profile of v4, /device:TPU:0, one launch (start us, length us, event | category | flops | bytes accessed | tf_op | source)
XLA Modules:
  0.0 89.7 jit_solution(1995123213357964337)
XLA Ops:
  0.6 0.0 copy-start.3
  0.6 0.0 copy-start.2
  0.7 0.0 copy-start.1
  0.7 0.0 copy-start
  0.7 0.0 copy-start.4
  0.7 0.7 copy-done.4
  1.4 0.0 copy-start.5
  1.4 2.4 %seeds.1 = f32[8,32,256]{2,1,0:T(8,128)} custom-call(s32[1]{0:T(128)} %bitcast.first_ref, s32[9]{0:T(128)S(1)} %copy-done.4, f32[1,9,288,256]{3,2,1,0:T(8,128)} %leg_ref.1), custom_call_target="tpu_custom_call" | custom-call | tf_op jit(solution)/shard_map/seeds/pallas_call | solution.py:115
  3.8 7.3 %all-to-all-start = ((f32[8,32,256]{2,1,0:T(8,128)}), f32[8,32,256]{2,1,0:T(8,128)S(1)}, u32[]{:S(2)}, u32[]{:S(2)}) async-start(f32[8,32,256]{2,1,0:T(8,128)} %seeds.1), calls=%async_computation | async-start | bytes 524288 | tf_op jit(solution)/shard_map/all_to_all | solution.py:614
  11.8 0.0 copy-done.3
  11.8 0.0 copy-done.2
  11.8 0.0 copy-done.1
  11.8 0.0 copy-done
  11.8 0.0 copy-done.5
  11.8 10.3 %tables.1 = (f32[2,40,128]{2,1,0:T(8,128)S(1)}, f32[2,24,128]{2,1,0:T(8,128)S(1)}) custom-call(s32[1]{0:T(128)} %bitcast.1.base_ref, s32[1]{0:T(128)S(6)} %copy.10.count_ref, s32[9]{0:T(128)S(1)} %copy-done.5, f32[256,128]{1,0:T(8,128)S(1)} %bitcast.12, s32[256,128]{1,0:T(8,128)S(1)} %bitcast.13, f32[256,128]{1,0:T(8,128)S(1)} %bitcast.14, ...), custom_call_target="tpu_custom_call" | custom-call | tf_op jit(solution)/shard_map/tables/pallas_call | solution.py:263
  22.2 0.0 all-to-all-done.recv_ref
  22.2 3.0 %functions.1 = (f32[2,2616,128]{2,1,0:T(8,128)S(1)}, f32[24,384]{1,0:T(8,128)S(1)}) custom-call(s32[9]{0:T(128)S(1)} %copy-done.5, f32[8,32,256]{2,1,0:T(8,128)S(1)} %all-to-all-done.recv_ref, f32[2,24,128]{2,1,0:T(8,128)S(1)} %get-tuple-element.21.ty_ref), custom_call_target="tpu_custom_call" | custom-call | tf_op jit(solution)/shard_map/functions/pallas_call | solution.py:378
  25.2 5.5 %all-gather = f32[96,384]{1,0:T(8,128)S(1)} all-gather(f32[24,384]{1,0:T(8,128)S(1)} %get-tuple-element.22), channel_id=2, replica_groups=mesh['obs'=4,'ord'=8] {'obs'}, dimensions={0}, use_global_device_ids=true | all-gather | bytes 184320 | tf_op jit(solution)/shard_map/all_gather | solution.py:621
  30.6 4.1 %step.2 = (f32[8,56,256]{2,1,0:T(8,128)}, f32[24,384]{1,0:T(8,128)S(1)}, f32[24,384]{1,0:T(8,128)S(1)}) custom-call(s32[9]{0:T(128)S(1)} %copy-done.5, f32[4,24,384]{2,1,0:T(8,128)S(1)} %bitcast.9, f32[9,288,288]{2,1,0:T(8,128)} %refs_1_.3, f32[2,2616,128]{2,1,0:T(8,128)S(1)} %get-tuple-element.23.refs_2_.func_ref, f32[2,40,128]{2,1,0:T(8,128)S(1)} %get-tuple-element.24.refs_3_), custom_call_target="tpu_custom_call" | custom-call | tf_op jit(solution)/shard_map/step/pallas_call | solution.py:456
  34.8 6.0 %all-to-all-start.1 = ((f32[8,56,256]{2,1,0:T(8,128)}), f32[8,56,256]{2,1,0:T(8,128)S(1)}, u32[]{:S(2)}, u32[]{:S(2)}) async-start(f32[8,56,256]{2,1,0:T(8,128)} %get-tuple-element.25), calls=%async_computation.1 | async-start | bytes 917504 | tf_op jit(solution)/shard_map/all_to_all | solution.py:623
  40.8 0.1 convert_element_type.6.ids_ref
  40.9 13.5 %all-to-all-done.1.recv_ref = f32[8,56,256]{2,1,0:T(8,128)S(1)} async-done(((f32[8,56,256]{2,1,0:T(8,128)}), f32[8,56,256]{2,1,0:T(8,128)S(1)}, u32[]{:S(2)}, u32[]{:S(2)}) %all-to-all-start.1) | async-done | bytes 458784 | tf_op jit(solution)/shard_map/all_to_all | solution.py:623
  54.4 3.9 %image.2 = (f32[24,384]{1,0:T(8,128)S(1)}, f32[8,128]{1,0:T(8,128)S(1)}, f32[2,216,128]{2,1,0:T(8,128)S(1)}, f32[2,216,128]{2,1,0:T(8,128)S(1)}, f32[2,2,72,128]{3,2,1,0:T(8,128)S(1)}) custom-call(s32[9]{0:T(128)S(1)} %copy-done.5, s32[72]{0:T(128)S(1)} %convert_element_type.6.ids_ref, f32[8,56,256]{2,1,0:T(8,128)S(1)} %all-to-all-done.1.recv_ref, ...), custom_call_target="tpu_custom_call" | custom-call | tf_op jit(solution)/shard_map/image/pallas_call | solution.py:569
  58.3 5.5 %all-gather.1 = f32[96,384]{1,0:T(8,128)S(1)} all-gather(f32[24,384]{1,0:T(8,128)S(1)} %get-tuple-element.26), channel_id=3, replica_groups=mesh['obs'=4,'ord'=8] {'obs'}, dimensions={0}, use_global_device_ids=true | all-gather | bytes 184320 | tf_op jit(solution)/shard_map/all_gather | solution.py:625
  63.7 4.0 %step.3 = (f32[8,24,256]{2,1,0:T(8,128)}, f32[24,384]{1,0:T(8,128)S(1)}, f32[24,384]{1,0:T(8,128)S(1)}, f32[24,384]{1,0:T(8,128)S(1)}) custom-call(s32[9]{0:T(128)S(1)} %copy-done.5, f32[4,24,384]{2,1,0:T(8,128)S(1)} %bitcast.10, f32[9,288,288]{2,1,0:T(8,128)} %refs_1_.3, f32[2,2616,128]{2,1,0:T(8,128)S(1)} %get-tuple-element.23.refs_2_.func_ref, ...), custom_call_target="tpu_custom_call" | custom-call | tf_op jit(solution)/shard_map/step/pallas_call | solution.py:456
  67.8 12.1 %all_to_all.15.recv_ref = f32[8,24,256]{2,1,0:T(8,128)S(1)} all-to-all(f32[8,24,256]{2,1,0:T(8,128)} %get-tuple-element.30), channel_id=1, replica_groups=mesh['obs'=4,'ord'=8] {'ord'}, dimensions={0} | all-to-all | bytes 393216 | tf_op jit(solution)/shard_map/all_to_all | solution.py:627
  79.9 3.7 %image.3 = (f32[24,384]{1,0:T(8,128)S(1)}, f32[8,128]{1,0:T(8,128)S(1)}, f32[24,384]{1,0:T(8,128)S(1)}, f32[2,2,72,128]{3,2,1,0:T(8,128)}) custom-call(s32[9]{0:T(128)S(1)} %copy-done.5, s32[72]{0:T(128)S(1)} %convert_element_type.6.ids_ref, f32[8,24,256]{2,1,0:T(8,128)S(1)} %all_to_all.15.recv_ref, f32[2,2616,128]{2,1,0:T(8,128)S(1)} %get-tuple-element.23.refs_2_.func_ref, ...), custom_call_target="tpu_custom_call" | custom-call | tf_op jit(solution)/shard_map/image/pallas_call | solution.py:569
  83.6 5.4 %all-gather.2 = f32[96,384]{1,0:T(8,128)S(1)} all-gather(f32[24,384]{1,0:T(8,128)S(1)} %get-tuple-element.35), channel_id=4, replica_groups=mesh['obs'=4,'ord'=8] {'obs'}, dimensions={0}, use_global_device_ids=true | all-gather | bytes 184320 | tf_op jit(solution)/shard_map/all_gather | solution.py:631
  89.0 0.7 last.1
  (1 shorter events, 0.0 us)
Async XLA Ops:
  0.6 11.2 %copy-start.3 = (f32[1,32768]{1,0:T(1,128)S(1)}, f32[1,32768]{1,0:T(1,128)}, u32[]{:S(2)}) copy-start(f32[1,32768]{1,0:T(1,128)} %param.12) | copy-start | bytes 393220
  0.6 11.2 %copy-start.2 = (f32[1,32768]{1,0:T(1,128)S(1)}, f32[1,32768]{1,0:T(1,128)}, u32[]{:S(2)}) copy-start(f32[1,32768]{1,0:T(1,128)} %param.11) | copy-start | bytes 393220
  0.7 11.2 %copy-start.1 = (s32[1,32768]{1,0:T(1,128)S(1)}, s32[1,32768]{1,0:T(1,128)}, u32[]{:S(2)}) copy-start(s32[1,32768]{1,0:T(1,128)} %param.9) | copy-start | bytes 393220
  0.7 11.2 %copy-start = (f32[1,32768]{1,0:T(1,128)S(1)}, f32[1,32768]{1,0:T(1,128)}, u32[]{:S(2)}) copy-start(f32[1,32768]{1,0:T(1,128)} %param.8) | copy-start | bytes 393220
  0.7 0.7 copy-start.4
  1.4 10.4 %copy-start.5 = (s32[9]{0:T(128)S(1)}, s32[9]{0:T(128)}, u32[]{:S(2)}) copy-start(s32[9]{0:T(128)} %own_ref.13) | copy-start | bytes 112
  3.8 18.4 %all-to-all-start = ((f32[8,32,256]{2,1,0:T(8,128)}), f32[8,32,256]{2,1,0:T(8,128)S(1)}, u32[]{:S(2)}, u32[]{:S(2)}) async-start(f32[8,32,256]{2,1,0:T(8,128)} %seeds.1), calls=%async_computation | async-start | bytes 524288 | tf_op jit(solution)/shard_map/all_to_all | solution.py:614
  34.8 19.6 %all-to-all-start.1 = ((f32[8,56,256]{2,1,0:T(8,128)}), f32[8,56,256]{2,1,0:T(8,128)S(1)}, u32[]{:S(2)}, u32[]{:S(2)}) async-start(f32[8,56,256]{2,1,0:T(8,128)} %get-tuple-element.25), calls=%async_computation.1 | async-start | bytes 917504 | tf_op jit(solution)/shard_map/all_to_all | solution.py:623

commit v5 on v4

--- a/solution.py
+++ b/solution.py
@@ -11,7 +11,7 @@
 SEGMENTS = 2
 VMEM_LIMIT = 24 << 20
 WINDOW = 32
-UNROLL = 4
+UNROLL = 8
 CHUNK = 1024
 F32 = jnp.float32
 BF16 = jnp.bfloat16
@@ -76,7 +76,8 @@
         copy.wait()
 
 
-def seeds_kernel(z, first_ref, own_ref, leg_ref, out_ref, stage, keep, sems, out_sems):
+def seeds_kernel(z, first_ref, own_ref, leg_ref, *refs):
+    held, (out_ref, *near), (stage, keep, sems, out_sems, near_sems) = refs[:4], refs[4:9], refs[9:]
     copies = []
 
     def fetch(i, at):
@@ -90,6 +91,9 @@
     fetch(0, 0)
     for copy in copies:
         copy.start()
+    moves = [pltpu.make_async_copy(held[n], near[n], near_sems.at[n]) for n in range(4)]
+    for move in moves:
+        move.start()
     lane = iota((z.seeds - z.id_row, z.cyc), 1)
     ids = jnp.zeros(lane.shape, F32)
     for slot in range(z.cnt):
@@ -108,24 +112,28 @@
         keep[top : top + 1, :] = jnp.sum(jnp.where(mine, block, 0.0), axis=0, keepdims=True)
     keep[z.cos_row : z.cos_row + 1, :] = stage[z.cnt * z.seg, 1:2, :]
     send_copies(z, keep, out_ref, out_sems)
-
-
-def make_seeds(z, first, own, legendre):
+    for move in moves:
+        move.wait()
+
+
+def make_seeds(z, first, own, legendre, held):
     slabs = z.cnt * z.seg + 1
     return pl.pallas_call(
         functools.partial(seeds_kernel, z),
-        in_specs=[SMEM, SMEM, HBM],
-        out_specs=HBM,
-        out_shape=pltpu.MemorySpace.HBM((z.nord, z.seeds, z.cyc), F32),
+        in_specs=[SMEM, SMEM, HBM] + [HBM] * 4,
+        out_specs=[HBM] + [VMEM] * 4,
+        out_shape=[pltpu.MemorySpace.HBM((z.nord, z.seeds, z.cyc), F32)]
+        + [jax.ShapeDtypeStruct(value.shape, value.dtype) for value in held],
         scratch_shapes=[
             pltpu.VMEM((slabs, 8, z.cyc), F32),
             pltpu.VMEM((z.seeds, z.cyc), F32),
             pltpu.SemaphoreType.DMA((slabs,)),
             pltpu.SemaphoreType.DMA((z.nord,)),
+            pltpu.SemaphoreType.DMA((4,)),
         ],
         compiler_params=pltpu.CompilerParams(vmem_limit_bytes=z.limit),
         name="seeds",
-    )(first, own, legendre)
+    )(first, own, legendre, *held)
 
 
 def sincos(angle):
@@ -312,7 +320,9 @@
     flip(z, cols_ref, out_ref)
 
 
-def functions_kernel(z, own_ref, recv_ref, ty_ref, func_ref, out_ref, seed0, seed1, first, cols):
+def functions_kernel(z, own_ref, recv_ref, ty_ref, inv_ref, func_ref, out_ref, inv_out, seed0, seed1, first, cols, sem):
+    fetch = pltpu.make_async_copy(inv_ref, inv_out, sem.at[0])
+    fetch.start()
     total = z.seg * z.cnt
     padded = up(total, 8)
     for slot in range(z.cnt):
@@ -371,22 +381,25 @@
                 func_ref[h, pl.ds(tile * 8 * z.seg_skew + t, left, stride=z.seg_skew), :] = now[h][:left]
             before, prev, now = prev, now, [None] * z.halves
     adjoint_into(z, func_ref, ty_ref, cols, out_ref)
-
-
-def make_functions(z, own, recv, ty):
+    fetch.wait()
+
+
+def make_functions(z, own, recv, ty, inv):
     padded = up(z.seg * z.cnt, 8)
     return pl.pallas_call(
         functools.partial(functions_kernel, z),
-        in_specs=[SMEM, VMEM, VMEM],
-        out_specs=[VMEM] * 2,
+        in_specs=[SMEM, VMEM, VMEM, HBM],
+        out_specs=[VMEM] * 3,
         out_shape=[
             jax.ShapeDtypeStruct((z.halves, z.func_rows, 128), F32),
             jax.ShapeDtypeStruct(z.state, F32),
+            jax.ShapeDtypeStruct(inv.shape, F32),
         ],
-        scratch_shapes=[pltpu.VMEM((padded, z.cyc), F32)] * 3 + [pltpu.VMEM((z.state[1], 128), F32)],
+        scratch_shapes=[pltpu.VMEM((padded, z.cyc), F32)] * 3
+        + [pltpu.VMEM((z.state[1], 128), F32), pltpu.SemaphoreType.DMA((1,))],
         compiler_params=pltpu.CompilerParams(vmem_limit_bytes=z.limit),
         name="functions",
-    )(own, recv, ty)
+    )(own, recv, ty, inv)
 
 
 def total_of(z, gathered_ref):
@@ -403,13 +416,10 @@
 def step_kernel(z, later, own_ref, *refs):
     if later:
         gathered_ref, inv_ref, func_ref, energy_ref, res_ref, dir_ref = refs[:6]
-        out_ref, newres_ref, prec_ref, sol_ref, cols, pay, inv_buf, sems, inv_sems = refs[6:]
+        out_ref, newres_ref, prec_ref, sol_ref, cols, pay, sems = refs[6:]
     else:
         gathered_ref, inv_ref, func_ref, sum_ref = refs[:4]
-        out_ref, newres_ref, prec_ref, cols, pay, inv_buf, sems, inv_sems = refs[4:]
-    fetches = [pltpu.make_async_copy(inv_ref.at[slot], inv_buf.at[slot], inv_sems.at[slot]) for slot in range(z.cnt)]
-    for fetch in fetches:
-        fetch.start()
+        out_ref, newres_ref, prec_ref, cols, pay, sems = refs[4:]
     summed, curvature = total_of(z, gathered_ref)
     if later:
         step_size = energy_ref[0:1, 0:1] / curvature
@@ -420,13 +430,12 @@
     cols[...] = jnp.zeros_like(cols)
     height = iota((8, 128), 0)
     for slot in range(z.cnt):
-        fetches[slot].wait()
         vec = [
             jnp.broadcast_to(newres_ref[k * z.cnt + slot : k * z.cnt + slot + 1, 0 : z.nb], (8, z.nb)) for k in range(2)
         ]
         acc = [[jnp.zeros((8, 128), F32)] * z.halves for k in range(2)]
         for a in range(z.steps):
-            block = inv_buf[slot, 8 * a : 8 * a + 8, :]
+            block = inv_ref[slot, 8 * a : 8 * a + 8, :]
             live = height >= own_ref[slot] - 8 * a
             f = [func_ref[h, pl.ds(z.func_row(slot, a), 8), :] for h in range(z.halves)]
             for k in range(2):
@@ -455,15 +464,13 @@
     args = [own, gathered, inv, func] + list(state)
     return pl.pallas_call(
         functools.partial(step_kernel, z, later),
-        in_specs=[SMEM, VMEM, HBM] + [VMEM] * (len(args) - 3),
+        in_specs=[SMEM] + [VMEM] * (len(args) - 1),
         out_specs=[HBM] + [VMEM] * (len(outs) - 1),
         out_shape=outs,
         scratch_shapes=[
             pltpu.VMEM((z.state[1], 128), F32),
             pltpu.VMEM(outs[0].shape[1:], F32),
-            pltpu.VMEM(inv.shape, F32),
             pltpu.SemaphoreType.DMA((z.nord,)),
-            pltpu.SemaphoreType.DMA((z.cnt,)),
         ],
         compiler_params=pltpu.CompilerParams(vmem_limit_bytes=z.limit),
         name="step",
@@ -475,7 +482,9 @@
         tc_ref, ts_ref, old_ref, old_energy_ref, prec_ref, old_dir_ref = refs[:6]
         out_ref, energy_ref, dir_ref, val_ref, rows, cols = refs[6:]
     else:
-        out_ref, energy_ref, tc_ref, ts_ref, val_ref, rows, cols = refs
+        inv_ref, out_ref, energy_ref, tc_ref, ts_ref, val_ref, inv_out, rows, cols, sem = refs
+        fetch = pltpu.make_async_copy(inv_ref, inv_out, sem.at[0])
+        fetch.start()
         top = 2 * z.cnt + 1
         for o in range(z.nord):
             at = z.off + o * z.share
@@ -557,24 +566,28 @@
     curvature = 0.5 * curvature
     adjoint_into(z, func_ref, rows, cols, out_ref)
     out_ref[2 * z.cnt : 2 * z.cnt + 1, :] = jnp.broadcast_to(full_sum(curvature), (1, z.state[1]))
-
-
-def make_image(z, own, ids, recv, func, state=()):
-    later = len(state) > 0
+    if not later:
+        fetch.wait()
+
+
+def make_image(z, own, ids, recv, func, state, later):
     vector = jax.ShapeDtypeStruct(z.state, F32)
     table = jax.ShapeDtypeStruct((z.halves, z.table, 128), F32)
     outs = [vector, jax.ShapeDtypeStruct((8, 128), F32)] + ([vector] if later else [table, table])
     outs.append(jax.ShapeDtypeStruct((2, z.halves, z.no, 128), F32))
+    if not later:
+        outs.append(jax.ShapeDtypeStruct(state[0].shape, F32))
     args = [own, ids, recv, func] + list(state)
     return pl.pallas_call(
         functools.partial(image_kernel, z, later),
-        in_specs=[SMEM, SMEM] + [VMEM] * (len(args) - 2),
+        in_specs=[SMEM, SMEM, VMEM, VMEM] + ([VMEM] * len(state) if later else [HBM]),
         out_specs=[VMEM] * len(outs),
         out_shape=outs,
         scratch_shapes=[
             pltpu.VMEM((z.halves, z.pay, 128), F32),
             pltpu.VMEM((z.state[1], 128), F32),
-        ],
+        ]
+        + ([] if later else [pltpu.SemaphoreType.DMA((1,))]),
         compiler_params=pltpu.CompilerParams(vmem_limit_bytes=z.limit),
         name="image",
     )(*args)
@@ -606,27 +619,27 @@
 
 def body(longitude, cycle_of, obs_count, observed, obs_weight, legendre, precond_inv, order_of_slot):
     z = Sizes(legendre, longitude.shape[1])
-    dense = lambda value: value.reshape(z.rows, 128)
+    dense = lambda value: pltpu.with_memory_space_constraint(value.reshape(z.rows, 128), pltpu.MemorySpace.HBM)
+    held = [dense(value) for value in (longitude, cycle_of, observed, obs_weight)]
     legendre = pltpu.with_memory_space_constraint(legendre, pltpu.MemorySpace.HBM)
+    order_of_slot = pltpu.with_memory_space_constraint(order_of_slot, pltpu.MemorySpace.HBM)
     inv = pltpu.with_memory_space_constraint(precond_inv, pltpu.MemorySpace.HBM)
     first = (lax.axis_index("ord") * z.cnt).astype(jnp.int32).reshape(1)
-    seeds = make_seeds(z, first, order_of_slot, legendre)
+    seeds, *near = make_seeds(z, first, order_of_slot, legendre, held)
     recv = lax.all_to_all(seeds, "ord", 0, 0)
     base = (lax.axis_index("ord") * z.share).astype(jnp.int32).reshape(1)
-    sums, ty = make_tables(
-        z, base, obs_count, order_of_slot, dense(longitude), dense(cycle_of), dense(observed), dense(obs_weight)
-    )
+    sums, ty = make_tables(z, base, obs_count, order_of_slot, *near)
     ids = recv[:, z.id_row, : z.cnt].reshape(z.no).astype(jnp.int32)
-    func, part = make_functions(z, order_of_slot, recv, ty)
+    func, part, near_inv = make_functions(z, order_of_slot, recv, ty, inv)
     gathered = lax.all_gather(part, "obs", axis=0)
-    values, res, direction = make_step(z, order_of_slot, gathered, inv, func, (sums,), False)
+    values, res, direction = make_step(z, order_of_slot, gathered, near_inv, func, (sums,), False)
     recv = lax.all_to_all(values, "ord", 0, 0)
-    part, energy, tc, ts, all_values = make_image(z, order_of_slot, ids, recv, func)
+    part, energy, tc, ts, all_values, near_inv = make_image(z, order_of_slot, ids, recv, func, (inv,), False)
     gathered = lax.all_gather(part, "obs", axis=0)
-    values, res, prec, sol = make_step(z, order_of_slot, gathered, inv, func, (energy, res, direction), True)
+    values, res, prec, sol = make_step(z, order_of_slot, gathered, near_inv, func, (energy, res, direction), True)
     recv = lax.all_to_all(values, "ord", 0, 0)
     part, energy, direction, all_values = make_image(
-        z, order_of_slot, ids, recv, func, (tc, ts, all_values, energy, prec, direction)
+        z, order_of_slot, ids, recv, func, (tc, ts, all_values, energy, prec, direction), True
     )
     gathered = lax.all_gather(part, "obs", axis=0)
     return tuple(make_last(z, gathered, energy, res, sol, direction))

time: 90.2 us -> 87.3 us (0.968)
  Pallas kernels: 32.2 us -> 30 us
    pallas_call x2, Pallas kernels: 8.19 us -> 5.55 us  [make_step(): pl.pallas_call(functools.partial(step_kernel, z, later), in_specs=[SMEM]...]
  transfers between devices with their start and end apart: 2 -> 2, of which waited for: 1 -> 1; matrix products, arithmetic and copies ran while one was open for 0% -> 0% of each run, Pallas kernels for 12% -> 11%
where the time goes in v5:
time: 87.3 us; the launch traced here: 86.7 us
  Pallas kernels  30 us (34%)
  blocking collectives  28.4 us (33%)
  waiting for transfers between devices  13.5 us (15%)
  starting transfers between devices  13.3 us (15%)
  between operations  1.35 us (2%)
    all_gather x3, blocking collectives, body(): gathered = lax.all_gather(part, 'obs', axis=0)  16.4 us
    all_to_all x1, waiting for transfers between devices, body(): recv = lax.all_to_all(values, 'ord', 0, 0)  13.5 us
    all_to_all x1, blocking collectives, body(): recv = lax.all_to_all(values, 'ord', 0, 0)  12.1 us
    pallas_call x1, Pallas kernels, make_tables(): pl.pallas_call(functools.partial(tables_kernel, z), in_specs=[SMEM, SMEM,...  9.9 us
    pallas_call x2, Pallas kernels, make_image(): pl.pallas_call(functools.partial(image_kernel, z, later), in_specs=[SMEM,...  7.77 us
    all_to_all x1, starting transfers between devices, body(): recv = lax.all_to_all(seeds, 'ord', 0, 0)  7.32 us
    all_to_all x1, starting transfers between devices, body(): recv = lax.all_to_all(values, 'ord', 0, 0)  6.01 us
    pallas_call x2, Pallas kernels, make_step(): pl.pallas_call(functools.partial(step_kernel, z, later), in_specs=[SMEM]...  5.55 us
  transfers between devices with their start and end apart: 2, of which 1 were waited for; matrix products, arithmetic and copies ran while one was open for 0% of the time, Pallas kernels for 11%

profile of v5, /device:TPU:0, one launch (start us, length us, event | category | flops | bytes accessed | tf_op | source)
XLA Modules:
  0.0 86.7 jit_solution(2155568729603863492)
XLA Ops:
  0.6 2.8 %seeds.1 = (f32[8,32,256]{2,1,0:T(8,128)}, f32[256,128]{1,0:T(8,128)S(1)}, s32[256,128]{1,0:T(8,128)S(1)}, f32[256,128]{1,0:T(8,128)S(1)}, f32[256,128]{1,0:T(8,128)S(1)}) custom-call(s32[1]{0:T(128)} %bitcast.first_ref, s32[9]{0:T(128)} %own_ref.13, f32[1,9,288,256]{3,2,1,0:T(8,128)} %leg_ref.1, f32[256,128]{1,0:T(8,128)} %bitcast.12, s32[256,128]{1,0:T(8,128)} %bitcast.13, ...), custom_call_target="tpu_custom_call" | custom-call | tf_op jit(solution)/shard_map/seeds/pallas_call | solution.py:121
  3.4 7.3 %all-to-all-start = ((f32[8,32,256]{2,1,0:T(8,128)}), f32[8,32,256]{2,1,0:T(8,128)S(1)}, u32[]{:S(2)}, u32[]{:S(2)}) async-start(f32[8,32,256]{2,1,0:T(8,128)} %get-tuple-element.28), calls=%async_computation | async-start | bytes 524288 | tf_op jit(solution)/shard_map/all_to_all | solution.py:629
  11.4 9.9 %tables.1 = (f32[2,40,128]{2,1,0:T(8,128)S(1)}, f32[2,24,128]{2,1,0:T(8,128)S(1)}) custom-call(s32[1]{0:T(128)} %bitcast.5.base_ref, s32[1]{0:T(128)S(6)} %copy.10.count_ref, s32[9]{0:T(128)} %own_ref.13, f32[256,128]{1,0:T(8,128)S(1)} %get-tuple-element.29.lon_ref, s32[256,128]{1,0:T(8,128)S(1)} %get-tuple-element.30.cyc_ref, ...), custom_call_target="tpu_custom_call" | custom-call | tf_op jit(solution)/shard_map/tables/pallas_call | solution.py:271
  21.3 0.0 all-to-all-done.recv_ref
  21.3 3.4 %functions.1 = (f32[2,2616,128]{2,1,0:T(8,128)S(1)}, f32[24,384]{1,0:T(8,128)S(1)}, f32[9,288,288]{2,1,0:T(8,128)S(1)}) custom-call(s32[9]{0:T(128)} %own_ref.13, f32[8,32,256]{2,1,0:T(8,128)S(1)} %all-to-all-done.recv_ref, f32[2,24,128]{2,1,0:T(8,128)S(1)} %get-tuple-element.33.ty_ref, f32[9,288,288]{2,1,0:T(8,128)} %refs_0_.1), custom_call_target="tpu_custom_call" | custom-call | tf_op jit(solution)/shard_map/functions/pallas_call | solution.py:389
  24.7 5.5 %all-gather = f32[96,384]{1,0:T(8,128)S(1)} all-gather(f32[24,384]{1,0:T(8,128)S(1)} %get-tuple-element.34), channel_id=2, replica_groups=mesh['obs'=4,'ord'=8] {'obs'}, dimensions={0}, use_global_device_ids=true | all-gather | bytes 184320 | tf_op jit(solution)/shard_map/all_gather | solution.py:634
  30.1 2.8 %step.2 = (f32[8,56,256]{2,1,0:T(8,128)}, f32[24,384]{1,0:T(8,128)S(1)}, f32[24,384]{1,0:T(8,128)S(1)}) custom-call(s32[9]{0:T(128)} %own_ref.13, f32[4,24,384]{2,1,0:T(8,128)S(1)} %bitcast.9, f32[9,288,288]{2,1,0:T(8,128)S(1)} %get-tuple-element.35.refs_1_, f32[2,2616,128]{2,1,0:T(8,128)S(1)} %get-tuple-element.36.refs_2_.func_ref, ...), custom_call_target="tpu_custom_call" | custom-call | tf_op jit(solution)/shard_map/step/pallas_call | solution.py:465
  32.9 6.0 %all-to-all-start.1 = ((f32[8,56,256]{2,1,0:T(8,128)}), f32[8,56,256]{2,1,0:T(8,128)S(1)}, u32[]{:S(2)}, u32[]{:S(2)}) async-start(f32[8,56,256]{2,1,0:T(8,128)} %get-tuple-element.38), calls=%async_computation.1 | async-start | bytes 917504 | tf_op jit(solution)/shard_map/all_to_all | solution.py:636
  39.0 0.1 convert_element_type.6.ids_ref
  39.1 13.5 %all-to-all-done.1.recv_ref = f32[8,56,256]{2,1,0:T(8,128)S(1)} async-done(((f32[8,56,256]{2,1,0:T(8,128)}), f32[8,56,256]{2,1,0:T(8,128)S(1)}, u32[]{:S(2)}, u32[]{:S(2)}) %all-to-all-start.1) | async-done | bytes 458784 | tf_op jit(solution)/shard_map/all_to_all | solution.py:636
  52.5 4.0 %image.2 = (f32[24,384]{1,0:T(8,128)S(1)}, f32[8,128]{1,0:T(8,128)S(1)}, f32[2,216,128]{2,1,0:T(8,128)S(1)}, f32[2,216,128]{2,1,0:T(8,128)S(1)}, f32[2,2,72,128]...) custom-call(s32[9]{0:T(128)} %own_ref.13, s32[72]{0:T(128)S(1)} %convert_element_type.6.ids_ref, ...), custom_call_target="tpu_custom_call" | custom-call | tf_op jit(solution)/shard_map/image/pallas_call | solution.py:581
  56.6 5.5 %all-gather.1 = f32[96,384]{1,0:T(8,128)S(1)} all-gather(f32[24,384]{1,0:T(8,128)S(1)} %get-tuple-element.39), channel_id=3, replica_groups=mesh['obs'=4,'ord'=8] {'obs'}, dimensions={0}, use_global_device_ids=true | all-gather | bytes 184320 | tf_op jit(solution)/shard_map/all_gather | solution.py:638
  62.0 2.7 %step.3 = (f32[8,24,256]{2,1,0:T(8,128)}, f32[24,384]{1,0:T(8,128)S(1)}, f32[24,384]{1,0:T(8,128)S(1)}, f32[24,384]{1,0:T(8,128)S(1)}) custom-call(s32[9]{0:T(128)} %own_ref.13, f32[4,24,384]{2,1,0:T(8,128)S(1)} %bitcast.10, f32[9,288,288]{2,1,0:T(8,128)S(1)} %get-tuple-element.40.refs_1_, f32[2,2616,128]{2,1,0:T(8,128)S(1)} %get-tuple-element.36.refs_2_.func_ref, ...), custom_call_target="tpu_custom_call" | custom-call | tf_op jit(solution)/shard_map/step/pallas_call | solution.py:465
  64.8 12.1 %all_to_all.15.recv_ref = f32[8,24,256]{2,1,0:T(8,128)S(1)} all-to-all(f32[8,24,256]{2,1,0:T(8,128)} %get-tuple-element.44), channel_id=1, replica_groups=mesh['obs'=4,'ord'=8] {'ord'}, dimensions={0} | all-to-all | bytes 393216 | tf_op jit(solution)/shard_map/all_to_all | solution.py:640
  76.8 3.8 %image.3 = (f32[24,384]{1,0:T(8,128)S(1)}, f32[8,128]{1,0:T(8,128)S(1)}, f32[24,384]{1,0:T(8,128)S(1)}, f32[2,2,72,128]{3,2,1,0:T(8,128)}) custom-call(s32[9]{0:T(128)} %own_ref.13, s32[72]{0:T(128)S(1)} %convert_element_type.6.ids_ref, f32[8,24,256]{2,1,0:T(8,128)S(1)} %all_to_all.15.recv_ref, f32[2,2616,128]{2,1,0:T(8,128)S(1)} %get-tuple-element.36.refs_2_.func_ref, ...), custom_call_target="tpu_custom_call" | custom-call | tf_op jit(solution)/shard_map/image/pallas_call | solution.py:581
  80.6 5.4 %all-gather.2 = f32[96,384]{1,0:T(8,128)S(1)} all-gather(f32[24,384]{1,0:T(8,128)S(1)} %get-tuple-element.49), channel_id=4, replica_groups=mesh['obs'=4,'ord'=8] {'obs'}, dimensions={0}, use_global_device_ids=true | all-gather | bytes 184320 | tf_op jit(solution)/shard_map/all_gather | solution.py:644
  86.1 0.7 last.1
  (1 shorter events, 0.0 us)
Async XLA Ops:
  3.4 17.9 %all-to-all-start = ((f32[8,32,256]{2,1,0:T(8,128)}), f32[8,32,256]{2,1,0:T(8,128)S(1)}, u32[]{:S(2)}, u32[]{:S(2)}) async-start(f32[8,32,256]{2,1,0:T(8,128)} %get-tuple-element.28), calls=%async_computation | async-start | bytes 524288 | tf_op jit(solution)/shard_map/all_to_all | solution.py:629
  32.9 19.6 %all-to-all-start.1 = ((f32[8,56,256]{2,1,0:T(8,128)}), f32[8,56,256]{2,1,0:T(8,128)S(1)}, u32[]{:S(2)}, u32[]{:S(2)}) async-start(f32[8,56,256]{2,1,0:T(8,128)} %get-tuple-element.38), calls=%async_computation.1 | async-start | bytes 917504 | tf_op jit(solution)/shard_map/all_to_all | solution.py:636

commit v6 on v5

--- a/solution.py
+++ b/solution.py
@@ -52,7 +52,9 @@
         self.freq = self.share * self.nord
         self.table = up(self.off + self.freq, 8)
         self.sums = up(2 * (self.share + self.cnt), 16)
-        self.pay_first = up(2 * self.cnt + 1 + 2 * self.share, 8)
+        self.spare = self.halves * 2 * self.cnt
+        self.sent = up(self.spare + 1, 8)
+        self.sent_first = up(self.spare + 1 + self.halves * 2 * self.share, 8)
         self.width = min(CHUNK // 128, self.rows)
         self.chunks = self.rows // self.width
         self.windows = self.cyc // WINDOW
@@ -404,7 +406,7 @@
 
 def total_of(z, gathered_ref):
     summed = gathered_ref[0]
-    for b in range(1, z.nobs):
+    for b in range(1, gathered_ref.shape[0]):
         summed = summed + gathered_ref[b]
     return summed, summed[2 * z.cnt : 2 * z.cnt + 1, 0:1]
 
@@ -448,19 +450,20 @@
         for k in range(2):
             r = k * z.cnt + slot
             for h in range(z.halves):
-                pay[r : r + 1, h * 128 : (h + 1) * 128] = jnp.sum(acc[k][h], axis=0, keepdims=True)
+                pay[h * 2 * z.cnt + r : h * 2 * z.cnt + r + 1, :] = jnp.sum(acc[k][h], axis=0, keepdims=True)
     flip(z, cols, prec_ref)
-    top = 2 * z.cnt + 1
-    pay[2 * z.cnt : top, :] = jnp.broadcast_to(full_sum(newres_ref[...] * prec_ref[...]), (1, z.cyc))
+    top = z.spare + 1
+    pay[z.spare : top, :] = jnp.broadcast_to(full_sum(newres_ref[...] * prec_ref[...]), (1, 128))
     if not later:
         for h in range(z.halves):
-            pay[top : top + 2 * z.share, h * 128 : (h + 1) * 128] = sum_ref[h, 0 : 2 * z.share, :]
+            at = top + h * 2 * z.share
+            pay[at : at + 2 * z.share, :] = sum_ref[h, 0 : 2 * z.share, :]
     send_copies(z, pay, out_ref, sems)
 
 
 def make_step(z, own, gathered, inv, func, state, later):
     vector = jax.ShapeDtypeStruct(z.state, F32)
-    outs = [pltpu.MemorySpace.HBM((z.nord, z.pay if later else z.pay_first, z.cyc), F32)] + [vector] * (2 + later)
+    outs = [pltpu.MemorySpace.HBM((z.nord, z.sent if later else z.sent_first, 128), F32)] + [vector] * (2 + later)
     args = [own, gathered, inv, func] + list(state)
     return pl.pallas_call(
         functools.partial(step_kernel, z, later),
@@ -485,13 +488,12 @@
         inv_ref, out_ref, energy_ref, tc_ref, ts_ref, val_ref, inv_out, rows, cols, sem = refs
         fetch = pltpu.make_async_copy(inv_ref, inv_out, sem.at[0])
         fetch.start()
-        top = 2 * z.cnt + 1
         for o in range(z.nord):
             at = z.off + o * z.share
             for h in range(z.halves):
-                lanes = slice(h * 128, (h + 1) * 128)
-                tc_ref[h, at : at + z.share, :] = recv_ref[o, top : top + z.share, lanes]
-                ts_ref[h, at : at + z.share, :] = recv_ref[o, top + z.share : top + 2 * z.share, lanes]
+                top = z.spare + 1 + h * 2 * z.share
+                tc_ref[h, at : at + z.share, :] = recv_ref[o, top : top + z.share, :]
+                ts_ref[h, at : at + z.share, :] = recv_ref[o, top + z.share : top + 2 * z.share, :]
 
         def mirror(q, carry):
             for h in range(z.halves):
@@ -500,18 +502,18 @@
             return carry
 
         lax.fori_loop(1, z.no, mirror, 0)
-    energy = recv_ref[0, 2 * z.cnt : 2 * z.cnt + 1, 0:128]
+    energy = recv_ref[0, z.spare : z.spare + 1, :]
     for o in range(1, z.nord):
-        energy = energy + recv_ref[o, 2 * z.cnt : 2 * z.cnt + 1, 0:128]
+        energy = energy + recv_ref[o, z.spare : z.spare + 1, :]
     energy_ref[...] = jnp.broadcast_to(energy, (8, 128))
 
     def place(o, carry):
         for i in range(z.cnt):
             order = ids_ref[o * z.cnt + i]
             for k in range(2):
-                r = k * z.cnt + i
                 for h in range(z.halves):
-                    val_ref[k, h, pl.ds(order, 1), :] = recv_ref[o, r : r + 1, h * 128 : (h + 1) * 128]
+                    r = (h * 2 + k) * z.cnt + i
+                    val_ref[k, h, pl.ds(order, 1), :] = recv_ref[o, r : r + 1, :]
         return carry
 
     lax.fori_loop(0, z.nord, place, 0)
@@ -617,6 +619,16 @@
     )(gathered, energy, res, sol, direction)
 
 
+def over_obs(z, part):
+    if z.nobs & (z.nobs - 1):
+        return lax.all_gather(part, "obs", axis=0)
+    bit = 1
+    while bit < z.nobs // 2:
+        part = part + lax.ppermute(part, "obs", [(i, i ^ bit) for i in range(z.nobs)])
+        bit *= 2
+    return (part + lax.ppermute(part, "obs", [(i, i ^ bit) for i in range(z.nobs)]))[None]
+
+
 def body(longitude, cycle_of, obs_count, observed, obs_weight, legendre, precond_inv, order_of_slot):
     z = Sizes(legendre, longitude.shape[1])
     dense = lambda value: pltpu.with_memory_space_constraint(value.reshape(z.rows, 128), pltpu.MemorySpace.HBM)
@@ -631,17 +643,17 @@
     sums, ty = make_tables(z, base, obs_count, order_of_slot, *near)
     ids = recv[:, z.id_row, : z.cnt].reshape(z.no).astype(jnp.int32)
     func, part, near_inv = make_functions(z, order_of_slot, recv, ty, inv)
-    gathered = lax.all_gather(part, "obs", axis=0)
+    gathered = over_obs(z, part)
     values, res, direction = make_step(z, order_of_slot, gathered, near_inv, func, (sums,), False)
     recv = lax.all_to_all(values, "ord", 0, 0)
     part, energy, tc, ts, all_values, near_inv = make_image(z, order_of_slot, ids, recv, func, (inv,), False)
-    gathered = lax.all_gather(part, "obs", axis=0)
+    gathered = over_obs(z, part)
     values, res, prec, sol = make_step(z, order_of_slot, gathered, near_inv, func, (energy, res, direction), True)
     recv = lax.all_to_all(values, "ord", 0, 0)
     part, energy, direction, all_values = make_image(
         z, order_of_slot, ids, recv, func, (tc, ts, all_values, energy, prec, direction), True
     )
-    gathered = lax.all_gather(part, "obs", axis=0)
+    gathered = over_obs(z, part)
     return tuple(make_last(z, gathered, energy, res, sol, direction))
 
 

time: 87.3 us -> 84.4 us (0.967)
  blocking collectives: 28.4 us -> 11.3 us
  waiting for transfers between devices: 13.5 us -> 23.2 us
  starting transfers between devices: 13.3 us -> 18 us
    all_gather x3 -> x0, blocking collectives: 16.4 us -> none  [body(): gathered = lax.all_gather(part, 'obs', axis=0)]
    ppermute x0 -> x6, waiting for transfers between devices: none -> 11 us  [over_obs(): lax.ppermute(part, 'obs', [(i, i ^ bit) for i in range(z.nobs)])]
    ppermute x0 -> x6, starting transfers between devices: none -> 4.63 us  [over_obs(): lax.ppermute(part, 'obs', [(i, i ^ bit) for i in range(z.nobs)])]
    all_to_all x1, waiting for transfers between devices: 13.5 us -> 12.2 us  [body(): recv = lax.all_to_all(values, 'ord', 0, 0)]
  transfers between devices with their start and end apart: 2 -> 8, of which waited for: 1 -> 7; matrix products, arithmetic and copies ran while one was open for 0% -> 0% of each run, Pallas kernels for 11% -> 12%
where the time goes in v6:
time: 84.4 us; the launch traced here: 83.9 us
  Pallas kernels  30 us (36%)
  waiting for transfers between devices  23.2 us (27%)
  starting transfers between devices  18 us (21%)
  blocking collectives  11.3 us (13%)
  between operations  1.37 us (2%)
    all_to_all x1, waiting for transfers between devices, body(): recv = lax.all_to_all(values, 'ord', 0, 0)  12.2 us
    all_to_all x1, blocking collectives, body(): recv = lax.all_to_all(values, 'ord', 0, 0)  11.3 us
    ppermute x6, waiting for transfers between devices, over_obs(): lax.ppermute(part, 'obs', [(i, i ^ bit) for i in range(z.nobs)])  11 us
    pallas_call x1, Pallas kernels, make_tables(): pl.pallas_call(functools.partial(tables_kernel, z), in_specs=[SMEM, SMEM,...  9.9 us
    pallas_call x2, Pallas kernels, make_image(): pl.pallas_call(functools.partial(image_kernel, z, later), in_specs=[SMEM,...  7.78 us
    all_to_all x1, starting transfers between devices, body(): recv = lax.all_to_all(seeds, 'ord', 0, 0)  7.32 us
    all_to_all x1, starting transfers between devices, body(): recv = lax.all_to_all(values, 'ord', 0, 0)  6.01 us
    pallas_call x2, Pallas kernels, make_step(): pl.pallas_call(functools.partial(step_kernel, z, later), in_specs=[SMEM]...  5.54 us
  transfers between devices with their start and end apart: 8, of which 7 were waited for; matrix products, arithmetic and copies ran while one was open for 0% of the time, Pallas kernels for 12%

profile of v6, /device:TPU:0, one launch (start us, length us, event | category | flops | bytes accessed | tf_op | source)
XLA Modules:
  0.0 83.9 jit_solution(53482887815638631)
XLA Ops:
  0.6 2.8 %seeds.1 = (f32[8,32,256]{2,1,0:T(8,128)}, f32[256,128]{1,0:T(8,128)S(1)}, s32[256,128]{1,0:T(8,128)S(1)}, f32[256,128]{1,0:T(8,128)S(1)}, f32[256,128]{1,0:T(8,128)S(1)}) custom-call(s32[1]{0:T(128)} %bitcast.first_ref, s32[9]{0:T(128)} %own_ref.13, f32[1,9,288,256]{3,2,1,0:T(8,128)} %leg_ref.1, f32[256,128]{1,0:T(8,128)} %bitcast.12, s32[256,128]{1,0:T(8,128)} %bitcast.13, ...), custom_call_target="tpu_custom_call" | custom-call | tf_op jit(solution)/shard_map/seeds/pallas_call | solution.py:123
  3.4 7.3 %all-to-all-start = ((f32[8,32,256]{2,1,0:T(8,128)}), f32[8,32,256]{2,1,0:T(8,128)S(1)}, u32[]{:S(2)}, u32[]{:S(2)}) async-start(f32[8,32,256]{2,1,0:T(8,128)} %get-tuple-element.28), calls=%async_computation | async-start | bytes 524288 | tf_op jit(solution)/shard_map/all_to_all | solution.py:641
  11.4 9.9 %tables.1 = (f32[2,40,128]{2,1,0:T(8,128)S(1)}, f32[2,24,128]{2,1,0:T(8,128)S(1)}) custom-call(s32[1]{0:T(128)} %bitcast.5.base_ref, s32[1]{0:T(128)S(6)} %copy.10.count_ref, s32[9]{0:T(128)} %own_ref.13, f32[256,128]{1,0:T(8,128)S(1)} %get-tuple-element.29.lon_ref, s32[256,128]{1,0:T(8,128)S(1)} %get-tuple-element.30.cyc_ref, ...), custom_call_target="tpu_custom_call" | custom-call | tf_op jit(solution)/shard_map/tables/pallas_call | solution.py:273
  21.3 0.0 all-to-all-done.recv_ref
  21.3 3.4 %functions.1 = (f32[2,2616,128]{2,1,0:T(8,128)S(1)}, f32[24,384]{1,0:T(8,128)S(1)}, f32[9,288,288]{2,1,0:T(8,128)S(1)}) custom-call(s32[9]{0:T(128)} %own_ref.13, f32[8,32,256]{2,1,0:T(8,128)S(1)} %all-to-all-done.recv_ref, f32[2,24,128]{2,1,0:T(8,128)S(1)} %get-tuple-element.33.ty_ref, f32[9,288,288]{2,1,0:T(8,128)} %refs_0_.1), custom_call_target="tpu_custom_call" | custom-call | tf_op jit(solution)/shard_map/functions/pallas_call | solution.py:391
  24.7 0.1 collective-permute-start
  24.7 1.2 %collective-permute-done = f32[24,384]{1,0:T(8,128)S(1)} collective-permute-done((f32[24,384]{1,0:T(8,128)S(1)}, f32[24,384]{1,0:T(8,128)S(1)}, u32[]{:S(2)}, u32[]{:S(2)}) %collective-permute-start) | collective-permute-done | bytes 36896 | tf_op jit(solution)/shard_map/ppermute | solution.py:627
  26.0 1.5 %collective-permute-start.1 = (f32[24,384]{1,0:T(8,128)S(1)}, f32[24,384]{1,0:T(8,128)S(1)}, u32[]{:S(2)}, u32[]{:S(2)}) collective-permute-start(f32[24,384]{1,0:T(8,128)S(1)} %add.18), channel_id=1, source_target_pairs={{0,16},{8,24},{16,0},{24,8},{1,17},{9,25},{17,1},{25,9},{2,18},{10... | collective-permute-start | bytes 110600 | tf_op jit(solution)/shard_map/ppermute | solution.py:629
  27.4 2.5 %collective-permute-done.1 = f32[24,384]{1,0:T(8,128)S(1)} collective-permute-done((f32[24,384]{1,0:T(8,128)S(1)}, f32[24,384]{1,0:T(8,128)S(1)}, u32[]{:S(2)}, u32[]{:S(2)}) %collective-permute-start.1) | collective-permute-done | bytes 36896 | tf_op jit(solution)/shard_map/ppermute | solution.py:629
  29.9 2.8 %step.2 = (f32[8,112,128]{2,1,0:T(8,128)}, f32[24,384]{1,0:T(8,128)S(1)}, f32[24,384]{1,0:T(8,128)S(1)}) custom-call(s32[9]{0:T(128)} %own_ref.13, f32[1,24,384]{2,1,0:T(8,128)S(1)} %add_bitcast_fusion.2.refs_0_, f32[9,288,288]{2,1,0:T(8,128)S(1)} %get-tuple-element.35.refs_1_, f32[2,2616,128]{2,1,0:T(8,128)S(1)} %get-tuple-element.36.refs_2_.func_ref, ...), custom_call_target="tpu_custom_call" | custom-call | tf_op jit(solution)/shard_map/step/pallas_call | solution.py:468
  32.7 6.0 %all-to-all-start.1 = ((f32[8,112,128]{2,1,0:T(8,128)}), f32[8,112,128]{2,1,0:T(8,128)S(1)}, u32[]{:S(2)}, u32[]{:S(2)}) async-start(f32[8,112,128]{2,1,0:T(8,128)} %get-tuple-element.38), calls=%async_computation.1 | async-start | bytes 917504 | tf_op jit(solution)/shard_map/all_to_all | solution.py:648
  38.8 0.1 convert_element_type.6.ids_ref
  38.8 12.2 %all-to-all-done.1.recv_ref = f32[8,112,128]{2,1,0:T(8,128)S(1)} async-done(((f32[8,112,128]{2,1,0:T(8,128)}), f32[8,112,128]{2,1,0:T(8,128)S(1)}, u32[]{:S(2)}, u32[]{:S(2)}) %all-to-all-start.1) | async-done | bytes 458784 | tf_op jit(solution)/shard_map/all_to_all | solution.py:648
  51.0 4.0 %image.2 = (f32[24,384]{1,0:T(8,128)S(1)}, f32[8,128]{1,0:T(8,128)S(1)}, f32[2,216,128]{2,1,0:T(8,128)S(1)}, f32[2,216,128]{2,1,0:T(8,128)S(1)}, f32[2,2,72,128]...) custom-call(s32[9]{0:T(128)} %own_ref.13, s32[72]{0:T(128)S(1)} %convert_element_type.6.ids_ref, ...), custom_call_target="tpu_custom_call" | custom-call | tf_op jit(solution)/shard_map/image/pallas_call | solution.py:583
  55.0 0.1 collective-permute-start.2
  55.1 1.2 %collective-permute-done.2 = f32[24,384]{1,0:T(8,128)S(1)} collective-permute-done((f32[24,384]{1,0:T(8,128)S(1)}, f32[24,384]{1,0:T(8,128)S(1)}, u32[]{:S(2)}, u32[]{:S(2)}) %collective-permute-start.2) | collective-permute-done | bytes 36896 | tf_op jit(solution)/shard_map/ppermute | solution.py:627
  56.3 1.5 %collective-permute-start.3 = (f32[24,384]{1,0:T(8,128)S(1)}, f32[24,384]{1,0:T(8,128)S(1)}, u32[]{:S(2)}, u32[]{:S(2)}) collective-permute-start(f32[24,384]{1,0:T(8,128)S(1)} %add.20), channel_id=1, source_target_pairs={{0,16},{8,24},{16,0},{24,8},{1,17},{9,25},{17,1},{25,9},{2,18},{10... | collective-permute-start | bytes 110600 | tf_op jit(solution)/shard_map/ppermute | solution.py:629
  57.8 2.5 %collective-permute-done.3 = f32[24,384]{1,0:T(8,128)S(1)} collective-permute-done((f32[24,384]{1,0:T(8,128)S(1)}, f32[24,384]{1,0:T(8,128)S(1)}, u32[]{:S(2)}, u32[]{:S(2)}) %collective-permute-start.3) | collective-permute-done | bytes 36896 | tf_op jit(solution)/shard_map/ppermute | solution.py:629
  60.3 2.7 %step.3 = (f32[8,40,128]{2,1,0:T(8,128)}, f32[24,384]{1,0:T(8,128)S(1)}, f32[24,384]{1,0:T(8,128)S(1)}, f32[24,384]{1,0:T(8,128)S(1)}) custom-call(s32[9]{0:T(128)} %own_ref.13, f32[1,24,384]{2,1,0:T(8,128)S(1)} %add_bitcast_fusion.1.refs_0_, f32[9,288,288]{2,1,0:T(8,128)S(1)} %get-tuple-element.40.refs_1_, ...), custom_call_target="tpu_custom_call" | custom-call | tf_op jit(solution)/shard_map/step/pallas_call | solution.py:468
  63.0 11.3 %all_to_all.15.recv_ref = f32[8,40,128]{2,1,0:T(8,128)S(1)} all-to-all(f32[8,40,128]{2,1,0:T(8,128)} %get-tuple-element.44), channel_id=1, replica_groups=mesh['obs'=4,'ord'=8] {'ord'}, dimensions={0} | all-to-all | bytes 327680 | tf_op jit(solution)/shard_map/all_to_all | solution.py:652
  74.3 3.8 %image.3 = (f32[24,384]{1,0:T(8,128)S(1)}, f32[8,128]{1,0:T(8,128)S(1)}, f32[24,384]{1,0:T(8,128)S(1)}, f32[2,2,72,128]{3,2,1,0:T(8,128)}) custom-call(s32[9]{0:T(128)} %own_ref.13, s32[72]{0:T(128)S(1)} %convert_element_type.6.ids_ref, f32[8,40,128]{2,1,0:T(8,128)S(1)} %all_to_all.15.recv_ref, f32[2,2616,128]{2,1,0:T(8,128)S(1)} %get-tuple-element.36.refs_2_.func_ref, ...), custom_call_target="tpu_custom_call" | custom-call | tf_op jit(solution)/shard_map/image/pallas_call | solution.py:583
  78.0 0.0 collective-permute-start.4
  78.0 1.2 %collective-permute-done.4 = f32[24,384]{1,0:T(8,128)S(1)} collective-permute-done((f32[24,384]{1,0:T(8,128)S(1)}, f32[24,384]{1,0:T(8,128)S(1)}, u32[]{:S(2)}, u32[]{:S(2)}) %collective-permute-start.4) | collective-permute-done | bytes 36896 | tf_op jit(solution)/shard_map/ppermute | solution.py:627
  79.3 1.5 %collective-permute-start.5 = (f32[24,384]{1,0:T(8,128)S(1)}, f32[24,384]{1,0:T(8,128)S(1)}, u32[]{:S(2)}, u32[]{:S(2)}) collective-permute-start(f32[24,384]{1,0:T(8,128)S(1)} %add.22), channel_id=1, source_target_pairs={{0,16},{8,24},{16,0},{24,8},{1,17},{9,25},{17,1},{25,9},{2,18},{10... | collective-permute-start | bytes 110600 | tf_op jit(solution)/shard_map/ppermute | solution.py:629
  80.8 2.5 %collective-permute-done.5 = f32[24,384]{1,0:T(8,128)S(1)} collective-permute-done((f32[24,384]{1,0:T(8,128)S(1)}, f32[24,384]{1,0:T(8,128)S(1)}, u32[]{:S(2)}, u32[]{:S(2)}) %collective-permute-start.5) | collective-permute-done | bytes 36896 | tf_op jit(solution)/shard_map/ppermute | solution.py:629
  83.2 0.7 last.1
  (7 shorter events, 0.1 us)
Async XLA Ops:
  3.4 17.9 %all-to-all-start = ((f32[8,32,256]{2,1,0:T(8,128)}), f32[8,32,256]{2,1,0:T(8,128)S(1)}, u32[]{:S(2)}, u32[]{:S(2)}) async-start(f32[8,32,256]{2,1,0:T(8,128)} %get-tuple-element.28), calls=%async_computation | async-start | bytes 524288 | tf_op jit(solution)/shard_map/all_to_all | solution.py:641
  24.7 1.3 %collective-permute-start = (f32[24,384]{1,0:T(8,128)S(1)}, f32[24,384]{1,0:T(8,128)S(1)}, u32[]{:S(2)}, u32[]{:S(2)}) collective-permute-start(f32[24,384]{1,0:T(8,128)S(1)} %get-tuple-element.34), channel_id=1, source_target_pairs={{0,8},{8,0},{16,24},{24,16},{1,9},{9,1},{17,25},{25,17},{2,10},{10... | collective-permute-start | bytes 110600 | tf_op jit(solution)/shard_map/ppermute | solution.py:627
  26.0 4.0 %collective-permute-start.1 = (f32[24,384]{1,0:T(8,128)S(1)}, f32[24,384]{1,0:T(8,128)S(1)}, u32[]{:S(2)}, u32[]{:S(2)}) collective-permute-start(f32[24,384]{1,0:T(8,128)S(1)} %add.18), channel_id=1, source_target_pairs={{0,16},{8,24},{16,0},{24,8},{1,17},{9,25},{17,1},{25,9},{2,18},{10... | collective-permute-start | bytes 110600 | tf_op jit(solution)/shard_map/ppermute | solution.py:629
  32.7 18.3 %all-to-all-start.1 = ((f32[8,112,128]{2,1,0:T(8,128)}), f32[8,112,128]{2,1,0:T(8,128)S(1)}, u32[]{:S(2)}, u32[]{:S(2)}) async-start(f32[8,112,128]{2,1,0:T(8,128)} %get-tuple-element.38), calls=%async_computation.1 | async-start | bytes 917504 | tf_op jit(solution)/shard_map/all_to_all | solution.py:648
  55.0 1.3 %collective-permute-start.2 = (f32[24,384]{1,0:T(8,128)S(1)}, f32[24,384]{1,0:T(8,128)S(1)}, u32[]{:S(2)}, u32[]{:S(2)}) collective-permute-start(f32[24,384]{1,0:T(8,128)S(1)} %get-tuple-element.39), channel_id=1, source_target_pairs={{0,8},{8,0},{16,24},{24,16},{1,9},{9,1},{17,25},{25,17},{2,10},{10... | collective-permute-start | bytes 110600 | tf_op jit(solution)/shard_map/ppermute | solution.py:627
  56.3 4.0 %collective-permute-start.3 = (f32[24,384]{1,0:T(8,128)S(1)}, f32[24,384]{1,0:T(8,128)S(1)}, u32[]{:S(2)}, u32[]{:S(2)}) collective-permute-start(f32[24,384]{1,0:T(8,128)S(1)} %add.20), channel_id=1, source_target_pairs={{0,16},{8,24},{16,0},{24,8},{1,17},{9,25},{17,1},{25,9},{2,18},{10... | collective-permute-start | bytes 110600 | tf_op jit(solution)/shard_map/ppermute | solution.py:629
  78.0 1.2 %collective-permute-start.4 = (f32[24,384]{1,0:T(8,128)S(1)}, f32[24,384]{1,0:T(8,128)S(1)}, u32[]{:S(2)}, u32[]{:S(2)}) collective-permute-start(f32[24,384]{1,0:T(8,128)S(1)} %get-tuple-element.49), channel_id=1, source_target_pairs={{0,8},{8,0},{16,24},{24,16},{1,9},{9,1},{17,25},{25,17},{2,10},{10... | collective-permute-start | bytes 110600 | tf_op jit(solution)/shard_map/ppermute | solution.py:627
  79.3 4.0 %collective-permute-start.5 = (f32[24,384]{1,0:T(8,128)S(1)}, f32[24,384]{1,0:T(8,128)S(1)}, u32[]{:S(2)}, u32[]{:S(2)}) collective-permute-start(f32[24,384]{1,0:T(8,128)S(1)} %add.22), channel_id=1, source_target_pairs={{0,16},{8,24},{16,0},{24,8},{1,17},{9,25},{17,1},{25,9},{2,18},{10... | collective-permute-start | bytes 110600 | tf_op jit(solution)/shard_map/ppermute | solution.py:629
